TPU v7x, 32 devices: a whole 2x2x4 slice. The times are simulated.
32 devices in a mesh: dp: 8 (over z, x), mp: 4 (over y, core).
Axes of the slice: x: 2, y: 2, z: 4, core: 2. Of those that a mesh axis runs over, the one named last changes fastest.
Arguments:
- token_ids: int32 [64, 512], P('dp'), may hold values from 0 to 30719
- seg_split: int32 [64], P('dp'), may hold values from 1 to 255
- lengths: int32 [64], P('dp'), may hold values from 256 to 512, as said below
- mlm_pos: int32 [64, 80], P('dp'), may hold values from 1 to 255
- mlm_labels: int32 [64, 80], P('dp'), may hold values from 0 to 30719
- sop_labels: int32 [64], P('dp'), may hold values from 0 to 1
- owner: int32 [8], replicated, may hold values from 0 to 7, as said below
- step_count: int32 [1], replicated, may hold values from 1 to 20
- table: float32 [30720, 768], P(('dp', 'mp')), may hold values from -0.6134347 to 0.6134347
- table_m: float32 [30720, 768], P(('dp', 'mp')), may hold values from -2.3841858e-06 to 2.3841858e-06
- table_v: float32 [30720, 768], P(('dp', 'mp')), may hold values from 1.4128509e-14 to 5.6514035e-14
- unit_master: float32 [16, 768, 768], P('dp', 'mp')
- unit_m: float32 [16, 768, 768], P('dp', 'mp'), may hold values from -2.3841858e-06 to 2.3841858e-06
- unit_v: float32 [16, 768, 768], P('dp', 'mp'), may hold values from 1.4128509e-14 to 5.6514035e-14
- small: float32 [522, 768], replicated
- small_m: float32 [522, 768], replicated, may hold values from -6.67572e-06 to 6.67572e-06
- small_v: float32 [522, 768], replicated, may hold values from 8.979885e-14 to 3.591954e-13
- taps: float32 [9, 384], replicated, may hold values from -0.75 to 0.75
- taps_m: float32 [9, 384], replicated, may hold values from -2.2888184e-05 to 2.2888184e-05
- taps_v: float32 [9, 384], replicated, may hold values from 1.1574074e-12 to 4.6296296e-12
Outputs:
- loss: float32 [], replicated
- grad_norm: float32 [], replicated
- table_new: float32 [30720, 768], P(('dp', 'mp'))
- table_m_new: float32 [30720, 768], P(('dp', 'mp'))
- table_v_new: float32 [30720, 768], P(('dp', 'mp'))
- table_copy: bfloat16 [30720, 768], P(('dp', 'mp'))
- unit_new: float32 [16, 768, 768], P('dp', 'mp')
- unit_m_new: float32 [16, 768, 768], P('dp', 'mp')
- unit_v_new: float32 [16, 768, 768], P('dp', 'mp')
- unit_copy: bfloat16 [16, 768, 768], P('dp', 'mp')
- small_new: float32 [522, 768], replicated
- small_m_new: float32 [522, 768], replicated
- small_v_new: float32 [522, 768], replicated
- taps_new: float32 [9, 384], replicated
- taps_m_new: float32 [9, 384], replicated
- taps_v_new: float32 [9, 384], replicated
Inputs may be any that keep to these rules, and one draw needn't show every extreme that they name: Tokens at positions from lengths on are padding; the first sequence is full. `owner`: every index of dp keeps at most 2 of the 8 layer matrices, and two indices keep exactly 2; slots beyond an index's matrices are unused. `mlm_pos`: masked positions lie below every length and may repeat.
All inputs are finite; a program needn't handle non-finite values.
Results may differ from a plain program's by a relative error of at most 0.0029.
The roundings to bfloat16 on the way count: a program that leaves them out, or rounds other values in their place, can miss the bound.
Values may be sent and summed in bfloat16 or wider, within the bound.
No kernel may reach another device: no remote copies, remote signals or barrier semaphores. Data moves between devices by JAX's collectives and lax.ppermute only.
A program may use at most 384 MiB of HBM per device.

v0:
```python
from functools import partial
import math

import jax
import jax.numpy as jnp
from jax import lax
from jax.sharding import PartitionSpec as P

DH = 64


highest = lax.Precision.HIGHEST
beta_one = 0.9
beta_two = 0.999
adam_eps = 1e-08
learn_rate = 0.03
weight_decay = 0.01
clip_bound = 0.02
norm_eps = 1e-06


def broadcast(block, axis, holder):
    block = jnp.where(lax.axis_index(axis) == holder, block, jnp.zeros_like(block))
    return lax.psum(block, axis)


def merged(x, axis, combine):
    everything = jax.tree.map(lambda part: lax.all_gather(part, axis), x)
    initial = jax.tree.map(lambda part: part[0], everything)

    def turn(k, so_far):
        return combine(so_far, jax.tree.map(lambda part: part[k], everything))

    return lax.fori_loop(1, lax.axis_size(axis), turn, initial)


def dot_right(left, right):
    return lax.dot_general(
        left, right, (((1,), (1,)), ((), ())), preferred_element_type=jnp.float32
    )


def dot_left(left, right):
    return lax.dot_general(
        left, right, (((0,), (0,)), ((), ())), preferred_element_type=jnp.float32
    )


def dot_plain(left, right):
    return jnp.dot(left, right, preferred_element_type=jnp.float32)


def layer_norm(stream, gain, offset):
    center = jnp.mean(stream, axis=-1, keepdims=True)
    shifted = stream - center
    spread = jnp.mean(shifted * shifted, axis=-1, keepdims=True)
    return shifted * lax.rsqrt(spread + norm_eps) * gain + offset


def norm_piece(stream, params, index):
    return layer_norm(stream, params[index], params[index + 3])


def embed_rows(word_rows, params, split_at):
    length = word_rows.shape[-2]
    second = (jnp.arange(length)[None, :] > split_at[:, None]).astype(jnp.float32)[..., None]
    summed = (
        word_rows
        + params[6 : 6 + length]
        + params[6 + length] * (1.0 - second)
        + params[7 + length] * second
    )
    return layer_norm(summed, params[0], params[3])


def conv_head(queries, key_rows, values, taps_head):
    length = queries.shape[0]
    width = taps_head.shape[0]
    logits = jnp.dot(queries * key_rows, taps_head.T, precision=highest)
    kernel = jax.nn.softmax(logits, axis=-1)
    padded = jnp.pad(values, ((width // 2, width // 2), (0, 0)))
    total = jnp.zeros_like(values)
    for offset in range(width):
        total = total + kernel[:, offset : offset + 1] * padded[offset : offset + length]
    return total


def exact_gelu(values):
    return jax.nn.gelu(values, approximate=False)


def sop_loss(cls_rows, params, labels, denom, length):
    logits = jnp.dot(cls_rows, params[length + 8 : length + 10].T, precision=highest)
    chosen = jnp.take_along_axis(logits, labels[:, None], axis=1)[:, 0]
    return jnp.sum(jax.nn.logsumexp(logits, axis=-1) - chosen) / denom


def pair_sum(pieces, part):
    rows = pieces.shape[0]
    return pieces.reshape(rows, 2, 2, 2 * part).sum(axis=2).reshape(rows, 4 * part)


def lse_merge(first, second):
    top = jnp.maximum(first[0], second[0])
    total = first[1] * jnp.exp(first[0] - top) + second[1] * jnp.exp(second[0] - top)
    return (top, total, first[2] + second[2])


def adam(weight, first, second, grad, count):
    first_new = beta_one * first + (1.0 - beta_one) * grad
    second_new = beta_two * second + (1.0 - beta_two) * grad * grad
    corr_one = 1.0 - jnp.power(beta_one, count)
    corr_two = 1.0 - jnp.power(beta_two, count)
    step = first_new / corr_one / (jnp.sqrt(second_new / corr_two) + adam_eps)
    return (weight - learn_rate * (step + weight_decay * weight), first_new, second_new)


def masked_scores(queries, key_rows, valid_len):
    scale = 1.0 / math.sqrt(queries.shape[1])
    scores = dot_right(queries, key_rows) * scale
    allowed = jnp.arange(key_rows.shape[0])[None, :] < valid_len
    return jnp.where(allowed, scores, -1e30)


def attend_forward(queries, key_rows, values, valid_len, taps_head):
    scores = masked_scores(queries, key_rows, valid_len)
    top = jnp.max(scores, axis=1, keepdims=True)
    weights = jnp.exp(scores - top)
    total = jnp.sum(weights, axis=1, keepdims=True)
    probs = (weights / total).astype(jnp.bfloat16)
    return (dot_plain(probs, values), (top + jnp.log(total))[:, 0])


def convolve_forward(queries, key_rows, values, valid_len, taps_head):
    mixed = conv_head(
        queries.astype(jnp.float32),
        key_rows.astype(jnp.float32),
        values.astype(jnp.float32),
        taps_head,
    )
    return (mixed, jnp.zeros((queries.shape[0],), jnp.float32))


def attend_backward(queries, key_rows, values, valid_len, taps_head, log_total, grad_out):
    scale = 1.0 / math.sqrt(queries.shape[1])
    probs = jnp.exp(masked_scores(queries, key_rows, valid_len) - log_total[:, None])
    grad_probs = dot_right(grad_out, values)
    grad_scores = (
        probs * (grad_probs - jnp.sum(probs * grad_probs, axis=1, keepdims=True))
    ).astype(jnp.bfloat16)
    grad_query = dot_plain(grad_scores, key_rows) * scale
    grad_keys = dot_left(grad_scores, queries) * scale
    grad_values = dot_left(probs.astype(jnp.bfloat16), grad_out)
    return (grad_query, grad_keys, grad_values, jnp.zeros_like(taps_head))


def convolve_backward(queries, key_rows, values, valid_len, taps_head, log_total, grad_out):
    _, pullback = jax.vjp(
        conv_head,
        queries.astype(jnp.float32),
        key_rows.astype(jnp.float32),
        values.astype(jnp.float32),
        taps_head,
    )
    return pullback(grad_out.astype(jnp.float32))


def conv_slot(shard_index, head, count):
    return jnp.maximum(shard_index * (shard_index + 1) // 2 + head - count, 0) * DH


def heads_forward(shard_index, taps, item):
    queries, key_rows, values, valid_len = item
    count = queries.shape[1] // DH
    outputs = []
    totals = []
    for head in range(count):
        cols = slice(head * DH, (head + 1) * DH)
        taps_head = lax.dynamic_slice_in_dim(taps, conv_slot(shard_index, head, count), DH, 1)
        mixed, log_total = lax.cond(
            head < count - shard_index,
            attend_forward,
            convolve_forward,
            queries[:, cols],
            key_rows[:, cols],
            values[:, cols],
            valid_len,
            taps_head,
        )
        outputs.append(mixed)
        totals.append(log_total)
    return (jnp.concatenate(outputs, axis=1), jnp.stack(totals, axis=1))


def heads_backward(shard_index, taps, item):
    queries, key_rows, values, valid_len, log_totals, grad_out = item
    count = queries.shape[1] // DH
    grads = ([], [], [])
    taps_grad = jnp.zeros_like(taps)
    for head in range(count):
        cols = slice(head * DH, (head + 1) * DH)
        start = conv_slot(shard_index, head, count)
        taps_head = lax.dynamic_slice_in_dim(taps, start, DH, 1)
        grad_query, grad_keys, grad_values, grad_taps = lax.cond(
            head < count - shard_index,
            attend_backward,
            convolve_backward,
            queries[:, cols],
            key_rows[:, cols],
            values[:, cols],
            valid_len,
            taps_head,
            log_totals[:, head],
            grad_out[:, cols],
        )
        grads[0].append(grad_query)
        grads[1].append(grad_keys)
        grads[2].append(grad_values)
        current = lax.dynamic_slice_in_dim(taps_grad, start, DH, 1)
        taps_grad = lax.dynamic_update_slice_in_dim(taps_grad, current + grad_taps, start, 1)
    stacked = jnp.stack([jnp.concatenate(group_list, axis=1) for group_list in grads])
    return (stacked, taps_grad)


def body(
    token_ids,
    seg_split,
    lengths,
    mlm_pos,
    mlm_labels,
    sop_labels,
    owner,
    step_count,
    table,
    table_m,
    table_v,
    unit_master,
    unit_m,
    unit_v,
    small,
    small_m,
    small_v,
    taps,
    taps_m,
    taps_v,
):
    mp_count = lax.axis_size("mp")
    dp_count = lax.axis_size("dp")
    shard_index = lax.axis_index("mp")
    my_index = lax.axis_index("dp")
    seqs, length = token_ids.shape
    tokens = seqs * length
    width = small.shape[1]
    part = unit_master.shape[1]
    vblock = table.shape[0]
    cap_slots = unit_master.shape[0]
    matrices = owner.shape[0]
    earlier = jnp.arange(matrices)[:, None] > jnp.arange(matrices)[None, :]
    slot_rank = jnp.sum(jnp.logical_and(earlier, owner[:, None] == owner[None, :]), axis=1)
    selector = jnp.logical_and(
        owner[None, :] == my_index, slot_rank[None, :] == jnp.arange(cap_slots)[:, None]
    ).astype(jnp.float32)
    fetched = []
    for matrix in range(matrices):
        own_slot = lax.dynamic_index_in_dim(
            unit_master, slot_rank[matrix], 0, keepdims=False
        ).astype(jnp.bfloat16)
        fetched.append(broadcast(own_slot, "dp", owner[matrix]))
    weights = jnp.stack(fetched)
    vocab = lax.all_gather(table.astype(jnp.bfloat16), "dp", axis=0, tiled=True)

    def locate(ids):
        block = ids // vblock
        return (block % mp_count == shard_index, block // mp_count * vblock + ids % vblock)

    word_mine, word_row = locate(token_ids.reshape(-1))
    picked_rows = jnp.where(word_mine[:, None], vocab[word_row].astype(jnp.float32), 0.0)
    word_rows = (
        lax.psum(picked_rows.astype(jnp.bfloat16), "mp")
        .astype(jnp.float32)
        .reshape(seqs, length, width)
    )
    embedded, embed_pull = jax.vjp(partial(embed_rows, split_at=seg_split), word_rows, small)
    embedded = embedded.reshape(tokens, width)
    low_in = embedded.astype(jnp.bfloat16)
    qkv = jnp.einsum(
        "td,kpd->ktp", low_in, weights[0:3], preferred_element_type=jnp.float32
    ).astype(jnp.bfloat16)
    qkv_seq = qkv.reshape(3, seqs, length, part)
    head_out, log_totals = lax.map(
        partial(heads_forward, shard_index, taps), (qkv_seq[0], qkv_seq[1], qkv_seq[2], lengths)
    )
    gathered = lax.all_gather(
        head_out.reshape(tokens, part).astype(jnp.bfloat16), "mp", axis=1, tiled=True
    )
    proj_cols = dot_right(gathered, weights[3]).astype(jnp.bfloat16)
    projected = lax.all_gather(proj_cols, "mp", axis=1, tiled=True)
    attended, norm_one_pull = jax.vjp(
        partial(norm_piece, index=1), embedded + projected.astype(jnp.float32), small
    )
    group_start = shard_index // 2 * 2 * part
    group_in = lax.dynamic_slice_in_dim(attended, group_start, 2 * part, 1).astype(jnp.bfloat16)
    weight_in = jnp.concatenate([weights[4], weights[5]], axis=0)
    weight_out = jnp.concatenate([weights[6], weights[7]], axis=0)
    hidden_pre = dot_plain(group_in, weight_in)
    hidden_f, gelu_pull = jax.vjp(exact_gelu, hidden_pre)
    hidden = hidden_f.astype(jnp.bfloat16)
    ffn_pieces = lax.all_gather(dot_right(hidden, weight_out), "mp", axis=1, tiled=True)
    ffn_out = pair_sum(ffn_pieces, part)
    final_rows, norm_two_pull = jax.vjp(partial(norm_piece, index=2), attended + ffn_out, small)
    positions = (jnp.arange(seqs)[:, None] * length + mlm_pos).reshape(-1)
    masked_rows = final_rows[positions].astype(jnp.bfloat16)
    logits = dot_right(masked_rows, vocab)
    label_mine, label_row = locate(mlm_labels.reshape(-1))
    onehot = jnp.logical_and(
        jnp.arange(vocab.shape[0])[None, :] == label_row[:, None], label_mine[:, None]
    ).astype(jnp.float32)
    local_top = jnp.max(logits, axis=1)
    local_total = jnp.sum(jnp.exp(logits - local_top[:, None]), axis=1)
    target = jnp.sum(logits * onehot, axis=1)
    top, total, target_all = merged((local_top, local_total, target), "mp", lse_merge)
    log_sum = top + jnp.log(total)
    count_all = seqs * mlm_pos.shape[1] * dp_count
    mlm_part = jnp.sum(log_sum - target_all) / count_all
    grad_logits = ((jnp.exp(logits - log_sum[:, None]) - onehot) / count_all).astype(jnp.bfloat16)
    grad_table = dot_left(grad_logits, masked_rows)
    grad_masked = lax.psum(dot_plain(grad_logits, vocab), "mp")
    cls_index = jnp.arange(seqs) * length
    sop_part, sop_pull = jax.vjp(
        partial(sop_loss, labels=sop_labels, denom=seqs * dp_count, length=length),
        final_rows[cls_index],
        small,
    )
    grad_cls, grad_small_sop = sop_pull(jnp.ones((), jnp.float32))
    grad_final = (
        jnp.zeros((tokens, width), jnp.float32)
        .at[positions]
        .add(grad_masked)
        .at[cls_index]
        .add(grad_cls)
    )
    grad_sum_two, grad_small_two = norm_two_pull(grad_final)
    grad_ffn = grad_sum_two.astype(jnp.bfloat16)
    grad_group = lax.dynamic_slice_in_dim(grad_ffn, group_start, 2 * part, 1)
    grad_hidden = dot_plain(grad_group, weight_out)
    grad_out_w = dot_left(grad_group, hidden)
    grad_pre = gelu_pull(grad_hidden)[0].astype(jnp.bfloat16)
    grad_in_w = dot_left(group_in, grad_pre)
    grad_pieces = lax.all_gather(dot_right(grad_pre, weight_in), "mp", axis=1, tiled=True)
    grad_attended = grad_sum_two + pair_sum(grad_pieces, part)
    grad_sum_one, grad_small_one = norm_one_pull(grad_attended)
    grad_proj = grad_sum_one.astype(jnp.bfloat16)
    grad_proj_cols = lax.dynamic_slice_in_dim(grad_proj, shard_index * part, part, 1)
    grad_proj_w = dot_left(grad_proj_cols, gathered)
    grad_heads = lax.psum_scatter(
        dot_plain(grad_proj_cols, weights[3]), "mp", scatter_dimension=1, tiled=True
    )
    grad_heads = grad_heads.astype(jnp.bfloat16).reshape(seqs, length, part)
    grad_qkv, grad_taps_seq = lax.map(
        partial(heads_backward, shard_index, taps),
        (qkv_seq[0], qkv_seq[1], qkv_seq[2], lengths, log_totals, grad_heads),
    )
    grad_qkv = jnp.moveaxis(grad_qkv, 1, 0).reshape(3, tokens, part).astype(jnp.bfloat16)
    grad_taps = jnp.sum(grad_taps_seq, axis=0)
    grad_qkv_w = jnp.einsum("ktp,td->kpd", grad_qkv, low_in, preferred_element_type=jnp.float32)
    grad_embed_part = jnp.einsum(
        "ktp,kpd->td", grad_qkv, weights[0:3], preferred_element_type=jnp.float32
    )
    grad_embedded = grad_sum_one + lax.psum(grad_embed_part, "mp")
    grad_word, grad_small_zero = embed_pull(grad_embedded.reshape(seqs, length, width))
    grad_word = jnp.where(word_mine[:, None], grad_word.reshape(tokens, width), 0.0)
    grad_table = grad_table.at[word_row].add(grad_word)
    grad_table_own = lax.psum_scatter(grad_table, "dp", scatter_dimension=0, tiled=True)
    grad_units = jnp.concatenate(
        [
            grad_qkv_w,
            grad_proj_w[None],
            grad_in_w.reshape(2, part, width),
            grad_out_w.reshape(2, part, width),
        ],
        axis=0,
    )
    grad_small = grad_small_zero + grad_small_one + grad_small_two + grad_small_sop
    units_sum, small_sum, taps_sum, loss = lax.psum(
        (grad_units, grad_small, grad_taps, mlm_part + sop_part), "dp"
    )
    square = (
        jnp.sum(grad_table_own * grad_table_own)
        + (jnp.sum(units_sum * units_sum) + jnp.sum(taps_sum * taps_sum)) / dp_count
        + jnp.sum(small_sum * small_sum) / (dp_count * mp_count)
    )
    norm_square, taps_full = lax.psum((square, taps_sum / dp_count), ("dp", "mp"))
    grad_norm = jnp.sqrt(norm_square)
    scale = clip_bound / jnp.maximum(grad_norm, clip_bound)
    count = step_count[0].astype(jnp.float32)
    table_new, table_m_new, table_v_new = adam(
        table, table_m, table_v, grad_table_own * scale, count
    )
    grad_slots = jnp.einsum("ck,kpd->cpd", selector, units_sum, precision=highest)
    used = jnp.sum(selector, axis=1)[:, None, None]
    unit_new, unit_m_new, unit_v_new = adam(unit_master, unit_m, unit_v, grad_slots * scale, count)
    unit_new = unit_new * used
    unit_m_new = unit_m_new * used
    unit_v_new = unit_v_new * used
    small_new, small_m_new, small_v_new = adam(small, small_m, small_v, small_sum * scale, count)
    taps_new, taps_m_new, taps_v_new = adam(taps, taps_m, taps_v, taps_full * scale, count)
    return (
        loss,
        grad_norm,
        table_new,
        table_m_new,
        table_v_new,
        table_new.astype(jnp.bfloat16),
        unit_new,
        unit_m_new,
        unit_v_new,
        unit_new.astype(jnp.bfloat16),
        small_new,
        small_m_new,
        small_v_new,
        taps_new,
        taps_m_new,
        taps_v_new,
    )


def solution(mesh):
    placed = (
        P("dp", None),
        P("dp"),
        P("dp"),
        P("dp", None),
        P("dp", None),
        P("dp"),
        P(),
        P(),
        P(("dp", "mp"), None),
        P(("dp", "mp"), None),
        P(("dp", "mp"), None),
        P("dp", "mp", None),
        P("dp", "mp", None),
        P("dp", "mp", None),
        P(),
        P(),
        P(),
        P(),
        P(),
        P(),
    )
    return jax.shard_map(
        body,
        mesh=mesh,
        in_specs=placed,
        out_specs=(
            P(),
            P(),
            P(("dp", "mp"), None),
            P(("dp", "mp"), None),
            P(("dp", "mp"), None),
            P(("dp", "mp"), None),
            P("dp", "mp", None),
            P("dp", "mp", None),
            P("dp", "mp", None),
            P("dp", "mp", None),
            P(),
            P(),
            P(),
            P(),
            P(),
            P(),
        ),
        check_vma=False,
    )
```

profile of v0, /device:TPU:0, one launch (start us, length us, event | category | flops | bytes accessed | tf_op | source)
XLA Modules:
  0.0 2733.3 jit_solution(881599179814197127)
XLA Ops:
  40.2 140.2 %all-gather.12.cloned.1.call-done = bf16[7680,768]{1,0:T(8,128)(2,1)} async-done(((bf16[960,768]{1,0:T(8,128)(2,1)}), bf16[7680,768]{1,0:T(8,128)(2,1)}) %all-gather.12.cloned.1.call-update) | async-done | bytes 11796496 | tf_op jit(solution)/shard_map/all_gather | solution.py:270
  180.4 24.9 gather_fusion
  232.0 22.1 copy.402
  254.8 41.1 %all-reduce.88.cloned.1.call-done = (bf16[192,768]{1,0:T(8,128)(2,1)}, bf16[1,192,768]{2,1,0:T(8,128)(2,1)}, bf16[1,192,768]{2,1,0:T(8,128)(2,1)}, bf16[1,192,76...) async-done(((bf16[192,768]{1,0:T(8,128)(2,1)}, ...) | async-done | bytes 2359312 | tf_op jit(solution)/shard_map/psum | solution.py:24
  300.9 115.9 %all-reduce.80.cloned.1.call-done = bf16[4096,768]{0,1:T(8,128)(2,1)} async-done(((bf16[4096,768]{0,1:T(8,128)(2,1)}), bf16[4096,768]{0,1:T(8,128)(2,1)}) %all-reduce.80.cloned.1.call-update) | async-done | bytes 6291472 | tf_op jit(solution)/shard_map/psum | solution.py:279
  448.1 73.7 %while.49 = (s32[]{:T(128)}, bf16[8,512,192]{2,1,0:T(8,128)(2,1)}, f32[8,512,3]{1,2,0:T(4,128)}, pred[]{:T(512)}, bf16[8,512,192]{2,1,0:T(8,128)(2,1)}, /*index=...) while((s32[]{:T(128)}, bf16[8,512,192]{2,1,0:T(8,128)(2,1)}, ...), condition=%wide.region_26.27_spmd, body=%wide.region_7.26_spmd.sunk | while | flops 208210944 | bytes 13109668 | solution.py:290
  525.9 46.5 %all-gather.14.cloned.1.call-done = bf16[4096,768]{0,1:T(8,128)(2,1)} async-done(((bf16[4096,192]{0,1:T(8,128)(2,1)}), bf16[4096,768]{0,1:T(8,128)(2,1)}) %all-gather.14.cloned.1.call-update) | async-done | bytes 6291472 | tf_op jit(solution)/shard_map/all_gather | solution.py:293
  578.1 46.3 %all-gather.16.cloned.1.call-done = bf16[4096,768]{0,1:T(8,128)(2,1)} async-done(((bf16[4096,192]{0,1:T(8,128)(2,1)}), bf16[4096,768]{0,1:T(8,128)(2,1)}) %all-gather.16.cloned.1.call-update) | async-done | bytes 6291472 | tf_op jit(solution)/shard_map/all_gather | solution.py:297
  651.7 32.8 %multiply_convert_fusion.4 = (bf16[4096,768]{0,1:T(8,128)(2,1)S(1)}, f32[4096,768]{0,1:T(8,128)}, f32[4096,768]{0,1:T(8,128)}) fusion(bf16[384,768]{1,0:T(8,128)(2,1)S(1)} %get-tuple-element.1794, f32[4096,768]{0,1:T(8,128)} %multiply_add_fusion.5, s32[]{:T(128)S(6)} %select_n.363), kind=kOutput, calls=%fused_computation.292 | convolution fusion | flops 2620391424 | bytes 35192836 | tf_op jit(solution)/shard_map/dot_general | solution.py:50
  693.2 154.3 %all-gather.18.cloned.1.call-done = f32[4096,1536]{1,0:T(8,128)} async-done(((f32[4096,384]{1,0:T(8,128)}), f32[4096,1536]{1,0:T(8,128)}) %all-gather.18.cloned.1.call-update) | async-done | bytes 25165840 | tf_op jit(solution)/shard_map/all_gather | solution.py:308
  847.5 29.6 %reshape.902 = f32[4096,2,2,384]{3,2,1,0:T(2,128)} reshape(f32[4096,1536]{1,0:T(8,128)} %all-gather.18.cloned.1.call-done) | data formatting | bytes 50331648 | tf_op jit(solution)/shard_map/reshape | solution.py:100
  877.1 46.3 %reduce_sum.772 = f32[4096,2,384]{2,1,0:T(2,128)} reduce(f32[4096,2,2,384]{3,2,1,0:T(2,128)} %reshape.902, f32[]{:T(128)} %constant.510.clone.1), dimensions={2}, to_apply=%region_34.35 | reduce | flops 3145728 | bytes 37748740 | tf_op jit(solution)/shard_map/reduce_sum | solution.py:100
  923.4 19.1 copy.301
  1069.2 46.1 %all-reduce.82.cloned.1.call-done = f32[640,768]{1,0:T(8,128)} async-done(((f32[640,768]{1,0:T(8,128)}), f32[640,768]{1,0:T(8,128)}) %all-reduce.82.cloned.1.call-update) | async-done | bytes 1966096 | tf_op jit(solution)/shard_map/psum | solution.py:327
  1178.9 15.9 add_convert_fusion
  1204.3 154.6 %all-gather.20.cloned.1.call-done = f32[4096,1536]{1,0:T(8,128)} async-done(((f32[4096,384]{1,0:T(8,128)}), f32[4096,1536]{1,0:T(8,128)}) %all-gather.20.cloned.1.call-update) | async-done | bytes 25165840 | tf_op jit(solution)/shard_map/all_gather | solution.py:349
  1358.9 29.4 %reshape.906 = f32[4096,2,2,384]{3,2,1,0:T(2,128)} reshape(f32[4096,1536]{1,0:T(8,128)} %all-gather.20.cloned.1.call-done) | data formatting | bytes 50331648 | tf_op jit(solution)/shard_map/reshape | solution.py:100
  1388.3 46.3 %reduce_sum.782 = f32[4096,2,384]{2,1,0:T(2,128)} reduce(f32[4096,2,2,384]{3,2,1,0:T(2,128)} %reshape.906, f32[]{:T(128)} %constant.510.clone.1), dimensions={2}, to_apply=%region_52.53 | reduce | flops 3145728 | bytes 37748740 | tf_op jit(solution)/shard_map/reduce_sum | solution.py:100
  1434.5 19.1 copy.308
  1453.7 15.8 fusion.192
  1497.3 95.9 %reduce-scatter.3.cloned.1.call-done = f32[4096,192]{0,1:T(8,128)} async-done(((f32[4096,768]{0,1:T(8,128)}), f32[4096,192]{0,1:T(8,128)}) %reduce-scatter.3.cloned.1.call-update) | async-done | bytes 3145744 | tf_op jit(solution)/shard_map/reduce_scatter | solution.py:355
  1597.7 122.4 %while.51 = (s32[]{:T(128)}, bf16[8,3,512,192]{3,2,1,0:T(8,128)(2,1)}, f32[8,9,384]{2,1,0:T(8,128)S(1)}, pred[]{:T(512)}, bf16[8,512,192]{1,2,0:T(8,128)(2,1)}, ...) while((s32[]{:T(128)}, ...), condition=%wide.region_102.103_spmd, body=%wide.region_56.102_spmd.sunk | while | flops 514131072 | bytes 36124104 | solution.py:359
  1757.5 21.6 copy.407
  1814.9 165.3 %all-reduce.84.cloned.1.call-done = f32[4096,768]{0,1:T(8,128)} async-done(((f32[4096,768]{0,1:T(8,128)}), f32[4096,768]{0,1:T(8,128)}) %all-reduce.84.cloned.1.call-update) | async-done | bytes 12582928 | tf_op jit(solution)/shard_map/psum | solution.py:369
  1980.3 19.6 multiply_reduce_fusion.10
  2015.3 21.7 copy.406
  2063.8 16.9 fusion.243
  2093.3 43.5 %scatter_fusion.1 = f32[7680,768]{1,0:T(8,128)} fusion(f32[7680,768]{1,0:T(8,128)} %fusion.243, s32[4096]{0:T(1024)S(1)} %bitcast.543, f32[4096,768]{1,0:T(8,128)} %copy.315), kind=kCustom, calls=%fused_computation.6 | custom fusion | flops 3145728 | bytes 37765120 | tf_op jit(solution)/shard_map/scatter-add | solution.py:372
  2139.0 38.2 %all-reduce.71 = (f32[]{:T(128)}, f32[9,384]{1,0:T(8,128)S(1)}) all-reduce(f32[]{:T(128)S(6)} %add.893, f32[9,384]{1,0:T(8,128)S(1)} %reduce_sum.789), channel_id=1, replica_groups=mesh['dp'=8,'mp'=4] {'dp'}, use_global_device_ids=true, to_apply=%region_46.47 | all-reduce | flops 3457 | bytes 27656 | tf_op jit(solution)/shard_map/psum | solution.py:384
  2177.9 101.9 %all-reduce.86.cloned.1.call-done = (f32[8,192,768]{2,1,0:T(8,128)}, f32[522,768]{1,0:T(8,128)}) async-done(((f32[8,192,768]{2,1,0:T(8,128)}, f32[522,768]{1,0:T(8,128)}), (f32[8,192,768]{2,1,0:T(8,128)}, f32[522,768]{1,0:T(8,128)})) %all-reduce.86.cloned.1.call-update) | async-done | bytes 6322192 | tf_op jit(solution)/shard_map/psum | solution.py:384
  2297.5 366.1 %reduce-scatter.5.cloned.1.call-done = f32[960,768]{1,0:T(8,128)} async-done(((f32[7680,768]{1,0:T(8,128)}), f32[960,768]{1,0:T(8,128)}) %reduce-scatter.5.cloned.1.call-update) | async-done | bytes 2949136 | tf_op jit(solution)/shard_map/reduce_scatter | solution.py:373
  2667.5 40.0 %all-reduce.70 = (f32[]{:T(128)}, f32[9,384]{1,0:T(8,128)S(1)}) all-reduce(f32[]{:T(128)S(6)} %add.906, f32[9,384]{1,0:T(8,128)S(1)} %get-tuple-element.1749), channel_id=1, replica_groups=mesh['dp'=8,'mp'=4] {'dp','mp'}, use_global_device_ids=true, to_apply=%region_125.126 | all-reduce | flops 3457 | bytes 27656 | tf_op jit(solution)/shard_map/psum | solution.py:392
  (1186 shorter events, 807.9 us)
Async XLA Ops:
  7.2 173.2 %all-gather.12.cloned.1.call-start = ((), (), s32[]{:S(2)}) async-start(), calls=%async_computation.2 | async-start | bytes 13271040 | tf_op jit(solution)/shard_map/all_gather | solution.py:270
  10.3 285.5 %all-reduce.88.cloned.1.call-start = ((), (), s32[]{:S(2)}) async-start(), calls=%async_computation.13 | async-start | bytes 4718592 | tf_op jit(solution)/shard_map/psum | solution.py:24
  39.1 377.7 %all-reduce.80.cloned.1.call-start = ((), (), s32[]{:S(2)}) async-start(), calls=%async_computation.3 | async-start | bytes 12582912 | tf_op jit(solution)/shard_map/psum | solution.py:279
  39.3 174.8 %copy-start.74 = (pred[4096]{0:T(1024)(128)(4,1)}, pred[4096]{0:T(1024)(128)(4,1)S(1)}, u32[]{:S(2)}) copy-start(pred[4096]{0:T(1024)(128)(4,1)S(1)} %fusion.147) | copy-start | bytes 12292
  221.7 350.8 %all-gather.14.cloned.1.call-start = ((), (), s32[]{:S(2)}) async-start(), calls=%async_computation.4 | async-start | bytes 7864320 | tf_op jit(solution)/shard_map/all_gather | solution.py:293
  222.6 194.2 %copy-start.40 = (f32[1,4,8,128]{3,1,2,0:T(4,128)}, f32[1,4,8,128]{3,1,2,0:T(4,128)S(1)}, u32[]{:S(2)}) copy-start(f32[1,4,8,128]{3,1,2,0:T(4,128)S(1)} %copy.403) | copy-start | bytes 49156
  254.8 170.2 %copy-start.70 = (f32[768]{0:T(1024)}, f32[768]{0:T(1024)S(1)}, u32[]{:S(2)}) copy-start(f32[768]{0:T(1024)S(1)} %get-tuple-element.1481) | copy-start | bytes 9220
  254.8 170.2 %copy-start.72 = (f32[768]{0:T(1024)}, f32[768]{0:T(1024)S(1)}, u32[]{:S(2)}) copy-start(f32[768]{0:T(1024)S(1)} %get-tuple-element.1482) | copy-start | bytes 9220
  254.8 369.7 %copy-start.60 = (f32[768]{0:T(1024)}, f32[768]{0:T(1024)S(1)}, u32[]{:S(2)}) copy-start(f32[768]{0:T(1024)S(1)} %get-tuple-element.1480) | copy-start | bytes 9220
  254.8 369.7 %copy-start.79 = (f32[768]{0:T(1024)}, f32[768]{0:T(1024)S(1)}, u32[]{:S(2)}) copy-start(f32[768]{0:T(1024)S(1)} %get-tuple-element.1479) | copy-start | bytes 9220
  254.8 687.8 %copy-start.46 = (f32[768]{0:T(1024)}, f32[768]{0:T(1024)S(1)}, u32[]{:S(2)}) copy-start(f32[768]{0:T(1024)S(1)} %get-tuple-element.1478) | copy-start | bytes 9220
  254.8 170.2 %copy-start.56 = (f32[4096]{0:T(1024)}, f32[4096]{0:T(1024)S(1)}, u32[]{:S(2)}) copy-start(f32[4096]{0:T(1024)S(1)} %broadcast_subtract_fusion) | copy-start | bytes 49156
  425.0 199.4 %copy-start.28 = (f32[4096]{0:T(1024)}, f32[4096]{0:T(1024)S(1)}, u32[]{:S(2)}) copy-start(f32[4096]{0:T(1024)S(1)} %broadcast_multiply_fusion.5) | copy-start | bytes 49156
  427.7 196.7 %copy-start.38 = (f32[4096]{0:T(1024)}, f32[4096]{0:T(1024)S(1)}, u32[]{:S(2)}) copy-start(f32[4096]{0:T(1024)S(1)} %get-tuple-element.1757) | copy-start | bytes 49156
  448.1 124.3 %copy-start.36 = (bf16[192,768]{1,0:T(8,128)(2,1)S(1)}, bf16[192,768]{1,0:T(8,128)(2,1)}, u32[]{:S(2)}) copy-start(bf16[192,768]{1,0:T(8,128)(2,1)} %get-tuple-element.1565) | copy-start | bytes 884740
  521.8 110.9 %copy-start.22 = (f32[9,64]{1,0:T(8,128)}, f32[9,64]{1,0:T(8,128)S(1)}, u32[]{:S(2)}) copy-start(f32[9,64]{1,0:T(8,128)S(1)} %get-tuple-element.2396) | copy-start | bytes 6916
  525.9 98.5 %all-gather.16.cloned.1.call-start = ((), (), s32[]{:S(2)}) async-start(), calls=%async_computation.5 | async-start | bytes 7864320 | tf_op jit(solution)/shard_map/all_gather | solution.py:297
  577.9 269.6 %all-gather.18.cloned.1.call-start = ((), (), s32[]{:S(2)}) async-start(), calls=%async_computation.6 | async-start | bytes 31457280 | tf_op jit(solution)/shard_map/all_gather | solution.py:308
  632.8 309.7 %copy-start.26 = (f32[4096]{0:T(1024)}, f32[4096]{0:T(1024)S(1)}, u32[]{:S(2)}) copy-start(f32[4096]{0:T(1024)S(1)} %broadcast_multiply_fusion.4) | copy-start | bytes 49156
  639.4 303.1 %copy-start.30 = (f32[4096]{0:T(1024)}, f32[4096]{0:T(1024)S(1)}, u32[]{:S(2)}) copy-start(f32[4096]{0:T(1024)S(1)} %fusion.151) | copy-start | bytes 49156
  692.6 422.7 %all-reduce.82.cloned.1.call-start = ((), (), s32[]{:S(2)}) async-start(), calls=%async_computation.7 | async-start | bytes 3932160 | tf_op jit(solution)/shard_map/psum | solution.py:327
  693.1 375.1 %copy-start.91 = (s32[8]{0:T(128)}, s32[8]{0:T(128)S(1)}, u32[]{:S(2)}) copy-start(s32[8]{0:T(128)S(1)} %get-tuple-element.1769) | copy-start | bytes 100
  1065.9 293.0 %all-gather.20.cloned.1.call-start = ((), (), s32[]{:S(2)}) async-start(), calls=%async_computation.8 | async-start | bytes 31457280 | tf_op jit(solution)/shard_map/all_gather | solution.py:349
  1203.8 389.3 %reduce-scatter.3.cloned.1.call-start = ((), (), s32[]{:S(2)}) async-start(), calls=%async_computation.9 | async-start | bytes 15728640 | tf_op jit(solution)/shard_map/reduce_scatter | solution.py:355
  1493.9 486.3 %all-reduce.84.cloned.1.call-start = ((), (), s32[]{:S(2)}) async-start(), calls=%async_computation.10 | async-start | bytes 25165824 | tf_op jit(solution)/shard_map/psum | solution.py:369
  1747.7 532.1 %all-reduce.86.cloned.1.call-start = ((), (), s32[]{:S(2)}) async-start(), calls=%async_computation.12 | async-start | bytes 12681216 | tf_op jit(solution)/shard_map/psum | solution.py:384
  1814.9 184.9 %copy-start.49 = (f32[4096]{0:T(1024)S(1)}, f32[4096]{0:T(1024)}, u32[]{:S(2)}) copy-start(f32[4096]{0:T(1024)} %copy-done.48) | copy-start | bytes 49156
  2063.8 599.9 %reduce-scatter.5.cloned.1.call-start = ((), (), s32[]{:S(2)}) async-start(), calls=%async_computation.11 | async-start | bytes 26542080 | tf_op jit(solution)/shard_map/reduce_scatter | solution.py:373
  2279.8 434.5 %copy-start.64 = (f32[9,384]{1,0:T(8,128)S(1)}, f32[9,384]{1,0:T(8,128)}, u32[]{:S(2)}) copy-start(f32[9,384]{1,0:T(8,128)} %param.55) | copy-start | bytes 41476
  2279.8 434.5 %copy-start.77 = (f32[9,384]{1,0:T(8,128)S(1)}, f32[9,384]{1,0:T(8,128)}, u32[]{:S(2)}) copy-start(f32[9,384]{1,0:T(8,128)} %param.57) | copy-start | bytes 41476
  2279.8 434.5 %copy-start.78 = (f32[9,384]{1,0:T(8,128)S(1)}, f32[9,384]{1,0:T(8,128)}, u32[]{:S(2)}) copy-start(f32[9,384]{1,0:T(8,128)} %param.56) | copy-start | bytes 41476
  2297.5 422.8 %copy-start.12 = (f32[960,768]{1,0:T(8,128)S(1)}, f32[960,768]{1,0:T(8,128)}, u32[]{:S(2)}) copy-start(f32[960,768]{1,0:T(8,128)} %param.46) | copy-start | bytes 8847364
  (90 other events, 2243.2 us)
Sparse Core Ops, SparseCore 0:
  10.8 169.5 all-gather.11
  186.0 109.8 all-reduce.87
  298.4 118.4 all-reduce.79
  526.0 46.3 all-gather.13
  578.0 46.3 all-gather.15
  692.7 154.8 all-gather.17
  1066.0 49.2 all-reduce.81
  1204.0 154.8 all-gather.19
  1494.0 99.0 reduce-scatter.2
  1747.8 232.3 all-reduce.83
  2063.9 215.8 all-reduce.85
  2284.0 379.5 reduce-scatter.4
where the time goes:
time: 2740 us; the launch traced here: 2730 us
  waiting for transfers between devices  1470 us (54%)
  other arithmetic  489 us (18%)
  local copies, waits for them, and re-layouts  396 us (14%)
  matrix products  230 us (8%)
  blocking collectives  93.7 us (3%)
  between operations  43.3 us (2%)
    reduce_scatter x1, waiting for transfers between devices, body(): lax.psum_scatter(grad_table, 'dp', scatter_dimension=0, tiled=True)  366 us
    psum x1, waiting for transfers between devices, body(): grad_embedded = grad_sum_one + lax.psum(grad_embed_part, 'mp')  165 us
    all_gather x1, waiting for transfers between devices, body(): lax.all_gather(dot_right(grad_pre, weight_in), 'mp', axis=1, tiled=True)  155 us
    all_gather x1, waiting for transfers between devices, body(): lax.all_gather(dot_right(hidden, weight_out), 'mp', axis=1, tiled=True)  154 us
    all_gather x1, waiting for transfers between devices, body(): vocab = lax.all_gather(table.astype(jnp.bfloat16), 'dp', axis=0, tiled=True)  140 us
    psum x1, waiting for transfers between devices, body(): lax.psum(picked_rows.astype(jnp.bfloat16), 'mp').astype(jnp.float32)  116 us
    psum x1, waiting for transfers between devices, body(): lax.psum((grad_units, grad_small, grad_taps, mlm_part + sop_part), 'dp')  102 us
    reduce_scatter x1, waiting for transfers between devices, body(): lax.psum_scatter(dot_plain(grad_proj_cols, weights[3]), 'mp', scatter_dim...  95.9 us
  transfers between devices with their start and end apart: 12, of which 12 were waited for; matrix products, arithmetic and copies ran while one was open for 9% of the time, Pallas kernels for 0%

commit v1 on v0

v1 whole, which is shorter than its diff:
```python
import math
from functools import partial

import jax
import jax.numpy as jnp
from jax import lax
from jax.sharding import Mesh, PartitionSpec as P

DH = 64
HEADS = 12
PER = 3
ATTN = tuple(h for h in range(HEADS) if h % PER < PER - h // PER)
CONV = tuple(h for h in range(HEADS) if h % PER >= PER - h // PER)

DP = ("dh", "dl")
MP = ("mh", "ml")
ALL = DP + MP
VG = ("dl", "mh", "ml")
RG = ("dh",)

f32 = jnp.float32
bf16 = jnp.bfloat16
i32 = jnp.int32
highest = lax.Precision.HIGHEST
beta_one = 0.9
beta_two = 0.999
adam_eps = 1e-08
learn_rate = 0.03
weight_decay = 0.01
clip_bound = 0.02
norm_eps = 1e-06


def dot_right(left, right):
    return lax.dot_general(left, right, (((1,), (1,)), ((), ())), preferred_element_type=f32)


def dot_left(left, right):
    return lax.dot_general(left, right, (((0,), (0,)), ((), ())), preferred_element_type=f32)


def dot_plain(left, right):
    return lax.dot_general(left, right, (((1,), (0,)), ((), ())), preferred_element_type=f32)


def halves(x):
    high = lax.reduce_precision(x, 8, 7)
    return high.astype(bf16), (x - high).astype(bf16)


def select_sum(chosen, values):
    high, low = halves(values)
    return dot_left(chosen, high) + dot_left(chosen, low)


def layer_norm(stream, gain, offset):
    center = jnp.mean(stream, axis=-1, keepdims=True)
    shifted = stream - center
    spread = jnp.mean(shifted * shifted, axis=-1, keepdims=True)
    return shifted * lax.rsqrt(spread + norm_eps) * gain + offset


def norm_piece(stream, params, index):
    return layer_norm(stream, params[index], params[index + 3])


def embed_rows(word_rows, params, split_at):
    length = word_rows.shape[-2]
    second = (jnp.arange(length)[None, :] > split_at[:, None]).astype(f32)[..., None]
    summed = (
        word_rows
        + params[6 : 6 + length]
        + params[6 + length] * (1.0 - second)
        + params[7 + length] * second
    )
    return layer_norm(summed, params[0], params[3])


def conv_heads(queries, key_rows, values, taps):
    length = queries.shape[1]
    width = taps.shape[1]
    logits = jnp.einsum("bthd,hod->btho", queries * key_rows, taps, precision=highest)
    kernel = jax.nn.softmax(logits, axis=-1)
    half = width // 2
    padded = jnp.pad(values, ((0, 0), (half, half), (0, 0), (0, 0)))
    total = jnp.zeros_like(values)
    for offset in range(width):
        total = total + kernel[..., offset : offset + 1] * padded[:, offset : offset + length]
    return total


def exact_gelu(values):
    return jax.nn.gelu(values, approximate=False)


def sop_loss(cls_rows, params, labels, denom, length):
    logits = jnp.dot(cls_rows, params[length + 8 : length + 10].T, precision=highest)
    chosen = jnp.take_along_axis(logits, labels[:, None], axis=1)[:, 0]
    return jnp.sum(jax.nn.logsumexp(logits, axis=-1) - chosen) / denom


def adam(weight, first, second, grad, count):
    first_new = beta_one * first + (1.0 - beta_one) * grad
    second_new = beta_two * second + (1.0 - beta_two) * grad * grad
    corr_one = 1.0 - jnp.power(beta_one, count)
    corr_two = 1.0 - jnp.power(beta_two, count)
    step = first_new / corr_one / (jnp.sqrt(second_new / corr_two) + adam_eps)
    return (weight - learn_rate * (step + weight_decay * weight), first_new, second_new)


def everyone(x, axes):
    count = lax.axis_size(axes)
    return lax.all_to_all(jnp.broadcast_to(x, (count,) + x.shape), axes, 0, 0, tiled=True)


def pick_heads(x, heads):
    return jnp.stack([x[:, :, h * DH : (h + 1) * DH] for h in heads], axis=2)


def attention_scores(queries, key_rows, lengths):
    scores = jnp.einsum("bqhd,bkhd->bhqk", queries, key_rows, preferred_element_type=f32)
    allowed = jnp.arange(key_rows.shape[1])[None, :] < lengths[:, None]
    return jnp.where(allowed[:, None, None, :], scores / math.sqrt(DH), -1e30)


def slots_of(ids, vblock, devices):
    owner = ids // vblock
    here = jnp.arange(ids.shape[0])
    same = ids[None, :] == ids[:, None]
    first = jnp.sum(jnp.logical_and(same, here[None, :] < here[:, None]), axis=1) == 0
    below = jnp.logical_and(owner[None, :] == owner[:, None], ids[None, :] < ids[:, None])
    rank = jnp.sum(jnp.logical_and(below, first[None, :]), axis=1).astype(i32)
    return owner, first, rank


def fetch_round(turn, capacity, devices, owner, first, rank, local, low_table):
    slot = jnp.where(rank // capacity == turn, owner * capacity + rank % capacity, -1)
    seats = jnp.arange(devices * capacity)
    chosen = jnp.logical_and(seats[:, None] == slot[None, :], first[None, :])
    request = jnp.sum(jnp.where(chosen, local[None, :] + 1, 0), axis=1) - 1
    message = jnp.full((devices, 128), jnp.max(rank), i32)
    message = message.at[:, :capacity].set(request.reshape(devices, capacity))
    got = lax.all_to_all(message, ALL, 0, 0, tiled=True)
    asked = got[:, :capacity].reshape(-1)
    served = (asked[:, None] == jnp.arange(low_table.shape[0])[None, :]).astype(bf16)
    rows = dot_plain(served, low_table).astype(bf16)
    rows = lax.all_to_all(rows, ALL, 0, 0, tiled=True)
    mine = (slot[:, None] == seats[None, :]).astype(bf16)
    return dot_plain(mine, rows), mine, served, jnp.max(got[:, capacity])


def return_round(mine, served, grad_word):
    sent = select_sum(mine, grad_word)
    got = lax.all_to_all(sent, ALL, 0, 0, tiled=True)
    return select_sum(served, got)


def body(
    token_ids,
    seg_split,
    lengths,
    mlm_pos,
    mlm_labels,
    sop_labels,
    owner,
    step_count,
    table,
    table_m,
    table_v,
    unit_master,
    unit_m,
    unit_v,
    small,
    small_m,
    small_v,
    taps,
    taps_m,
    taps_v,
):
    mp_count = lax.axis_size(MP)
    dp_count = lax.axis_size(DP)
    devices = mp_count * dp_count
    mp_index = lax.axis_index(MP)
    dp_index = lax.axis_index(DP)
    group_seqs, length = token_ids.shape
    width = small.shape[1]
    part = unit_master.shape[1]
    vblock = table.shape[0]
    cap_slots = unit_master.shape[0]
    matrices = owner.shape[0]
    seqs = group_seqs // mp_count
    tokens = seqs * length
    masks = mlm_pos.shape[1]
    total_seqs = group_seqs * dp_count
    count_all = total_seqs * masks

    def my(x):
        return lax.dynamic_slice_in_dim(x, mp_index * seqs, seqs, 0)

    token_ids, seg_split, lengths = my(token_ids), my(seg_split), my(lengths)
    mlm_pos, mlm_labels, sop_labels = my(mlm_pos), my(mlm_labels), my(sop_labels)

    earlier = jnp.arange(matrices)[:, None] > jnp.arange(matrices)[None, :]
    slot_rank = jnp.sum(jnp.logical_and(earlier, owner[:, None] == owner[None, :]), axis=1)
    slot_index = owner * cap_slots + slot_rank
    selector = jnp.logical_and(
        owner[None, :] == dp_index, slot_rank[None, :] == jnp.arange(cap_slots)[:, None]
    ).astype(f32)
    all_slots = lax.all_gather(unit_master.astype(bf16), DP, axis=0, tiled=True)
    picked = jnp.stack(
        [lax.dynamic_index_in_dim(all_slots, slot_index[k], 0, False) for k in range(matrices)]
    )
    gathered = lax.all_gather(picked, MP, axis=0)
    units = [gathered[:, k].reshape(mp_count * part, width) for k in range(matrices)]
    low_table = table.astype(bf16)
    vocab = lax.all_gather(low_table, RG, axis=0, tiled=True)

    ids = token_ids.reshape(-1)
    capacity = max(8, -(-1280 // devices))
    home, first, rank = slots_of(ids, vblock, devices)
    local = ids % vblock
    fetch = partial(
        fetch_round,
        capacity=capacity,
        devices=devices,
        owner=home,
        first=first,
        rank=rank,
        local=local,
        low_table=low_table,
    )
    word_rows, mine, served, top_rank = fetch(0)
    turns = top_rank // capacity + 1

    def more(state):
        return state[0] < turns

    def fetch_more(state):
        return (state[0] + 1, state[1] + fetch(state[0])[0])

    _, word_rows = lax.while_loop(more, fetch_more, (jnp.int32(1), word_rows))

    embedded, embed_pull = jax.vjp(
        partial(embed_rows, split_at=seg_split), word_rows.reshape(seqs, length, width), small
    )
    embedded = embedded.reshape(tokens, width)
    low_in = embedded.astype(bf16)
    qkv = [dot_right(low_in, units[k]).astype(bf16).reshape(seqs, length, width) for k in range(3)]
    qa, ka, va = [pick_heads(x, ATTN) for x in qkv]
    qc, kc, vc = [pick_heads(x, CONV).astype(f32) for x in qkv]
    scores = attention_scores(qa, ka, lengths)
    probs = jax.nn.softmax(scores, axis=-1)
    low_probs = probs.astype(bf16)
    out_a = jnp.einsum("bhqk,bkhd->bqhd", low_probs, va, preferred_element_type=f32)
    taps_heads = jnp.moveaxis(taps.reshape(taps.shape[0], len(CONV), DH), 1, 0)
    out_c, conv_pull = jax.vjp(conv_heads, qc, kc, vc, taps_heads)
    pieces = [None] * HEADS
    for at, head in enumerate(ATTN):
        pieces[head] = out_a[:, :, at]
    for at, head in enumerate(CONV):
        pieces[head] = out_c[:, :, at]
    heads = jnp.concatenate(pieces, axis=-1).reshape(tokens, width).astype(bf16)
    projected = dot_right(heads, units[3]).astype(bf16).astype(f32)
    attended, norm_one_pull = jax.vjp(partial(norm_piece, index=1), embedded + projected, small)
    low_mid = attended.astype(bf16)
    hidden_pre, ffn = [], []
    w_in, w_out, hidden, gelu_pull = [], [], [], []
    for s in range(mp_count):
        rows = slice(s * part, (s + 1) * part)
        w_in.append(jnp.concatenate([units[4][rows], units[5][rows]], axis=0))
        w_out.append(jnp.concatenate([units[6][rows], units[7][rows]], axis=0))
        g = s // 2
        low_group = low_mid[:, 2 * part * g : 2 * part * (g + 1)]
        pre = dot_plain(low_group, w_in[s])
        act, pull = jax.vjp(exact_gelu, pre)
        hidden.append(act.astype(bf16))
        gelu_pull.append(pull)
        ffn.append(dot_right(hidden[s], w_out[s]))
    ffn_out = jnp.concatenate([ffn[0] + ffn[1], ffn[2] + ffn[3]], axis=1)
    final_rows, norm_two_pull = jax.vjp(partial(norm_piece, index=2), attended + ffn_out, small)

    positions = (jnp.arange(seqs)[:, None] * length + mlm_pos).reshape(-1)
    at_mask = (positions[:, None] == jnp.arange(tokens)[None, :]).astype(bf16)
    masked_rows = dot_plain(at_mask, final_rows.astype(bf16)).astype(bf16)
    all_masked = lax.all_gather(masked_rows, VG, axis=0, tiled=True)
    all_labels = everyone(mlm_labels.reshape(-1), VG).reshape(-1)
    logits = dot_right(all_masked, vocab)
    copies = lax.axis_size(RG)
    group_count = lax.axis_size(VG)
    block = all_labels // vblock
    label_mine = block % group_count == lax.axis_index(VG)
    label_row = block // group_count * vblock + all_labels % vblock
    onehot = jnp.logical_and(
        jnp.arange(copies * vblock)[None, :] == label_row[:, None], label_mine[:, None]
    )
    top = jnp.max(logits, axis=1)
    total = jnp.sum(jnp.exp(logits - top[:, None]), axis=1)
    target = jnp.sum(jnp.where(onehot, logits, 0.0), axis=1)
    stats = everyone(jnp.stack([top, total, target]), VG)
    top_all = jnp.max(stats[:, 0], axis=0)
    total_all = jnp.sum(stats[:, 1] * jnp.exp(stats[:, 0] - top_all), axis=0)
    log_sum = top_all + jnp.log(total_all)
    mlm_part = jnp.sum(log_sum - jnp.sum(stats[:, 2], axis=0)) / count_all / group_count
    grad_logits = (
        (jnp.exp(logits - log_sum[:, None]) - onehot.astype(f32)) / count_all
    ).astype(bf16)
    grad_masked = lax.psum_scatter(
        dot_plain(grad_logits, vocab), VG, scatter_dimension=0, tiled=True
    )
    grad_table = lax.psum_scatter(
        dot_left(grad_logits, all_masked), RG, scatter_dimension=0, tiled=True
    )
    cls_index = jnp.arange(seqs) * length
    sop_part, sop_pull = jax.vjp(
        partial(sop_loss, labels=sop_labels, denom=total_seqs, length=length),
        final_rows[cls_index],
        small,
    )
    grad_cls, grad_small_sop = sop_pull(jnp.ones((), f32))
    grad_final = select_sum(at_mask, grad_masked).reshape(seqs, length, width)
    grad_final = jnp.concatenate(
        [grad_final[:, :1] + grad_cls[:, None], grad_final[:, 1:]], axis=1
    ).reshape(tokens, width)

    grad_sum_two, grad_small_two = norm_two_pull(grad_final)
    grad_ffn = grad_sum_two.astype(bf16)
    grad_in, grad_in_w, grad_out_w = [], [], []
    for s in range(mp_count):
        cols = slice(2 * part * (s // 2), 2 * part * (s // 2 + 1))
        grad_group = grad_ffn[:, cols]
        grad_hidden = dot_plain(grad_group, w_out[s])
        grad_out_w.append(dot_left(grad_group, hidden[s]))
        grad_pre = gelu_pull[s](grad_hidden)[0].astype(bf16)
        grad_in_w.append(dot_left(low_mid[:, cols], grad_pre))
        grad_in.append(dot_right(grad_pre, w_in[s]))
    grad_attended = grad_sum_two + jnp.concatenate(
        [grad_in[0] + grad_in[1], grad_in[2] + grad_in[3]], axis=1
    )
    grad_sum_one, grad_small_one = norm_one_pull(grad_attended)
    grad_proj = grad_sum_one.astype(bf16)
    grad_proj_w = dot_left(grad_proj, heads)
    grad_heads = dot_plain(grad_proj, units[3]).astype(bf16).reshape(seqs, length, width)
    ga = pick_heads(grad_heads, ATTN)
    gc = pick_heads(grad_heads, CONV).astype(f32)
    grad_probs = jnp.einsum("bqhd,bkhd->bhqk", ga, va, preferred_element_type=f32)
    grad_scores = (
        probs * (grad_probs - jnp.sum(probs * grad_probs, axis=-1, keepdims=True))
    ).astype(bf16)
    scale = 1.0 / math.sqrt(DH)
    dqa = jnp.einsum("bhqk,bkhd->bqhd", grad_scores, ka, preferred_element_type=f32) * scale
    dka = jnp.einsum("bhqk,bqhd->bkhd", grad_scores, qa, preferred_element_type=f32) * scale
    dva = jnp.einsum("bhqk,bqhd->bkhd", low_probs, ga, preferred_element_type=f32)
    dqc, dkc, dvc, grad_taps = conv_pull(gc)
    grad_taps = jnp.moveaxis(grad_taps, 0, 1).reshape(taps.shape)
    grad_qkv = []
    for attn_part, conv_part in ((dqa, dqc), (dka, dkc), (dva, dvc)):
        pieces = [None] * HEADS
        for at, head in enumerate(ATTN):
            pieces[head] = attn_part[:, :, at]
        for at, head in enumerate(CONV):
            pieces[head] = conv_part[:, :, at]
        grad_qkv.append(jnp.concatenate(pieces, axis=-1).reshape(tokens, width).astype(bf16))
    grad_qkv_w = [dot_left(g, low_in) for g in grad_qkv]
    grad_embedded = grad_sum_one + sum(dot_plain(grad_qkv[k], units[k]) for k in range(3))
    grad_word, grad_small_zero = embed_pull(grad_embedded.reshape(seqs, length, width))
    grad_word = grad_word.reshape(tokens, width)

    words = return_round(mine, served, grad_word)

    def return_more(state):
        _, mine_r, served_r, _ = fetch(state[0])
        return (state[0] + 1, state[1] + return_round(mine_r, served_r, grad_word))

    _, words = lax.while_loop(more, return_more, (jnp.int32(1), words))
    grad_table_own = grad_table + words

    def stack_parts(pieces):
        return jnp.stack([p.reshape(mp_count, part, width) for p in pieces], axis=1)

    in_w = jnp.stack([g.reshape(2, part, width) for g in grad_in_w])
    out_w = jnp.stack([g.reshape(2, part, width) for g in grad_out_w])
    grad_units = jnp.concatenate(
        [stack_parts(grad_qkv_w + [grad_proj_w]), in_w, out_w], axis=1
    ).reshape(mp_count * matrices * part, width)
    units_part = lax.psum_scatter(grad_units, MP, scatter_dimension=0, tiled=True)
    units_part = units_part.reshape(matrices, part * width)
    seat = (slot_index[None, :] == jnp.arange(dp_count * cap_slots)[:, None]).astype(f32)
    slotted = sum(seat[:, k, None] * units_part[k][None, :] for k in range(matrices))
    grad_slots = lax.psum_scatter(
        slotted.reshape(dp_count * cap_slots, part, width), DP, scatter_dimension=0, tiled=True
    )
    grad_small = grad_small_zero + grad_small_one + grad_small_two + grad_small_sop
    small_sum, taps_sum, loss = lax.psum((grad_small, grad_taps, mlm_part + sop_part), ALL)
    square = (
        jnp.sum(grad_table_own * grad_table_own)
        + jnp.sum(grad_slots * grad_slots)
        + (jnp.sum(taps_sum * taps_sum) + jnp.sum(small_sum * small_sum)) / devices
    )
    squares = everyone(jnp.full((128,), square, f32), ALL)
    grad_norm = jnp.sqrt(jnp.sum(squares[:, 0]))
    scale = clip_bound / jnp.maximum(grad_norm, clip_bound)
    count = step_count[0].astype(f32)
    table_new, table_m_new, table_v_new = adam(
        table, table_m, table_v, grad_table_own * scale, count
    )
    used = jnp.sum(selector, axis=1)[:, None, None]
    unit_new, unit_m_new, unit_v_new = adam(unit_master, unit_m, unit_v, grad_slots * scale, count)
    unit_new = unit_new * used
    unit_m_new = unit_m_new * used
    unit_v_new = unit_v_new * used
    small_new, small_m_new, small_v_new = adam(small, small_m, small_v, small_sum * scale, count)
    taps_new, taps_m_new, taps_v_new = adam(taps, taps_m, taps_v, taps_sum * scale, count)
    return (
        loss,
        grad_norm,
        table_new,
        table_m_new,
        table_v_new,
        table_new.astype(bf16),
        unit_new,
        unit_m_new,
        unit_v_new,
        unit_new.astype(bf16),
        small_new,
        small_m_new,
        small_v_new,
        taps_new,
        taps_m_new,
        taps_v_new,
    )


def solution(mesh):
    dp, mp = mesh.devices.shape
    fine = Mesh(mesh.devices.reshape(dp // 2, 2, mp // 2, 2), ALL)
    rows = P(DP)
    vocab = P(ALL)
    slots = P(DP, MP)
    placed = (rows,) * 6 + (P(),) * 2 + (vocab,) * 3 + (slots,) * 3 + (P(),) * 6
    return jax.shard_map(
        body,
        mesh=fine,
        in_specs=placed,
        out_specs=(P(),) * 2 + (vocab,) * 4 + (slots,) * 4 + (P(),) * 6,
        check_vma=False,
    )
```

time: 2740 us -> 1480 us (0.54)
  waiting for transfers between devices: 1470 us -> 624 us
  other arithmetic: 489 us -> 173 us
  local copies, waits for them, and re-layouts: 396 us -> 271 us
  blocking collectives: 93.7 us -> 124 us
    psum x5 -> x1, waiting for transfers between devices: 470 us -> 0.01 us  [body(): lax.psum((grad_small, grad_taps, mlm_part + sop_part), ALL)]
    all_gather x5 -> x4, waiting for transfers between devices: 542 us -> 81.9 us  [the longest x1 65.7 us: body(): all_slots = lax.all_gather(unit_master.astype(bf16), DP, axis=0, tiled=True)]
    reduce_sum x32 -> x13, other arithmetic: 119 us -> 30 us  [the longest x1 13.2 us: body(): total = jnp.sum(jnp.exp(logits - top[:, None]), axis=1)]
    unnamed x242 -> x624, local copies, waits for them, and re-layouts: 91.3 us -> 175 us
    scatter-add x3 -> x0, other arithmetic: 66.5 us -> none  [the longest x1 43.5 us: body(): grad_table = grad_table.at[word_row].add(grad_word)]
    reduce_sum x6 -> x4, other arithmetic: 70.3 us -> 7.5 us  [layer_norm(): return shifted * lax.rsqrt(spread + norm_eps) * gain + offset]
    all_to_all x0 -> x5, waiting for transfers between devices: none -> 49.4 us  [the longest x1 32.6 us: fetch_round(): rows = lax.all_to_all(rows, ALL, 0, 0, tiled=True)]
    gather x3 -> x0, local copies, waits for them, and re-layouts: 41.8 us -> none  [the longest x2 33.7 us: body(): vocab[word_row].astype(jnp.float32)]
  transfers between devices with their start and end apart: 12 -> 14, of which waited for: 12 -> 10; matrix products, arithmetic and copies ran while one was open for 9% -> 22% of each run, Pallas kernels for 0% -> 0%
where the time goes in v1:
time: 1480 us; the launch traced here: 1470 us
  waiting for transfers between devices  624 us (42%)
  local copies, waits for them, and re-layouts  271 us (18%)
  matrix products  214 us (14%)
  other arithmetic  173 us (12%)
  blocking collectives  124 us (8%)
  between operations  41.6 us (3%)
  starting transfers between devices  18.8 us (1%)
    reduce_scatter x1, waiting for transfers between devices, body(): lax.psum_scatter(dot_left(grad_logits, all_masked), RG, scatter_dimension...  184 us
    unnamed x624, local copies, waits for them, and re-layouts  175 us
    reduce_scatter x1, waiting for transfers between devices, body(): lax.psum_scatter(slotted.reshape(dp_count * cap_slots, part, width), DP,...  163 us
    psum x1, blocking collectives, body(): lax.psum((grad_small, grad_taps, mlm_part + sop_part), ALL)  116 us
    reduce_scatter x1, waiting for transfers between devices, body(): lax.psum_scatter(grad_units, MP, scatter_dimension=0, tiled=True)  115 us
    dot_general x16, matrix products, dot_plain(): lax.dot_general(left, right, (((1,), (0,)), ((), ())), preferred_element_...  82.9 us
    all_gather x1, waiting for transfers between devices, body(): all_slots = lax.all_gather(unit_master.astype(bf16), DP, axis=0, tiled=True)  65.7 us
    dot_general x19, matrix products, dot_left(): lax.dot_general(left, right, (((0,), (0,)), ((), ())), preferred_element_...  55 us
  transfers between devices with their start and end apart: 14, of which 10 were waited for; matrix products, arithmetic and copies ran while one was open for 22% of the time, Pallas kernels for 0%

profile of v1, /device:TPU:0, one launch (start us, length us, event | category | flops | bytes accessed | tf_op | source)
XLA Modules:
  0.0 1467.2 jit_solution(1929466778945774583)
XLA Ops:
  27.7 65.7 %all-gather.6.cloned.1.call-done = bf16[16,192,768]{2,1,0:T(8,128)(2,1)} async-done(((bf16[2,192,768]{2,1,0:T(8,128)(2,1)}), bf16[16,192,768]{2,1,0:T(8,128)(2,1)}) %all-gather.6.cloned.1.call-update) | async-done | bytes 4718608 | tf_op jit(solution)/shard_map/all_gather | solution.py:209
  118.0 5.8 all-to-all-done.4
  145.9 32.6 %all-to-all-done.5 = bf16[32,40,768]{2,1,0:T(8,128)(2,1)} async-done(((bf16[32,40,768]{2,1,0:T(8,128)(2,1)}), bf16[32,40,768]{2,1,0:T(8,128)(2,1)}, u32[]{:S(2)}, u32[]{:S(2)}) %all-to-all-start.5) | async-done | bytes 1966112 | tf_op jit(solution)/shard_map/all_to_all | solution.py:147
  258.5 9.6 add_convert_fusion.5
  315.6 7.3 fusion.272
  322.9 6.1 fusion.119
  342.5 9.4 multiply_convert_fusion.5
  353.4 9.2 multiply_convert_fusion.3
  364.1 9.2 multiply_convert_fusion.4
  374.6 9.6 multiply_convert_fusion.2
  402.0 16.2 %all-gather.8.cloned.1.call-done = bf16[1280,768]{1,0:T(8,128)(2,1)} async-done(((bf16[160,768]{1,0:T(8,128)(2,1)}), bf16[1280,768]{1,0:T(8,128)(2,1)}) %all-gather.8.cloned.1.call-update) | async-done | bytes 1966096 | tf_op jit(solution)/shard_map/all_gather | solution.py:285
  418.2 14.7 %fusion.275 = (f32[1280]{0:T(1024)S(1)}, f32[1280,3840]{1,0:T(8,128)}) fusion(bf16[1280,768]{1,0:T(8,128)(2,1)} %all-gather.8.cloned.1.call-done, bf16[3840,768]{1,0:T(8,128)(2,1)} %all-gather.10.cloned.1.call-done), kind=kOutput, calls=%fused_computation.665 | convolution fusion | flops 7554661376 | bytes 27530240 | tf_op jit(solution)/shard_map/dot_general | solution.py:35
  432.9 13.2 exponential_reduce_fusion
  446.2 8.2 all_to_all.137
  455.1 9.2 multiply_convert_fusion
  468.1 9.7 fusion.279
  480.8 5.9 copy.663
  496.8 30.9 %reduce-scatter.7.cloned.1.call-done = f32[160,768]{1,0:T(8,128)} async-done(((f32[1280,768]{1,0:T(8,128)}), f32[160,768]{1,0:T(8,128)}) %reduce-scatter.7.cloned.1.call-update) | async-done | bytes 491536 | tf_op jit(solution)/shard_map/reduce_scatter | solution.py:307
  535.8 5.9 copy.744
  586.5 11.9 multiply_reduce_fusion
  598.5 7.0 multiply_convert_fusion.1
  621.2 21.7 %convert_multiply_fusion.8 = (f32[2,512,6,64]{3,1,0,2:T(8,128)S(1)}, f32[2,512,6,64]{3,1,0,2:T(8,128)}, f32[2,512,6,64]{3,1,0,2:T(8,128)}, f32[2,512,6,64]{3,1,0...) fusion(bf16[2,512,6,64]{3,1,0,2:T(8,128)(2,1)} %fusion.173, ...), kind=kLoop, calls=%fused_computation.76 | loop fusion | flops 11347968 | bytes 17743872 | tf_op jit(solution)/shard_map/transpose(jvp())/mul | solution.py:88
  707.0 7.8 multiply_reduce_fusion.5
  741.1 12.4 fusion.53
  785.3 13.3 fusion.278
  817.7 115.6 %all-reduce.32 = (f32[]{:T(128)}, f32[9,384]{1,0:T(8,128)S(1)}) all-reduce(f32[]{:T(128)S(6)} %add.838, f32[9,384]{1,0:T(8,128)S(1)} %reshape.1309), channel_id=1, replica_groups=mesh['dh'=4,'dl'=2,'mh'=2,'ml'=2] {'dh','dl','mh','ml'}, use_global_device_ids=true, to_apply=%region_31.32 | all-reduce | flops 3457 | bytes 27656 | tf_op jit(solution)/shard_map/psum | solution.py:393
  941.2 114.8 %reduce-scatter.9.cloned.1.call-done = f32[1536,768]{1,0:T(8,128)} async-done(((f32[6144,768]{1,0:T(8,128)}), f32[1536,768]{1,0:T(8,128)}) %reduce-scatter.9.cloned.1.call-update) | async-done | bytes 4718608 | tf_op jit(solution)/shard_map/reduce_scatter | solution.py:385
  1058.7 7.3 multiply_add_fusion
  1074.2 183.5 %reduce-scatter.5.cloned.1.call-done = f32[960,768]{1,0:T(8,128)} async-done(((f32[3840,768]{1,0:T(8,128)}), f32[960,768]{1,0:T(8,128)}) %reduce-scatter.5.cloned.1.call-update) | async-done | bytes 2949136 | tf_op jit(solution)/shard_map/reduce_scatter | solution.py:310
  1263.5 162.7 %reduce-scatter.11.cloned.1.call-done = f32[2,192,768]{2,1,0:T(8,128)} async-done(((f32[16,192,768]{2,1,0:T(8,128)}), f32[2,192,768]{2,1,0:T(8,128)}) %reduce-scatter.11.cloned.1.call-update) | async-done | bytes 1179664 | tf_op jit(solution)/shard_map/reduce_scatter | solution.py:389
  1434.9 6.2 all-to-all-done.9
  1443.2 7.9 fusion.244
  (922 shorter events, 474.8 us)
Async XLA Ops:
  7.2 100.0 %copy-start = (s32[8,512]{1,0:T(8,128)S(1)}, s32[8,512]{1,0:T(8,128)}, u32[]{:S(2)}) copy-start(s32[8,512]{1,0:T(8,128)} %param.30) | copy-start | bytes 49156
  7.2 86.2 %all-gather.6.cloned.1.call-start = ((), (), s32[]{:S(2)}) async-start(), calls=%async_computation.14 | async-start | bytes 5308416 | tf_op jit(solution)/shard_map/all_gather | solution.py:209
  9.4 184.1 %all-gather.12.cloned.1.call-start = ((), (), s32[]{:S(2)}) async-start(), calls=%async_computation.22 | async-start | bytes 11796480 | tf_op jit(solution)/shard_map/all_gather | solution.py:213
  110.3 68.3 %copy-start.189 = (s32[1024]{0:T(1024)}, s32[1024]{0:T(1024)S(1)}, u32[]{:S(2)}) copy-start(s32[1024]{0:T(1024)S(1)} %get-tuple-element.779) | copy-start | bytes 12292
  114.0 9.8 all-to-all-start.4
  129.0 49.5 %all-to-all-start.5 = ((bf16[32,40,768]{2,1,0:T(8,128)(2,1)}), bf16[32,40,768]{2,1,0:T(8,128)(2,1)}, u32[]{:S(2)}, u32[]{:S(2)}) async-start(bf16[32,40,768]{2,1,0:T(8,128)(2,1)} %bitcast.679), calls=%async_computation.5 | async-start | bytes 3932160 | tf_op jit(solution)/shard_map/all_to_all | solution.py:147
  132.6 269.3 %all-gather.10.cloned.1.call-start = ((), (), s32[]{:S(2)}) async-start(), calls=%async_computation.16 | async-start | bytes 7372800 | tf_op jit(solution)/shard_map/all_gather | solution.py:216
  133.4 284.8 %all-gather.8.cloned.1.call-start = ((), (), s32[]{:S(2)}) async-start(), calls=%async_computation.15 | async-start | bytes 2211840 | tf_op jit(solution)/shard_map/all_gather | solution.py:285
  134.2 54.4 %copy-start.152 = (f32[1,4,2,128]{3,1,2,0:T(4,128)}, f32[1,4,2,128]{3,1,2,0:T(4,128)S(1)}, u32[]{:S(2)}) copy-start(f32[1,4,2,128]{3,1,2,0:T(4,128)S(1)} %copy.755) | copy-start | bytes 12292
  141.0 110.8 %copy-start.137 = (f32[9,6,64]{2,1,0:T(8,128)}, f32[9,6,64]{2,1,0:T(8,128)S(1)}, u32[]{:S(2)}) copy-start(f32[9,6,64]{2,1,0:T(8,128)S(1)} %reshape.1290) | copy-start | bytes 41476
  143.2 193.5 %copy-start.138 = (f32[768]{0:T(1024)}, f32[768]{0:T(1024)S(1)}, u32[]{:S(2)}) copy-start(f32[768]{0:T(1024)S(1)} %get-tuple-element.517) | copy-start | bytes 9220
  192.6 144.1 %copy-start.154 = (f32[1024]{0:T(1024)}, f32[1024]{0:T(1024)S(1)}, u32[]{:S(2)}) copy-start(f32[1024]{0:T(1024)S(1)} %get-tuple-element.769) | copy-start | bytes 12292
  393.0 8.5 all-to-all-start.6
  396.8 130.9 %reduce-scatter.7.cloned.1.call-start = ((), (), s32[]{:S(2)}) async-start(), calls=%async_computation.18 | async-start | bytes 4423680 | tf_op jit(solution)/shard_map/reduce_scatter | solution.py:307
  477.9 459.1 %all-reduce.35.cloned.1.call-start = ((), (), s32[]{:S(2)}) async-start(), calls=%async_computation.21 | async-start | bytes 3244032 | tf_op jit(solution)/shard_map/psum | solution.py:393
  761.6 294.4 %reduce-scatter.9.cloned.1.call-start = ((), (), s32[]{:S(2)}) async-start(), calls=%async_computation.19 | async-start | bytes 23592960 | tf_op jit(solution)/shard_map/reduce_scatter | solution.py:385
  783.8 473.9 %reduce-scatter.5.cloned.1.call-start = ((), (), s32[]{:S(2)}) async-start(), calls=%async_computation.17 | async-start | bytes 14745600 | tf_op jit(solution)/shard_map/reduce_scatter | solution.py:310
  807.0 259.0 %all-to-all-start.8 = ((f32[32,40,768]{2,1,0:T(8,128)}), f32[32,40,768]{2,1,0:T(8,128)}, u32[]{:S(2)}, u32[]{:S(2)}) async-start(f32[32,40,768]{2,1,0:T(8,128)} %bitcast.678), calls=%async_computation.10 | async-start | bytes 7864320 | tf_op jit(solution)/shard_map/all_to_all | solution.py:154
  811.7 614.5 %reduce-scatter.11.cloned.1.call-start = ((), (), s32[]{:S(2)}) async-start(), calls=%async_computation.20 | async-start | bytes 10616832 | tf_op jit(solution)/shard_map/reduce_scatter | solution.py:389
  941.1 117.5 %copy-start.191 = (f32[16]{0:T(128)S(1)}, f32[16]{0:T(128)}, u32[]{:S(2)}) copy-start(f32[16]{0:T(128)} %get-tuple-element.773) | copy-start | bytes 196
  941.1 117.5 %copy-start.192 = (f32[16]{0:T(128)S(1)}, f32[16]{0:T(128)}, u32[]{:S(2)}) copy-start(f32[16]{0:T(128)} %get-tuple-element.774) | copy-start | bytes 196
  941.1 117.5 %copy-start.193 = (f32[16]{0:T(128)S(1)}, f32[16]{0:T(128)}, u32[]{:S(2)}) copy-start(f32[16]{0:T(128)} %get-tuple-element.775) | copy-start | bytes 196
  941.1 117.5 %copy-start.194 = (f32[16]{0:T(128)S(1)}, f32[16]{0:T(128)}, u32[]{:S(2)}) copy-start(f32[16]{0:T(128)} %get-tuple-element.776) | copy-start | bytes 196
  941.1 117.5 %copy-start.195 = (f32[16]{0:T(128)S(1)}, f32[16]{0:T(128)}, u32[]{:S(2)}) copy-start(f32[16]{0:T(128)} %get-tuple-element.777) | copy-start | bytes 196
  1074.1 183.5 %copy-start.45 = (f32[960,768]{1,0:T(8,128)}, f32[960,768]{1,0:T(8,128)S(1)}, u32[]{:S(2)}) copy-start(f32[960,768]{1,0:T(8,128)S(1)} %get-tuple-element.419) | copy-start | bytes 8847364
  1257.7 176.4 %copy-start.206 = (s32[8]{0:T(128)S(1)}, s32[8]{0:T(128)}, u32[]{:S(2)}) copy-start(s32[8]{0:T(128)} %copy-done.205) | copy-start | bytes 100
  1257.7 176.4 %copy-start.207 = (pred[8]{0:T(512)(128)(4,1)S(1)}, pred[8]{0:T(512)(128)(4,1)}, u32[]{:S(2)}) copy-start(pred[8]{0:T(512)(128)(4,1)} %broadcast_compare_fusion.2) | copy-start | bytes 28
  1257.7 184.8 %copy-start.141 = (f32[9,384]{1,0:T(8,128)S(1)}, f32[9,384]{1,0:T(8,128)}, u32[]{:S(2)}) copy-start(f32[9,384]{1,0:T(8,128)} %param.47) | copy-start | bytes 41476
  1257.7 184.8 %copy-start.171 = (f32[9,384]{1,0:T(8,128)S(1)}, f32[9,384]{1,0:T(8,128)}, u32[]{:S(2)}) copy-start(f32[9,384]{1,0:T(8,128)} %param.49) | copy-start | bytes 41476
  1257.7 184.8 %copy-start.172 = (f32[9,384]{1,0:T(8,128)S(1)}, f32[9,384]{1,0:T(8,128)}, u32[]{:S(2)}) copy-start(f32[9,384]{1,0:T(8,128)} %param.48) | copy-start | bytes 41476
  1257.7 185.4 %copy-start.21 = (f32[960,768]{1,0:T(8,128)S(1)}, f32[960,768]{1,0:T(8,128)}, u32[]{:S(2)}) copy-start(f32[960,768]{1,0:T(8,128)} %param.38) | copy-start | bytes 8847364
  1430.3 10.8 all-to-all-start.9
  (213 other events, 1180.1 us)
Sparse Core Ops, SparseCore 0:
  10.8 82.5 all-gather.5
  107.2 83.6 all-gather.11
  193.1 108.8 all-gather.9
  391.8 26.3 all-gather.7
  478.0 49.5 reduce-scatter.6
  761.7 153.3 all-reduce.34
  917.7 138.3 reduce-scatter.8
  1058.5 199.1 reduce-scatter.4
  1261.7 164.4 reduce-scatter.10

commit v2 on v1

v2 whole, which is shorter than its diff:
```python
import math
from functools import partial

import jax
import jax.numpy as jnp
from jax import lax
from jax.experimental import pallas as pl
from jax.experimental.pallas import tpu as pltpu
from jax.sharding import Mesh, PartitionSpec as P

DH = 64
HEADS = 12
PER = 3
ATTN = tuple(h for h in range(HEADS) if h % PER < PER - h // PER)
CONV = tuple(h for h in range(HEADS) if h % PER >= PER - h // PER)

FIRST = min(CONV) // 2 * 2

DP = ("dh", "dl")
MP = ("mh", "ml")
ALL = DP + MP
VG = ("dh", "mh")
RG = ("dl", "ml")
CHIPS = ("dh", "dl", "mh")

f32 = jnp.float32
bf16 = jnp.bfloat16
i32 = jnp.int32
highest = lax.Precision.HIGHEST
beta_one = 0.9
beta_two = 0.999
adam_eps = 1e-08
learn_rate = 0.03
weight_decay = 0.01
clip_bound = 0.02
norm_eps = 1e-06
VMEM = 60 << 20


def dot_right(left, right):
    return lax.dot_general(left, right, (((1,), (1,)), ((), ())), preferred_element_type=f32)


def dot_left(left, right):
    return lax.dot_general(left, right, (((0,), (0,)), ((), ())), preferred_element_type=f32)


def dot_plain(left, right):
    return lax.dot_general(left, right, (((1,), (0,)), ((), ())), preferred_element_type=f32)


def halves(x):
    high = lax.reduce_precision(x, 8, 7)
    return high.astype(bf16), (x - high).astype(bf16)


def select_sum(chosen, values):
    high, low = halves(values)
    return dot_left(chosen, high) + dot_left(chosen, low)


def sop_loss(cls_rows, params, labels, denom, length):
    logits = jnp.dot(cls_rows, params[length + 8 : length + 10].T, precision=highest)
    chosen = jnp.take_along_axis(logits, labels[:, None], axis=1)[:, 0]
    return jnp.sum(jax.nn.logsumexp(logits, axis=-1) - chosen) / denom


def adam(weight, first, second, grad, count):
    first_new = beta_one * first + (1.0 - beta_one) * grad
    second_new = beta_two * second + (1.0 - beta_two) * grad * grad
    corr_one = 1.0 - jnp.power(beta_one, count)
    corr_two = 1.0 - jnp.power(beta_two, count)
    step = first_new / corr_one / (jnp.sqrt(second_new / corr_two) + adam_eps)
    return (weight - learn_rate * (step + weight_decay * weight), first_new, second_new)


def everyone(x, axes):
    count = lax.axis_size(axes)
    return lax.all_to_all(jnp.broadcast_to(x, (count,) + x.shape), axes, 0, 0, tiled=True)


def swap(x, axis, bit):
    count = lax.axis_size(axis)
    return lax.ppermute(x, axis, [(i, i ^ (1 << bit)) for i in range(count)])


def bits_of(axis):
    return lax.axis_size(axis).bit_length() - 1


def fold(x, axis, bit, dim):
    me = (lax.axis_index(axis) >> bit) & 1
    sent = lax.dynamic_index_in_dim(x, 1 - me, dim, False)
    kept = lax.dynamic_index_in_dim(x, me, dim, False)
    return kept + swap(sent, axis, bit)


def grow(x, axis):
    for bit in range(bits_of(axis)):
        x = jnp.concatenate([x, swap(x, axis, bit)], axis=0)
    return x


def shrink(x, axis):
    for bit in reversed(range(bits_of(axis))):
        half = x.shape[0] // 2
        x = x[:half] + swap(x[half:], axis, bit)
    return x


def relative(x, index):
    for bit in range(x.shape[0].bit_length() - 1):
        y = x.reshape((x.shape[0] >> (bit + 1), 2, 1 << bit) + x.shape[1:])
        x = jnp.where((index >> bit) & 1 == 1, y[:, ::-1], y).reshape(x.shape)
    return x


def rows_norm(x):
    center = jnp.mean(x, axis=-1, keepdims=True)
    shifted = x - center
    inv = lax.rsqrt(jnp.mean(shifted * shifted, axis=-1, keepdims=True) + norm_eps)
    return shifted * inv, inv


def erf(x):
    x = jnp.clip(x, -3.832506856900711, 3.832506856900711)
    y = x * x
    top = jnp.float32(0.00022905065861350646)
    for c in (0.0034082910107109506, 0.050955695062380861, 0.18520832239976145, 1.128379143519084):
        top = top * y + c
    low = jnp.float32(-1.1791602954361697e-7)
    for c in (
        0.000023547966471313185,
        0.0010179625278914885,
        0.014070470171167667,
        0.11098505178285362,
        0.49746925110067538,
        1.0,
    ):
        low = low * y + c
    return x * top / low


def head_mask(rows, groups):
    row = lax.broadcasted_iota(i32, (rows, groups * DH), 0)
    col = lax.broadcasted_iota(i32, (rows, groups * DH), 1)
    return lax.rem(row, groups) == lax.div(col, DH)


def split3(x):
    a = x.astype(bf16)
    r = x - a.astype(f32)
    b = r.astype(bf16)
    c = (r - b.astype(f32)).astype(bf16)
    return a, b, c


def dot_exact(a, b, dims):
    return lax.dot_general(a, b, (dims, ((), ())), precision=highest, preferred_element_type=f32)


def conv_kernel_rows(prod, taps_ref, groups):
    width = taps_ref.shape[0]
    spread = jnp.concatenate(
        [jnp.broadcast_to(taps_ref[o : o + 1, :], (groups, prod.shape[1])) for o in range(width)], axis=0
    )
    spread = jnp.where(head_mask(width * groups, groups), spread, 0.0)
    logits = dot_exact(spread, prod, ((1,), (1,)))
    parts = [logits[o * groups : (o + 1) * groups] for o in range(width)]
    top = parts[0]
    for p in parts[1:]:
        top = jnp.maximum(top, p)
    weights = [jnp.exp(p - top) for p in parts]
    total = weights[0]
    for w in weights[1:]:
        total = total + w
    inv = 1.0 / total
    return [w * inv for w in weights], spread


def spread_rows(rows, groups):
    three = jnp.concatenate(split3(rows), axis=0)
    ones = head_mask(3 * groups, groups).astype(bf16)
    return lax.dot_general(three, ones, (((0,), (0,)), ((), ())), preferred_element_type=f32)


def forward_heads(
    split_ref, length_ref, word_ref, places_ref, edge_ref, taps_ref, units_ref,
    emb_ref, qkv_ref, lse_ref, heads_ref, pad_ref,
):
    at = pl.program_id(0)
    length, width = word_ref.shape[1:]
    later = lax.broadcasted_iota(i32, (length, 1), 0) > split_ref[at]
    summed = word_ref[0].astype(f32) + places_ref[...]
    summed = summed + jnp.where(later, edge_ref[7:8, :], edge_ref[6:7, :])
    normed, _ = rows_norm(summed)
    embedded = normed * edge_ref[0:1, :] + edge_ref[3:4, :]
    emb_ref[0] = embedded
    low_in = embedded.astype(bf16)
    part = units_ref.shape[2]
    for k in range(3):
        unit = units_ref[:, k].reshape(width, width)
        qkv_ref[0, :, k * width : (k + 1) * width] = dot_right(low_in, unit).astype(bf16)
    allowed = lax.broadcasted_iota(i32, (length, length), 1) < length_ref[at]
    lanes = lax.broadcasted_iota(i32, (length, 128), 1)
    lse = jnp.zeros((length, 128), f32)
    outs = {}
    for n, h in enumerate(ATTN):
        q = qkv_ref[0, :, h * DH : (h + 1) * DH]
        k = qkv_ref[0, :, width + h * DH : width + (h + 1) * DH]
        v = qkv_ref[0, :, 2 * width + h * DH : 2 * width + (h + 1) * DH]
        scores = jnp.where(allowed, dot_right(q, k) * (1.0 / math.sqrt(DH)), -1e30)
        top = jnp.max(scores, axis=1, keepdims=True)
        weights = jnp.exp(scores - top)
        total = jnp.sum(weights, axis=1, keepdims=True)
        probs = (weights * (1.0 / total)).astype(bf16)
        outs[h] = dot_plain(probs, v).astype(bf16)
        lse = jnp.where(lanes == n, top + jnp.log(total), lse)
    lse_ref[0] = lse
    groups = HEADS - FIRST
    base = FIRST * DH
    q = qkv_ref[0, :, base:width].astype(f32)
    k = qkv_ref[0, :, width + base : 2 * width].astype(f32)
    kernel, _ = conv_kernel_rows(q * k, taps_ref, groups)
    taps = len(kernel)
    pad_ref[0:8, :] = jnp.zeros((8, width - base), f32)
    pad_ref[8 + length : 16 + length, :] = jnp.zeros((8, width - base), f32)
    pad_ref[8 : 8 + length, :] = qkv_ref[0, :, 2 * width + base :].astype(f32)
    total = jnp.zeros((length, width - base), f32)
    for o in range(taps):
        start = 8 + o - taps // 2
        total = total + spread_rows(kernel[o], groups) * pad_ref[start : start + length, :]
    total = total.astype(bf16)
    for h in CONV:
        outs[h] = total[:, (h - FIRST) * DH : (h - FIRST + 1) * DH]
    heads_ref[0] = jnp.concatenate([outs[h] for h in range(HEADS)], axis=1)


def ffn_weights(units_ref, s, first):
    return jnp.concatenate([units_ref[s, first], units_ref[s, first + 1]], axis=0)


def forward_ffn(
    pos_ref, heads_ref, emb_ref, edge_ref, units_ref, one_ref, two_ref, mask_ref, cls_ref
):
    length, width = emb_ref.shape[1:]
    mp_count, part = units_ref.shape[0], units_ref.shape[2]
    unit = units_ref[:, 0].reshape(width, width)
    projected = dot_right(heads_ref[0], unit).astype(bf16).astype(f32)
    one = emb_ref[0] + projected
    one_ref[0] = one
    normed, _ = rows_norm(one)
    attended = normed * edge_ref[1:2, :] + edge_ref[4:5, :]
    low_mid = attended.astype(bf16)
    for g in range(2):
        cols = slice(2 * part * g, 2 * part * (g + 1))
        total = None
        for s in (2 * g, 2 * g + 1):
            pre = dot_plain(low_mid[:, cols], ffn_weights(units_ref, s, 1))
            hidden = (pre * (0.5 + 0.5 * erf(pre * math.sqrt(0.5)))).astype(bf16)
            out = dot_right(hidden, ffn_weights(units_ref, s, 3))
            total = out if total is None else total + out
        two_ref[0, :, cols] = attended[:, cols] + total
    normed, _ = rows_norm(two_ref[0])
    final = normed * edge_ref[2:3, :] + edge_ref[5:6, :]
    masks = mask_ref.shape[1]
    picked = lax.broadcasted_iota(i32, (masks, length), 1) == pos_ref[0][:, 0:1]
    mask_ref[0] = dot_plain(picked.astype(bf16), final.astype(bf16)).astype(bf16)
    cls_ref[0] = final[0:8]


def norm_grad(grad, normed, inv, gain):
    scaled = grad * gain
    mean = jnp.mean(scaled, axis=-1, keepdims=True)
    along = jnp.mean(scaled * normed, axis=-1, keepdims=True)
    return inv * (scaled - mean - normed * along)


def down(x):
    return jnp.sum(x, axis=0, keepdims=True)


def backward_ffn(
    pos_ref, grad_ref, cls_ref, one_ref, two_ref, heads_ref, edge_ref, units_ref,
    sum_ref, back_ref, wide_ref, edges_ref,
):
    at = pl.program_id(0)
    length, width = one_ref.shape[1:]
    mp_count, part = units_ref.shape[0], units_ref.shape[2]

    @pl.when(at == 0)
    def _():
        wide_ref[...] = jnp.zeros_like(wide_ref)
        edges_ref[...] = jnp.zeros_like(edges_ref)

    masks = grad_ref.shape[1]
    picked = (lax.broadcasted_iota(i32, (masks, length), 1) == pos_ref[0][:, 0:1]).astype(bf16)
    high = grad_ref[0].astype(bf16)
    low = (grad_ref[0] - high.astype(f32)).astype(bf16)
    grad = dot_left(picked, high) + dot_left(picked, low)
    rows = lax.broadcasted_iota(i32, (length, 1), 0)
    grad = grad + jnp.where(rows == 0, cls_ref[0][0:1, :], 0.0)
    normed, inv = rows_norm(two_ref[0])
    edges_ref[2:3, :] += down(grad * normed)
    edges_ref[5:6, :] += down(grad)
    grad_two = norm_grad(grad, normed, inv, edge_ref[2:3, :])
    low_two = grad_two.astype(bf16)
    normed, inv = rows_norm(one_ref[0])
    low_mid = (normed * edge_ref[1:2, :] + edge_ref[4:5, :]).astype(bf16)
    backs = []
    for g in range(2):
        cols = slice(2 * part * g, 2 * part * (g + 1))
        total = None
        for s in (2 * g, 2 * g + 1):
            w_in = ffn_weights(units_ref, s, 1)
            w_out = ffn_weights(units_ref, s, 3)
            pre = dot_plain(low_mid[:, cols], w_in)
            half = 0.5 + 0.5 * erf(pre * math.sqrt(0.5))
            hidden = (pre * half).astype(bf16)
            slope = half + pre * (jnp.exp(-0.5 * pre * pre) * (1.0 / math.sqrt(2.0 * math.pi)))
            grad_hidden = dot_plain(low_two[:, cols], w_out)
            w = dot_left(low_two[:, cols], hidden)
            wide_ref[s, 3] += w[:part]
            wide_ref[s, 4] += w[part:]
            grad_pre = (grad_hidden * slope).astype(bf16)
            w = dot_left(low_mid[:, cols], grad_pre)
            wide_ref[s, 1] += w[:part]
            wide_ref[s, 2] += w[part:]
            back = dot_right(grad_pre, w_in)
            total = back if total is None else total + back
        backs.append(total)
    grad = grad_two + jnp.concatenate(backs, axis=1)
    edges_ref[1:2, :] += down(grad * normed)
    edges_ref[4:5, :] += down(grad)
    grad_one = norm_grad(grad, normed, inv, edge_ref[1:2, :])
    sum_ref[0] = grad_one
    low_one = grad_one.astype(bf16)
    wide_ref[:, 0] += dot_left(low_one, heads_ref[0]).reshape(mp_count, part, width)
    unit = units_ref[:, 0].reshape(width, width)
    back_ref[0] = dot_plain(low_one, unit).astype(bf16)


def backward_heads(
    split_ref, length_ref, word_ref, places_ref, edge_ref, taps_ref, units_ref,
    qkv_ref, lse_ref, back_ref, sum_ref,
    gword_ref, gplaces_ref, gedge_ref, gtaps_ref, wide_ref,
    pad_ref, shift_ref,
):
    at = pl.program_id(0)
    length, width = word_ref.shape[1:]

    @pl.when(at == 0)
    def _():
        wide_ref[...] = jnp.zeros_like(wide_ref)
        gplaces_ref[...] = jnp.zeros_like(gplaces_ref)
        gedge_ref[...] = jnp.zeros_like(gedge_ref)
        gtaps_ref[...] = jnp.zeros_like(gtaps_ref)

    groups = HEADS - FIRST
    base = FIRST * DH
    span = width - base
    q = qkv_ref[0, :, base:width].astype(f32)
    k = qkv_ref[0, :, width + base : 2 * width].astype(f32)
    prod = q * k
    kernel, spread = conv_kernel_rows(prod, taps_ref, groups)
    taps = len(kernel)
    out = back_ref[0, :, base:].astype(f32)
    pad_ref[0:8, :] = jnp.zeros((8, span), f32)
    pad_ref[8 + length : 16 + length, :] = jnp.zeros((8, span), f32)
    pad_ref[8 : 8 + length, :] = qkv_ref[0, :, 2 * width + base :].astype(f32)
    shift_ref[0:8, :] = jnp.zeros((8, span), f32)
    shift_ref[8 + length : 16 + length, :] = jnp.zeros((8, span), f32)
    grad_values = jnp.zeros((length, span), f32)
    lanes = 128
    dots = jnp.zeros((length, lanes), f32)
    column = lax.broadcasted_iota(i32, (span, lanes), 0)
    lane = lax.broadcasted_iota(i32, (span, lanes), 1)
    for o in range(taps):
        start = 8 + o - taps // 2
        moved = out * pad_ref[start : start + length, :]
        high = moved.astype(bf16)
        low = (moved - high.astype(f32)).astype(bf16)
        ones = (lane == o * groups + lax.div(column, DH)).astype(bf16)
        dots = dots + dot_plain(high, ones) + dot_plain(low, ones)
        shift_ref[8 : 8 + length, :] = spread_rows(kernel[o], groups) * out
        back = 8 + taps // 2 - o
        grad_values = grad_values + shift_ref[back : back + length, :]
    dots = dots.T
    parts = [dots[o * groups : (o + 1) * groups] for o in range(taps)]
    along = kernel[0] * parts[0]
    for o in range(1, taps):
        along = along + kernel[o] * parts[o]
    grad_logits = jnp.concatenate([kernel[o] * (parts[o] - along) for o in range(taps)], axis=0)
    grad_prod = dot_exact(grad_logits, spread, ((0,), (0,)))
    grad_taps = dot_exact(grad_logits, prod, ((1,), (0,)))
    grad_taps = jnp.where(head_mask(taps * groups, groups), grad_taps, 0.0)
    for o in range(taps):
        gtaps_ref[o : o + 1, :] += down(grad_taps[o * groups : (o + 1) * groups])
    grads = [(grad_prod * k).astype(bf16), (grad_prod * q).astype(bf16), grad_values.astype(bf16)]
    pieces = [[None] * HEADS for _ in range(3)]
    for h in CONV:
        for n in range(3):
            pieces[n][h] = grads[n][:, (h - FIRST) * DH : (h - FIRST + 1) * DH]

    allowed = lax.broadcasted_iota(i32, (length, length), 1) < length_ref[at]
    scale = 1.0 / math.sqrt(DH)
    for n, h in enumerate(ATTN):
        qh = qkv_ref[0, :, h * DH : (h + 1) * DH]
        kh = qkv_ref[0, :, width + h * DH : width + (h + 1) * DH]
        vh = qkv_ref[0, :, 2 * width + h * DH : 2 * width + (h + 1) * DH]
        gh = back_ref[0, :, h * DH : (h + 1) * DH]
        scores = jnp.where(allowed, dot_right(qh, kh) * scale, -1e30)
        probs = jnp.exp(scores - lse_ref[0][:, n : n + 1])
        grad_probs = dot_right(gh, vh)
        total = jnp.sum(probs * grad_probs, axis=1, keepdims=True)
        grad_scores = (probs * (grad_probs - total)).astype(bf16)
        pieces[0][h] = (dot_plain(grad_scores, kh) * scale).astype(bf16)
        pieces[1][h] = (dot_left(grad_scores, qh) * scale).astype(bf16)
        pieces[2][h] = dot_left(probs.astype(bf16), gh).astype(bf16)
    later = lax.broadcasted_iota(i32, (length, 1), 0) > split_ref[at]
    summed = word_ref[0].astype(f32) + places_ref[...]
    summed = summed + jnp.where(later, edge_ref[7:8, :], edge_ref[6:7, :])
    normed, inv = rows_norm(summed)
    low_in = (normed * edge_ref[0:1, :] + edge_ref[3:4, :]).astype(bf16)
    grad = sum_ref[0]
    for n in range(3):
        g = jnp.concatenate(pieces[n], axis=1)
        wide_ref[:, n] += dot_left(g, low_in).reshape(units_ref.shape[0], -1, width)
        grad = grad + dot_plain(g, units_ref[:, n].reshape(width, width))
    gedge_ref[0:1, :] += down(grad * normed)
    gedge_ref[3:4, :] += down(grad)
    grad = norm_grad(grad, normed, inv, edge_ref[0:1, :])
    gword_ref[0] = grad
    gplaces_ref[...] += grad
    second = down(jnp.where(later, grad, 0.0))
    gedge_ref[6:7, :] += down(grad) - second
    gedge_ref[7:8, :] += second


def whole(shape):
    return pl.BlockSpec(shape, lambda b, *_: (0,) * len(shape))


def fixed(shape):
    return pl.BlockSpec(shape, lambda b, *_: (0,) * len(shape), pipeline_mode=pl.Buffered(1))


def each(shape):
    return pl.BlockSpec((1,) + shape, lambda b, *_: (b,) + (0,) * len(shape))


def run(kernel, scalars, ins, outs, scratch, flops, name):
    arrays = [x for x, _ in ins]
    seqs = next(x.shape[0] for x, spec in ins if spec.block_shape[0] == 1 and x.ndim == 3)
    shapes = [jax.ShapeDtypeStruct(shape, dtype) for (shape, dtype), _ in outs]
    moved = sum(math.prod(x.shape) * x.dtype.itemsize for x in arrays + shapes)
    return pl.pallas_call(
        kernel,
        out_shape=shapes,
        grid_spec=pltpu.PrefetchScalarGridSpec(
            num_scalar_prefetch=len(scalars),
            grid=(seqs,),
            in_specs=[spec for _, spec in ins],
            out_specs=[spec for _, spec in outs],
            scratch_shapes=scratch,
        ),
        compiler_params=pltpu.CompilerParams(
            dimension_semantics=("arbitrary",), vmem_limit_bytes=VMEM
        ),
        cost_estimate=pl.CostEstimate(flops=flops, bytes_accessed=moved, transcendentals=0),
        name=name,
    )(*scalars, *arrays)


def slots_of(ids, vblock, devices):
    owner = ids // vblock
    here = jnp.arange(ids.shape[0])
    same = ids[None, :] == ids[:, None]
    first = jnp.sum(jnp.logical_and(same, here[None, :] < here[:, None]), axis=1) == 0
    below = jnp.logical_and(owner[None, :] == owner[:, None], ids[None, :] < ids[:, None])
    rank = jnp.sum(jnp.logical_and(below, first[None, :]), axis=1).astype(i32)
    return owner, first, rank


def fetch_round(turn, capacity, devices, owner, first, rank, local, low_table):
    slot = jnp.where(rank // capacity == turn, owner * capacity + rank % capacity, -1)
    seats = jnp.arange(devices * capacity)
    chosen = jnp.logical_and(seats[:, None] == slot[None, :], first[None, :])
    request = jnp.sum(jnp.where(chosen, local[None, :] + 1, 0), axis=1) - 1
    message = jnp.full((devices, 128), jnp.max(rank), i32)
    message = message.at[:, :capacity].set(request.reshape(devices, capacity))
    got = lax.all_to_all(message, ALL, 0, 0, tiled=True)
    asked = got[:, :capacity].reshape(-1)
    served = (asked[:, None] == jnp.arange(low_table.shape[0])[None, :]).astype(bf16)
    rows = dot_plain(served, low_table).astype(bf16)
    rows = lax.all_to_all(rows, ALL, 0, 0, tiled=True)
    mine = (slot[:, None] == seats[None, :]).astype(bf16)
    return dot_plain(mine, rows).astype(bf16), mine, served, jnp.max(got[:, capacity])


def return_round(mine, served, grad_word):
    sent = select_sum(mine, grad_word)
    got = lax.all_to_all(sent, ALL, 0, 0, tiled=True)
    return select_sum(served, got)


def body(
    token_ids,
    seg_split,
    lengths,
    mlm_pos,
    mlm_labels,
    sop_labels,
    owner,
    step_count,
    table,
    table_m,
    table_v,
    unit_master,
    unit_m,
    unit_v,
    small,
    small_m,
    small_v,
    taps,
    taps_m,
    taps_v,
):
    mp_count = lax.axis_size(MP)
    dp_count = lax.axis_size(DP)
    devices = mp_count * dp_count
    mp_index = lax.axis_index(MP)
    dp_index = lax.axis_index(DP)
    group_seqs, length = token_ids.shape
    width = small.shape[1]
    part = unit_master.shape[1]
    vblock = table.shape[0]
    cap_slots = unit_master.shape[0]
    matrices = owner.shape[0]
    seqs = group_seqs // mp_count
    tokens = seqs * length
    masks = mlm_pos.shape[1]
    total_seqs = group_seqs * dp_count
    count_all = total_seqs * masks

    def my(x):
        return lax.dynamic_slice_in_dim(x, mp_index * seqs, seqs, 0)

    token_ids, seg_split, lengths = my(token_ids), my(seg_split), my(lengths)
    mlm_pos, mlm_labels, sop_labels = my(mlm_pos), my(mlm_labels), my(sop_labels)

    earlier = jnp.arange(matrices)[:, None] > jnp.arange(matrices)[None, :]
    slot_rank = jnp.sum(jnp.logical_and(earlier, owner[:, None] == owner[None, :]), axis=1)
    slot_index = owner * cap_slots + slot_rank
    selector = jnp.logical_and(
        owner[None, :] == dp_index, slot_rank[None, :] == jnp.arange(cap_slots)[:, None]
    ).astype(f32)
    rest = part // dp_count
    low_slots = unit_master.astype(bf16).reshape(cap_slots, dp_count, rest, width)
    got_slots = lax.all_to_all(jnp.moveaxis(low_slots, 1, 0), DP, 0, 0, tiled=True)
    got_slots = got_slots.reshape(dp_count * cap_slots, rest, width)
    picked = jnp.stack(
        [lax.dynamic_index_in_dim(got_slots, slot_index[k], 0, False) for k in range(matrices)]
    )
    shards = jnp.moveaxis(lax.all_gather(picked, DP, axis=0), 0, 1)
    shards = shards.reshape(matrices, part, width)
    first_units = lax.all_gather(shards[:3], MP, axis=0)
    last_units = lax.all_gather(shards[3:], MP, axis=0)
    low_table = table.astype(bf16)
    vocab = lax.all_gather(low_table, RG, axis=0, tiled=True)

    ids = token_ids.reshape(-1)
    capacity = max(8, -(-1280 // devices))
    home, first, rank = slots_of(ids, vblock, devices)
    local = ids % vblock
    fetch = partial(
        fetch_round,
        capacity=capacity,
        devices=devices,
        owner=home,
        first=first,
        rank=rank,
        local=local,
        low_table=low_table,
    )
    word_rows, mine, served, top_rank = fetch(0)
    turns = top_rank // capacity + 1

    def more(state):
        return state[0] < turns

    def fetch_more(state):
        return (state[0] + 1, state[1] + fetch(state[0])[0])

    _, word_rows = lax.while_loop(more, fetch_more, (jnp.int32(1), word_rows))

    words_in = word_rows.reshape(seqs, length, width)
    places = small[6 : 6 + length]
    edge = jnp.concatenate([small[:6], small[6 + length : 8 + length]])
    span = (HEADS - FIRST) * DH
    taps_span = [
        taps[:, CONV.index(h) * DH : (CONV.index(h) + 1) * DH]
        if h in CONV
        else jnp.zeros((taps.shape[0], DH), f32)
        for h in range(FIRST, HEADS)
    ]
    taps_span = jnp.concatenate(taps_span, axis=1)
    act = (length, width)
    flop = 2 * tokens * width * width
    embedded, qkv, lse, heads = run(
        forward_heads,
        (seg_split, lengths),
        [
            (words_in, each(act)),
            (places, fixed(places.shape)),
            (edge, fixed(edge.shape)),
            (taps_span, fixed(taps_span.shape)),
            (first_units, fixed(first_units.shape)),
        ],
        [
            (((seqs,) + act, f32), each(act)),
            (((seqs, length, 3 * width), bf16), each((length, 3 * width))),
            (((seqs, length, 128), f32), each((length, 128))),
            (((seqs,) + act, bf16), each(act)),
        ],
        [pltpu.VMEM((length + 16, span), f32)],
        8 * flop,
        "forward_heads",
    )
    spots = mlm_pos[:, :, None]
    one, two, masked_rows, cls_rows = run(
        forward_ffn,
        (),
        [
            (spots, each((masks, 1))),
            (heads, each(act)),
            (embedded, each(act)),
            (edge, fixed(edge.shape)),
            (last_units, fixed(last_units.shape)),
        ],
        [
            (((seqs,) + act, f32), each(act)),
            (((seqs,) + act, f32), each(act)),
            (((seqs, masks, width), bf16), each((masks, width))),
            (((seqs, 8, width), f32), each((8, width))),
        ],
        [],
        8 * flop,
        "forward_ffn",
    )
    masked_rows = masked_rows.reshape(seqs * masks, width)

    all_masked = grow(grow(masked_rows, "dh"), "mh")
    all_labels = grow(grow(mlm_labels.reshape(-1), "dh"), "mh")
    logits = dot_right(all_masked, vocab)
    group_count = lax.axis_size(VG)
    block = all_labels // vblock
    block_ml = block % lax.axis_size("ml")
    block_mh = block // lax.axis_size("ml") % lax.axis_size("mh")
    block_dl = block // mp_count % lax.axis_size("dl")
    block_dh = block // (mp_count * lax.axis_size("dl"))
    label_mine = jnp.logical_and(
        block_dh == lax.axis_index("dh"), block_mh == lax.axis_index("mh")
    )
    label_row = (block_dl * lax.axis_size("ml") + block_ml) * vblock + all_labels % vblock
    onehot = jnp.logical_and(
        jnp.arange(vocab.shape[0])[None, :] == label_row[:, None], label_mine[:, None]
    )
    top = jnp.max(logits, axis=1)
    total = jnp.sum(jnp.exp(logits - top[:, None]), axis=1)
    target = jnp.sum(jnp.where(onehot, logits, 0.0), axis=1)
    order = lax.axis_index("mh") * lax.axis_size("dh") + lax.axis_index("dh")
    stats = jnp.stack([top, total, target]).reshape(3, group_count, -1)
    stats = relative(jnp.moveaxis(stats, 1, 0), order)
    stats = stats.reshape(lax.axis_size("mh"), lax.axis_size("dh"), 3, -1)
    stats = jnp.moveaxis(stats, 0, 1).reshape(group_count, 3, -1)
    stats = everyone(stats, VG)
    top_all = jnp.max(stats[:, :, 0], axis=0)
    total_all = jnp.sum(stats[:, :, 1] * jnp.exp(stats[:, :, 0] - top_all), axis=0)
    log_all = top_all + jnp.log(total_all)
    log_sum = log_all.reshape(lax.axis_size("dh"), lax.axis_size("mh"), -1)
    log_sum = jnp.moveaxis(log_sum, 0, 1).reshape(group_count, -1)
    log_sum = relative(log_sum, order).reshape(-1)
    target_all = jnp.sum(stats[:, :, 2], axis=0)
    mlm_part = jnp.sum(log_all - target_all) / count_all / group_count
    grad_logits = (
        (jnp.exp(logits - log_sum[:, None]) - onehot.astype(f32)) / count_all
    ).astype(bf16)
    grad_masked = shrink(shrink(dot_plain(grad_logits, vocab), "mh"), "dh")
    grad_table = dot_left(grad_logits, all_masked).reshape(2, 2, vblock, width)
    grad_table = fold(fold(grad_table, "ml", 0, 1), "dl", 0, 0)
    sop_part, sop_pull = jax.vjp(
        partial(sop_loss, labels=sop_labels, denom=total_seqs, length=length), cls_rows[:, 0], small
    )
    grad_cls, grad_small_sop = sop_pull(jnp.ones((), f32))
    grad_cls = jnp.pad(grad_cls[:, None], ((0, 0), (0, 7), (0, 0)))
    sum_one, grad_heads, wide_last, edge_last = run(
        backward_ffn,
        (),
        [
            (spots, each((masks, 1))),
            (grad_masked.reshape(seqs, masks, width), each((masks, width))),
            (grad_cls, each((8, width))),
            (one, each(act)),
            (two, each(act)),
            (heads, each(act)),
            (edge, fixed(edge.shape)),
            (last_units, fixed(last_units.shape)),
        ],
        [
            (((seqs,) + act, f32), each(act)),
            (((seqs,) + act, bf16), each(act)),
            ((last_units.shape, f32), fixed(last_units.shape)),
            ((edge.shape, f32), fixed(edge.shape)),
        ],
        [],
        16 * flop,
        "backward_ffn",
    )
    grad_word, grad_places, edge_first, grad_taps, wide_first = run(
        backward_heads,
        (seg_split, lengths),
        [
            (words_in, each(act)),
            (places, fixed(places.shape)),
            (edge, fixed(edge.shape)),
            (taps_span, fixed(taps_span.shape)),
            (first_units, fixed(first_units.shape)),
            (qkv, each((length, 3 * width))),
            (lse, each((length, 128))),
            (grad_heads, each(act)),
            (sum_one, each(act)),
        ],
        [
            (((seqs,) + act, f32), each(act)),
            ((act, f32), fixed(act)),
            ((edge.shape, f32), fixed(edge.shape)),
            ((taps_span.shape, f32), fixed(taps_span.shape)),
            ((first_units.shape, f32), fixed(first_units.shape)),
        ],
        [pltpu.VMEM((length + 16, span), f32)] * 2,
        20 * flop,
        "backward_heads",
    )
    grad_taps = jnp.concatenate(
        [grad_taps[:, (h - FIRST) * DH : (h - FIRST + 1) * DH] for h in CONV], axis=1
    )
    grad_word = grad_word.reshape(tokens, width)

    words = return_round(mine, served, grad_word)

    def return_more(state):
        _, mine_r, served_r, _ = fetch(state[0])
        return (state[0] + 1, state[1] + return_round(mine_r, served_r, grad_word))

    _, words = lax.while_loop(more, return_more, (jnp.int32(1), words))
    grad_table_own = grad_table + words

    def reduce_units(x, axes):
        many = x.shape[1]
        x = x.reshape(2, 2, many, dp_count, rest, width)
        dims = {"mh": 0, "ml": 1}
        for axis in axes:
            if axis in dims:
                x = fold(x, axis, 0, dims.pop(axis))
                dims = {name: 0 for name in dims}
            else:
                where = x.ndim - 3
                lead = x.shape[:where]
                if axis == "dl":
                    x = x.reshape(lead + (x.shape[where] // 2, 2) + x.shape[-2:])
                    x = fold(x, "dl", 0, where + 1)
                else:
                    for bit in reversed(range(bits_of("dh"))):
                        x = x.reshape(lead + (2, x.shape[where] // 2) + x.shape[-2:])
                        x = fold(x, "dh", bit, where)
        return x.reshape(many, rest, width)

    pieces_last = lax.psum_scatter(
        wide_last.reshape(-1, width), MP, scatter_dimension=0, tiled=True
    )
    pieces_last = jnp.moveaxis(pieces_last.reshape(-1, dp_count, rest, width), 1, 0)
    pieces_last = lax.psum_scatter(
        pieces_last.reshape(-1, width), DP, scatter_dimension=0, tiled=True
    ).reshape(-1, rest, width)
    pieces_first = reduce_units(wide_first, ("ml", "dl", "mh", "dh"))
    summed = jnp.concatenate([pieces_first, pieces_last])
    seat = (slot_index[None, :] == jnp.arange(dp_count * cap_slots)[:, None]).astype(f32)
    slotted = sum(seat[:, k, None, None] * summed[k][None] for k in range(matrices))
    slotted = slotted.reshape(dp_count, cap_slots, rest, width)
    grad_slots = lax.all_to_all(slotted, DP, 0, 0, tiled=True)
    grad_slots = jnp.moveaxis(grad_slots, 0, 1).reshape(cap_slots, part, width)

    edge_sum = edge_first + edge_last
    same = devices // 2
    half = fold(grad_places.reshape(2, length // 2, width), "ml", 0, 0)
    piece = -(-(length // 2) // same)
    half = jnp.pad(half, ((0, piece * same - length // 2), (0, 0)))
    got = lax.all_to_all(half.reshape(same, piece, width), CHIPS, 0, 0, tiled=True)
    places_own = jnp.sum(got, axis=0)
    places_half = everyone(places_own, CHIPS).reshape(same * piece, width)[: length // 2]
    other = swap(places_half, "ml", 0)
    low_first = lax.axis_index("ml") == 0
    places_sum = jnp.concatenate(
        [jnp.where(low_first, places_half, other), jnp.where(low_first, other, places_half)]
    )
    misc = jnp.concatenate(
        [
            edge_sum.reshape(-1),
            grad_small_sop[8 + length :].reshape(-1),
            grad_taps.reshape(-1),
            jnp.reshape(mlm_part + sop_part, (1,)),
        ]
    )
    size = misc.shape[0]
    lane = -(-size // (devices * 128)) * 128
    misc = jnp.pad(misc, (0, devices * lane - size)).reshape(devices, lane)
    misc_own = jnp.sum(lax.all_to_all(misc, ALL, 0, 0, tiled=True), axis=0)
    misc = everyone(misc_own, ALL).reshape(-1)
    ends = (small.shape[0] - length) * width
    ends_sum = misc[:ends].reshape(-1, width)
    small_sum = jnp.concatenate([ends_sum[:6], places_sum, ends_sum[6:]])
    taps_sum = misc[ends : size - 1].reshape(taps.shape)
    loss = misc[size - 1]
    square = (
        jnp.sum(grad_table_own * grad_table_own)
        + jnp.sum(grad_slots * grad_slots)
        + jnp.sum(places_own * places_own)
        + (jnp.sum(ends_sum * ends_sum) + jnp.sum(taps_sum * taps_sum)) / devices
    )
    squares = everyone(jnp.full((128,), square, f32), ALL)
    grad_norm = jnp.sqrt(jnp.sum(squares[:, 0]))
    scale = clip_bound / jnp.maximum(grad_norm, clip_bound)
    count = step_count[0].astype(f32)
    table_new, table_m_new, table_v_new = adam(
        table, table_m, table_v, grad_table_own * scale, count
    )
    used = jnp.sum(selector, axis=1)[:, None, None]
    unit_new, unit_m_new, unit_v_new = adam(unit_master, unit_m, unit_v, grad_slots * scale, count)
    unit_new = unit_new * used
    unit_m_new = unit_m_new * used
    unit_v_new = unit_v_new * used
    small_new, small_m_new, small_v_new = adam(small, small_m, small_v, small_sum * scale, count)
    taps_new, taps_m_new, taps_v_new = adam(taps, taps_m, taps_v, taps_sum * scale, count)
    return (
        loss,
        grad_norm,
        table_new,
        table_m_new,
        table_v_new,
        table_new.astype(bf16),
        unit_new,
        unit_m_new,
        unit_v_new,
        unit_new.astype(bf16),
        small_new,
        small_m_new,
        small_v_new,
        taps_new,
        taps_m_new,
        taps_v_new,
    )


def solution(mesh):
    dp, mp = mesh.devices.shape
    fine = Mesh(mesh.devices.reshape(dp // 2, 2, mp // 2, 2), ALL)
    rows = P(DP)
    vocab = P(ALL)
    slots = P(DP, MP)
    placed = (rows,) * 6 + (P(),) * 2 + (vocab,) * 3 + (slots,) * 3 + (P(),) * 6
    return jax.shard_map(
        body,
        mesh=fine,
        in_specs=placed,
        out_specs=(P(),) * 2 + (vocab,) * 4 + (slots,) * 4 + (P(),) * 6,
        check_vma=False,
    )
```

time: 1480 us -> 919 us (0.62)
  local copies, waits for them, and re-layouts: 271 us -> 46.2 us
  waiting for transfers between devices: 624 us -> 456 us
  matrix products: 214 us -> 64.6 us
  Pallas kernels: 0 us -> 136 us
  blocking collectives: 124 us -> 12.5 us
  other arithmetic: 173 us -> 94.5 us
  starting transfers between devices: 18.8 us -> 54.2 us
    reduce_scatter x4 -> x2, waiting for transfers between devices: 492 us -> 0.02 us  [the longest x1 0.02 us: body(): lax.psum_scatter(pieces_last.reshape(-1, width), DP, scatter_dimension=0,...]
    ppermute x0 -> x18, waiting for transfers between devices: none -> 256 us  [swap(): return lax.ppermute(x, axis, [(i, i ^ 1 << bit) for i in range(count)])]
    unnamed x624 -> x130, local copies, waits for them, and re-layouts: 175 us -> 9.7 us
    pallas_call x0 -> x4, Pallas kernels: none -> 136 us  [run(): pl.pallas_call(kernel, out_shape=shapes, grid_spec=pltpu.PrefetchScalarGr...]
    psum x1 -> x0, blocking collectives: 116 us -> none  [body(): lax.psum((grad_small, grad_taps, mlm_part + sop_part), ALL)]
    dot_general x16 -> x3, matrix products: 82.9 us -> 18.3 us  [dot_plain(): lax.dot_general(left, right, (((1,), (0,)), ((), ())), preferred_element_...]
    all_to_all x2 -> x3, waiting for transfers between devices: 10.9 us -> 70 us  [everyone(): lax.all_to_all(jnp.broadcast_to(x, (count,) + x.shape), axes, 0, 0, tiled...]
    dot_general x8 -> x0, matrix products: 34.1 us -> none  [the longest x1 11.9 us: body(): jnp.einsum('bqhd,bkhd->bhqk', ga, va, preferred_element_type=f32)]
  transfers between devices with their start and end apart: 14 -> 34, of which waited for: 10 -> 20; matrix products, arithmetic and copies ran while one was open for 22% -> 14% of each run, Pallas kernels for 0% -> 10%
where the time goes in v2:
time: 919 us; the launch traced here: 910 us
  waiting for transfers between devices  456 us (50%)
  Pallas kernels  136 us (15%)
  other arithmetic  94.5 us (10%)
  matrix products  64.6 us (7%)
  starting transfers between devices  54.2 us (6%)
  local copies, waits for them, and re-layouts  46.2 us (5%)
  between operations  40.3 us (4%)
  blocking collectives  12.5 us (1%)
    ppermute x18, waiting for transfers between devices, swap(): return lax.ppermute(x, axis, [(i, i ^ 1 << bit) for i in range(count)])  256 us
    pallas_call x4, Pallas kernels, run(): pl.pallas_call(kernel, out_shape=shapes, grid_spec=pltpu.PrefetchScalarGr...  136 us
    all_to_all x3, waiting for transfers between devices, everyone(): lax.all_to_all(jnp.broadcast_to(x, (count,) + x.shape), axes, 0, 0, tiled...  70 us
    all_gather x1, waiting for transfers between devices, body(): shards = jnp.moveaxis(lax.all_gather(picked, DP, axis=0), 0, 1)  53.6 us
    all_to_all x1, waiting for transfers between devices, fetch_round(): rows = lax.all_to_all(rows, ALL, 0, 0, tiled=True)  37.3 us
    dot_general x5, matrix products, dot_left(): lax.dot_general(left, right, (((0,), (0,)), ((), ())), preferred_element_...  27.8 us
  transfers between devices with their start and end apart: 34, of which 20 were waited for; matrix products, arithmetic and copies ran while one was open for 14% of the time, Pallas kernels for 10%

profile of v2, /device:TPU:0, one launch (start us, length us, event | category | flops | bytes accessed | tf_op | source)
XLA Modules:
  0.0 910.3 jit_solution(16157542462574046650)
XLA Ops:
  9.4 7.3 all-to-all-start.6
  34.5 53.6 %all-gather.12.cloned.1.call-done = bf16[64,24,768]{2,1,0:T(8,128)(2,1)} async-done(((bf16[8,24,768]{2,1,0:T(8,128)(2,1)}), bf16[64,24,768]{2,1,0:T(8,128)(2,1)}) %all-gather.12.cloned.1.call-update) | async-done | bytes 2359312 | tf_op jit(solution)/shard_map/all_gather | solution.py:565
  103.2 5.8 all-to-all-done.4
  126.5 37.3 %all-to-all-done.5 = bf16[32,40,768]{2,1,0:T(8,128)(2,1)} async-done(((bf16[32,40,768]{2,1,0:T(8,128)(2,1)}), bf16[32,40,768]{2,1,0:T(8,128)(2,1)}, u32[]{:S(2)}, u32[]{:S(2)}) %all-to-all-start.5) | async-done | bytes 1966112 | tf_op jit(solution)/shard_map/all_to_all | solution.py:496
  163.8 5.2 fusion.50
  169.0 5.9 while.30
  175.0 20.5 %forward_heads.1 = (f32[2,512,768]{2,1,0:T(8,128)}, bf16[2,512,2304]{2,1,0:T(8,128)(2,1)}, f32[2,512,128]{2,1,0:T(8,128)}, bf16[2,512,768]{2,1,0:T(8,128)(2,1)}) custom-call(s32[2]{0:T(128)} %dynamic_slice.95.split_ref, s32[2]{0:T(128)} %dynamic_slice.96.length_ref, bf16[2,512,768]{2,1,0:T(8,128)(2,1)} %bitcast.288, f32[512,768]{1,0:T(8,128)} %slice.264.places_ref, ...), custom_call_target="tpu_custom_call" | custom-call | flops 9663676416 | bytes 16689152 | tf_op jit(solution)/shard_map/forward_heads/pallas_call | solution.py:457
  195.6 22.9 %forward_ffn.1 = (f32[2,512,768]{2,1,0:T(8,128)}, f32[2,512,768]{2,1,0:T(8,128)}, bf16[2,80,768]{2,1,0:T(8,128)(2,1)}, f32[2,8,768]{2,1,0:T(8,128)}) custom-call(s32[2,80,1]{2,1,0:T(8,128)} %copy.161.pos_ref, bf16[2,512,768]{2,1,0:T(8,128)(2,1)} %get-tuple-element.438.heads_ref, f32[2,512,768]{2,1,0:T(8,128)} %get-tuple-element.439.emb_ref, ...), custom_call_target="tpu_custom_call" | custom-call | flops 9663676416 | bytes 17228416 | tf_op jit(solution)/shard_map/forward_ffn/pallas_call | solution.py:457
  218.6 7.7 collective-permute-done
  228.4 22.3 %collective-permute-done.1 = bf16[320,768]{1,0:T(8,128)(2,1)S(1)} collective-permute-done((bf16[320,768]{1,0:T(8,128)(2,1)S(1)}, bf16[320,768]{1,0:T(8,128)(2,1)S(1)}, u32[]{:S(2)}, u32[]{:S(2)}) %collective-permute-start.1) | collective-permute-done | bytes 491552 | tf_op jit(solution)/shard_map/ppermute | solution.py:84
  263.0 11.5 %collective-permute-done.5 = s32[640]{0:T(1024)S(1)} collective-permute-done((s32[640]{0:T(1024)S(1)}, s32[640]{0:T(1024)S(1)}, u32[]{:S(2)}, u32[]{:S(2)}) %collective-permute-start.5) | collective-permute-done | bytes 2592 | tf_op jit(solution)/shard_map/ppermute | solution.py:84
  274.7 16.5 %fusion.116 = (f32[1280]{0:T(1024)S(1)}, f32[1280,3840]{1,0:T(8,128)}) fusion(bf16[3840,768]{1,0:T(8,128)(2,1)} %all-gather.10.cloned.1.call-done, bf16[640,768]{1,0:T(8,128)(2,1)S(1)} %collective-permute-done.2, bf16[320,768]{1,0:T(8,128)(2,1)S(1)} %collective-permute-done.1, bf16[160,768]{1,0:T(8,128)(2,1)S(1)} %collective-permute-done, ...), kind=kOutput, calls=%fused_computation.299 | convolution fusion | flops 7562525696 | bytes 27530240 | tf_op jit(solution)/shard_map/dot_general | solution.py:41
  291.3 10.7 %exponential_reduce_fusion = (f32[1280]{0:T(1024)S(1)}, f32[1280]{0:T(1024)S(1)}) fusion(f32[1280,3840]{1,0:T(8,128)} %get-tuple-element.565, f32[1280]{0:T(1024)S(1)} %get-tuple-element.564, pred[1280]{0:T(1024)(128)(4,1)S(1)} %fusion.74, s32[1280]{0:T(1024)S(1)} %fusion.68), kind=kLoop, calls=%fused_computation.64 | loop fusion | flops 29488640 | bytes 19682560 | tf_op jit(solution)/shard_map/reduce_sum | solution.py:670
  302.6 12.5 %all_to_all.166 = f32[8,8,3,160]{3,1,2,0:T(8,128)S(1)} all-to-all(f32[8,8,3,160]{3,1,2,0:T(8,128)S(1)} %broadcast_in_dim.140), channel_id=1, replica_groups=mesh['dh'=4,'dl'=2,'mh'=2,'ml'=2] {'dh','mh'}, dimensions={0} | all-to-all | bytes 245760 | tf_op jit(solution)/shard_map/all_to_all | solution.py:79
  316.1 11.9 %multiply_convert_fusion = bf16[1280,3840]{1,0:T(8,128)(2,1)S(1)} fusion(f32[1280,3840]{1,0:T(8,128)} %get-tuple-element.565, f32[1280]{0:T(1024)S(1)} %sub.175, s32[1280]{0:T(1024)S(1)} %fusion.68, pred[1280]{0:T(1024)(128)(4,1)S(1)} %fusion.74), kind=kLoop, calls=%fused_computation.61 | loop fusion | flops 34406400 | bytes 29502720 | tf_op jit(solution)/shard_map/convert_element_type | solution.py:688
  328.0 8.0 fusion.118
  337.1 41.6 %collective-permute-done.6 = f32[640,768]{1,0:T(8,128)S(1)} collective-permute-done((f32[640,768]{1,0:T(8,128)S(1)}, f32[640,768]{1,0:T(8,128)S(1)}, u32[]{:S(2)}, u32[]{:S(2)}) %collective-permute-start.6) | collective-permute-done | bytes 1966112 | tf_op jit(solution)/shard_map/ppermute | solution.py:84
  381.8 39.1 %collective-permute-done.7 = f32[320,768]{1,0:T(8,128)} collective-permute-done((f32[320,768]{1,0:T(8,128)S(1)}, f32[320,768]{1,0:T(8,128)}, u32[]{:S(2)}, u32[]{:S(2)}) %collective-permute-start.7) | collective-permute-done | bytes 983072 | tf_op jit(solution)/shard_map/ppermute | solution.py:84
  425.3 10.2 %collective-permute-done.8 = f32[160,768]{1,0:T(8,128)S(1)} collective-permute-done((f32[160,768]{1,0:T(8,128)S(1)}, f32[160,768]{1,0:T(8,128)S(1)}, u32[]{:S(2)}, u32[]{:S(2)}) %collective-permute-start.8) | collective-permute-done | bytes 491552 | tf_op jit(solution)/shard_map/ppermute | solution.py:84
  436.3 43.1 %backward_ffn.1 = (f32[2,512,768]{2,1,0:T(8,128)}, bf16[2,512,768]{2,1,0:T(8,128)(2,1)}, f32[4,5,192,768]{3,2,1,0:T(8,128)}, f32[8,768]{1,0:T(8,128)}) custom-call(s32[2,80,1]{2,1,0:T(8,128)} %copy.161.pos_ref, f32[2,80,768]{2,1,0:T(8,128)} %bitcast.266, f32[2,8,768]{2,1,0:T(8,128)} %pad.25.cls_ref, f32[2,512,768]{2,1,0:T(8,128)} %get-tuple-element.442.one_ref, ...), custom_call_target="tpu_custom_call" | custom-call | flops 19327352832 | bytes 30868096 | tf_op jit(solution)/shard_map/backward_ffn/pallas_call | solution.py:457
  480.8 49.7 %backward_heads.1 = (f32[2,512,768]{2,1,0:T(8,128)}, f32[512,768]{1,0:T(8,128)}, f32[8,768]{1,0:T(8,128)}, f32[9,512]{1,0:T(8,128)}, f32[4,3,192,768]{3,2,1,0:T(8,128)}) custom-call(s32[2]{0:T(128)} %dynamic_slice.95.split_ref, s32[2]{0:T(128)} %dynamic_slice.96.length_ref, bf16[2,512,768]{2,1,0:T(8,128)(2,1)S(1)} %bitcast.289, ...), custom_call_target="tpu_custom_call" | custom-call | flops 24159191040 | bytes 28528640 | tf_op jit(solution)/shard_map/backward_heads/pallas_call | solution.py:457
  567.4 9.7 %all-to-all-done.12 = f32[16,16,768]{2,1,0:T(8,128)} async-done(((f32[16,16,768]{2,1,0:T(8,128)}), f32[16,16,768]{2,1,0:T(8,128)}, u32[]{:S(2)}, u32[]{:S(2)}) %all-to-all-start.12) | async-done | bytes 786464 | tf_op jit(solution)/shard_map/all_to_all | solution.py:799
  581.2 11.5 %fusion.55 = f32[3840,768]{1,0:T(8,128)S(1)} fusion(bf16[1280,3840]{1,0:T(8,128)(2,1)} %copy-done.6, bf16[640,768]{1,0:T(8,128)(2,1)} %copy-done.53, bf16[320,768]{1,0:T(8,128)(2,1)} %copy-done.35, bf16[160,768]{1,0:T(8,128)(2,1)} %copy-done.28, bf16[160,768]{1,0:T(8,128)(2,1)} %bitcast.264), kind=kOutput, calls=%fused_computation.140 | convolution fusion | flops 7557611520 | bytes 23592960 | tf_op jit(solution)/shard_map/dot_general | solution.py:45
  609.3 61.0 %collective-permute-done.12 = f32[2,3,4,24,768]{4,3,2,1,0:T(8,128)} collective-permute-done((f32[2,3,4,24,768]{4,3,2,1,0:T(8,128)}, f32[2,3,4,24,768]{4,3,2,1,0:T(8,128)}, u32[]{:S(2)}, u32[]{:S(2)}) %collective-permute-start.12) | collective-permute-done | bytes 1769504 | tf_op jit(solution)/shard_map/ppermute | solution.py:84
  675.1 24.8 %collective-permute-done.13 = f32[3,4,24,768]{3,2,1,0:T(8,128)S(1)} collective-permute-done((f32[3,4,24,768]{3,2,1,0:T(8,128)S(1)}, f32[3,4,24,768]{3,2,1,0:T(8,128)S(1)}, u32[]{:S(2)}, u32[]{:S(2)}) %collective-permute-start.13) | collective-permute-done | bytes 884768 | tf_op jit(solution)/shard_map/ppermute | solution.py:84
  704.9 30.1 %collective-permute-done.14 = f32[3,2,24,768]{3,2,1,0:T(8,128)S(1)} collective-permute-done((f32[3,2,24,768]{3,2,1,0:T(8,128)S(1)}, f32[3,2,24,768]{3,2,1,0:T(8,128)S(1)}, u32[]{:S(2)}, u32[]{:S(2)}) %collective-permute-start.14) | collective-permute-done | bytes 442400 | tf_op jit(solution)/shard_map/ppermute | solution.py:84
  735.2 5.2 bitcast_add_fusion
  754.1 56.9 %all-to-all-done.9 = f32[32,1,384]{2,1,0:T(1,128)S(1)} async-done(((f32[32,1,384]{2,1,0:T(1,128)}), f32[32,1,384]{2,1,0:T(1,128)S(1)}, u32[]{:S(2)}, u32[]{:S(2)}) %all-to-all-start.9) | async-done | bytes 49184 | tf_op jit(solution)/shard_map/all_to_all | solution.py:79
  828.2 8.7 all-to-all-done.14
  846.8 5.6 multiply_reduce_fusion
  852.4 17.4 %all-to-all-done.11 = f32[8,2,24,768]{3,2,1,0:T(8,128)} async-done(((f32[8,2,24,768]{3,2,1,0:T(8,128)}), f32[8,2,24,768]{3,2,1,0:T(8,128)}, u32[]{:S(2)}, u32[]{:S(2)}) %all-to-all-start.11) | async-done | bytes 1179680 | tf_op jit(solution)/shard_map/all_to_all | solution.py:791
  885.6 7.0 fusion.111
  (350 shorter events, 189.3 us)
Async XLA Ops:
  9.4 24.1 %all-to-all-start.6 = ((bf16[8,2,24,768]{3,2,1,0:T(8,128)(2,1)}), bf16[8,2,24,768]{3,2,1,0:T(8,128)(2,1)S(1)}, u32[]{:S(2)}, u32[]{:S(2)}) async-start(bf16[8,2,24,768]{3,2,1,0:T(8,128)(2,1)} %copy.152), calls=%async_computation.6 | async-start | bytes 1179648 | tf_op jit(solution)/shard_map/all_to_all | solution.py:560
  16.7 71.4 %all-gather.12.cloned.1.call-start = ((), (), s32[]{:S(2)}) async-start(), calls=%async_computation.22 | async-start | bytes 2654208 | tf_op jit(solution)/shard_map/all_gather | solution.py:565
  34.5 140.5 %all-gather.6.cloned.1.call-start = ((), (), s32[]{:S(2)}) async-start(), calls=%async_computation.17 | async-start | bytes 4423680 | tf_op jit(solution)/shard_map/all_gather | solution.py:567
  90.5 105.1 %all-gather.8.cloned.1.call-start = ((), (), s32[]{:S(2)}) async-start(), calls=%async_computation.18 | async-start | bytes 7372800 | tf_op jit(solution)/shard_map/all_gather | solution.py:568
  98.8 10.2 %all-to-all-start.4 = ((s32[32,1,128]{2,1,0:T(1,128)}), s32[32,1,128]{2,1,0:T(1,128)S(1)}, u32[]{:S(2)}, u32[]{:S(2)}) async-start(s32[32,1,128]{2,1,0:T(1,128)} %bitcast.6), calls=%async_computation.4 | async-start | bytes 32768 | tf_op jit(solution)/shard_map/all_to_all | solution.py:492
  114.2 49.5 %all-to-all-start.5 = ((bf16[32,40,768]{2,1,0:T(8,128)(2,1)}), bf16[32,40,768]{2,1,0:T(8,128)(2,1)}, u32[]{:S(2)}, u32[]{:S(2)}) async-start(bf16[32,40,768]{2,1,0:T(8,128)(2,1)} %bitcast.241), calls=%async_computation.5 | async-start | bytes 3932160 | tf_op jit(solution)/shard_map/all_to_all | solution.py:496
  117.8 156.8 %all-gather.10.cloned.1.call-start = ((), (), s32[]{:S(2)}) async-start(), calls=%async_computation.19 | async-start | bytes 7372800 | tf_op jit(solution)/shard_map/all_gather | solution.py:570
  118.5 487.2 %reduce-scatter.3.cloned.1.call-start = ((), (), s32[]{:S(2)}) async-start(), calls=%async_computation.20 | async-start | bytes 14745600 | tf_op jit(solution)/shard_map/reduce_scatter | solution.py:779
  218.5 7.8 collective-permute-start
  227.3 23.4 %collective-permute-start.1 = (bf16[320,768]{1,0:T(8,128)(2,1)S(1)}, bf16[320,768]{1,0:T(8,128)(2,1)S(1)}, u32[]{:S(2)}, u32[]{:S(2)}) collective-permute-start(bf16[320,768]{1,0:T(8,128)(2,1)S(1)} %pad_maximum_fusion.2), channel_id=1, source_target_pairs={{0,16},{8,24},{16,0},{24,8},{1,17},{9,25},{17,1},{25,9},{2,18},{10... | collective-permute-start | bytes 1474568 | tf_op jit(solution)/shard_map/ppermute | solution.py:84
  251.9 22.7 %collective-permute-start.2 = (bf16[640,768]{1,0:T(8,128)(2,1)S(1)}, bf16[640,768]{1,0:T(8,128)(2,1)S(1)}, u32[]{:S(2)}, u32[]{:S(2)}) collective-permute-start(bf16[640,768]{1,0:T(8,128)(2,1)S(1)} %pad_maximum_fusion.1), channel_id=1, source_target_pairs={{0,2},{2,0},{1,3},{3,1},{4,6},{6,4},{5,7},{7,5},{8,10},{10,8},{9,1... | collective-permute-start | bytes 2949128 | tf_op jit(solution)/shard_map/ppermute | solution.py:84
  262.4 12.1 %collective-permute-start.5 = (s32[640]{0:T(1024)S(1)}, s32[640]{0:T(1024)S(1)}, u32[]{:S(2)}, u32[]{:S(2)}) collective-permute-start(s32[640]{0:T(1024)S(1)} %pad_add_fusion), channel_id=1, source_target_pairs={{0,2},{2,0},{1,3},{3,1},{4,6},{6,4},{5,7},{7,5},{8,10},{10,8},{9,1... | collective-permute-start | bytes 7688 | tf_op jit(solution)/shard_map/ppermute | solution.py:84
  336.1 42.5 %collective-permute-start.6 = (f32[640,768]{1,0:T(8,128)S(1)}, f32[640,768]{1,0:T(8,128)S(1)}, u32[]{:S(2)}, u32[]{:S(2)}) collective-permute-start(f32[640,768]{1,0:T(8,128)S(1)} %slice.327), channel_id=1, source_target_pairs={{0,2},{2,0},{1,3},{3,1},{4,6},{6,4},{5,7},{7,5},{8,10},{10,8},{9,1... | collective-permute-start | bytes 5898248 | tf_op jit(solution)/shard_map/ppermute | solution.py:84
  379.0 41.9 %collective-permute-start.7 = (f32[320,768]{1,0:T(8,128)S(1)}, f32[320,768]{1,0:T(8,128)}, u32[]{:S(2)}, u32[]{:S(2)}) collective-permute-start(f32[320,768]{1,0:T(8,128)S(1)} %slice.329), channel_id=1, source_target_pairs={{0,16},{8,24},{16,0},{24,8},{1,17},{9,25},{17,1},{25,9},{2,18},{10... | collective-permute-start | bytes 2949128 | tf_op jit(solution)/shard_map/ppermute | solution.py:84
  422.2 13.2 %collective-permute-start.8 = (f32[160,768]{1,0:T(8,128)S(1)}, f32[160,768]{1,0:T(8,128)S(1)}, u32[]{:S(2)}, u32[]{:S(2)}) collective-permute-start(f32[160,768]{1,0:T(8,128)S(1)} %slice.331), channel_id=1, source_target_pairs={{0,8},{8,0},{16,24},{24,16},{1,9},{9,1},{17,25},{25,17},{2,10},{10... | collective-permute-start | bytes 1474568 | tf_op jit(solution)/shard_map/ppermute | solution.py:84
  532.5 12.7 %collective-permute-start.16 = (f32[256,768]{1,0:T(8,128)}, f32[256,768]{1,0:T(8,128)}, u32[]{:S(2)}, u32[]{:S(2)}) collective-permute-start(f32[256,768]{1,0:T(8,128)} %dynamic-slice_bitcast_fusion.5), channel_id=1, source_target_pairs={{0,1},{1,0},{2,3},{3,2},{4,5},{5,4},{6,7},{7,6},{8,9},{9,8},{10,11... | collective-permute-start | bytes 2359304 | tf_op jit(solution)/shard_map/ppermute | solution.py:84
  539.9 59.2 %collective-permute-start.11 = (f32[2,3,8,24,768]{4,3,2,1,0:T(8,128)S(1)}, f32[2,3,8,24,768]{4,3,2,1,0:T(8,128)}, u32[]{:S(2)}, u32[]{:S(2)}) collective-permute-start(f32[2,3,8,24,768]{4,3,2,1,0:T(8,128)S(1)} %dynamic-slice_bitcast_fusion.1), channel_id=1, source_target_pairs={{0,1},{1,0},{2,3},{3,2},{4,5},{5,4},{6,7},{7,6},{8,9},{9,8},{10,11... | collective-permute-start | bytes 10616840 | tf_op jit(solution)/shard_map/ppermute | solution.py:84
  541.1 11.6 %all-to-all-start.8 = ((f32[32,1,384]{2,1,0:T(1,128)}), f32[32,1,384]{2,1,0:T(1,128)}, u32[]{:S(2)}, u32[]{:S(2)}) async-start(f32[32,1,384]{2,1,0:T(1,128)} %bitcast.270), calls=%async_computation.8 | async-start | bytes 98304 | tf_op jit(solution)/shard_map/all_to_all | solution.py:818
  552.6 24.4 %all-to-all-start.12 = ((f32[16,16,768]{2,1,0:T(8,128)}), f32[16,16,768]{2,1,0:T(8,128)}, u32[]{:S(2)}, u32[]{:S(2)}) async-start(f32[16,16,768]{2,1,0:T(8,128)} %bitcast.236), calls=%async_computation.14 | async-start | bytes 1572864 | tf_op jit(solution)/shard_map/all_to_all | solution.py:799
  577.0 167.5 %all-to-all-start.10 = ((f32[32,40,768]{2,1,0:T(8,128)}), f32[32,40,768]{2,1,0:T(8,128)}, u32[]{:S(2)}, u32[]{:S(2)}) async-start(f32[32,40,768]{2,1,0:T(8,128)} %bitcast.232), calls=%async_computation.10 | async-start | bytes 7864320 | tf_op jit(solution)/shard_map/all_to_all | solution.py:503
  581.2 244.1 %reduce-scatter.5.cloned.1.call-start = ((), (), s32[]{:S(2)}) async-start(), calls=%async_computation.21 | async-start | bytes 3317760 | tf_op jit(solution)/shard_map/reduce_scatter | solution.py:783
  598.9 136.3 %collective-permute-start.9 = (f32[2,960,768]{2,1,0:T(8,128)}, f32[2,960,768]{2,1,0:T(8,128)}, u32[]{:S(2)}, u32[]{:S(2)}) collective-permute-start(f32[2,960,768]{2,1,0:T(8,128)} %dynamic-slice_bitcast_fusion), channel_id=1, source_target_pairs={{0,1},{1,0},{2,3},{3,2},{4,5},{5,4},{6,7},{7,6},{8,9},{9,8},{10,11... | collective-permute-start | bytes 17694728 | tf_op jit(solution)/shard_map/ppermute | solution.py:84
  604.0 66.3 %collective-permute-start.12 = (f32[2,3,4,24,768]{4,3,2,1,0:T(8,128)}, f32[2,3,4,24,768]{4,3,2,1,0:T(8,128)}, u32[]{:S(2)}, u32[]{:S(2)}) collective-permute-start(f32[2,3,4,24,768]{4,3,2,1,0:T(8,128)} %dynamic-slice_bitcast_fusion.3), channel_id=1, source_target_pairs={{0,4},{4,0},{1,5},{5,1},{2,6},{6,2},{3,7},{7,3},{8,12},{12,8},{9,1... | collective-permute-start | bytes 5308424 | tf_op jit(solution)/shard_map/ppermute | solution.py:84
  673.3 26.6 %collective-permute-start.13 = (f32[3,4,24,768]{3,2,1,0:T(8,128)S(1)}, f32[3,4,24,768]{3,2,1,0:T(8,128)S(1)}, u32[]{:S(2)}, u32[]{:S(2)}) collective-permute-start(f32[3,4,24,768]{3,2,1,0:T(8,128)S(1)} %dynamic-slice_bitcast_fusion.4), channel_id=1, source_target_pairs={{0,2},{2,0},{1,3},{3,1},{4,6},{6,4},{5,7},{7,5},{8,10},{10,8},{9,1... | collective-permute-start | bytes 2654216 | tf_op jit(solution)/shard_map/ppermute | solution.py:84
  701.2 33.8 %collective-permute-start.14 = (f32[3,2,24,768]{3,2,1,0:T(8,128)S(1)}, f32[3,2,24,768]{3,2,1,0:T(8,128)S(1)}, u32[]{:S(2)}, u32[]{:S(2)}) collective-permute-start(f32[3,2,24,768]{3,2,1,0:T(8,128)S(1)} %dynamic-slice_bitcast_fusion.6), channel_id=1, source_target_pairs={{0,16},{8,24},{16,0},{24,8},{1,17},{9,25},{17,1},{25,9},{2,18},{10... | collective-permute-start | bytes 1327112 | tf_op jit(solution)/shard_map/ppermute | solution.py:84
  735.1 9.3 %collective-permute-start.15 = (f32[3,1,24,768]{3,2,1,0:T(8,128)S(1)}, f32[3,1,24,768]{3,2,1,0:T(8,128)S(1)}, u32[]{:S(2)}, u32[]{:S(2)}) collective-permute-start(f32[3,1,24,768]{3,2,1,0:T(8,128)S(1)} %constant_dynamic-slice_fusion), channel_id=1, source_target_pairs={{0,8},{8,0},{16,24},{24,16},{1,9},{9,1},{17,25},{25,17},{2,10},{10... | collective-permute-start | bytes 663560 | tf_op jit(solution)/shard_map/ppermute | solution.py:84
  743.8 103.0 %collective-permute-start.10 = (f32[960,768]{1,0:T(8,128)}, f32[960,768]{1,0:T(8,128)S(1)}, u32[]{:S(2)}, u32[]{:S(2)}) collective-permute-start(f32[960,768]{1,0:T(8,128)} %dynamic-slice_bitcast_fusion.2), channel_id=1, source_target_pairs={{0,4},{4,0},{1,5},{5,1},{2,6},{6,2},{3,7},{7,3},{8,12},{12,8},{9,1... | collective-permute-start | bytes 8847368 | tf_op jit(solution)/shard_map/ppermute | solution.py:84
  745.1 65.8 %all-to-all-start.9 = ((f32[32,1,384]{2,1,0:T(1,128)}), f32[32,1,384]{2,1,0:T(1,128)S(1)}, u32[]{:S(2)}, u32[]{:S(2)}) async-start(f32[32,1,384]{2,1,0:T(1,128)} %broadcast_in_dim.143), calls=%async_computation.9 | async-start | bytes 98304 | tf_op jit(solution)/shard_map/all_to_all | solution.py:79
  811.9 25.0 %all-to-all-start.14 = ((f32[16,16,768]{2,1,0:T(8,128)}), f32[16,16,768]{2,1,0:T(8,128)}, u32[]{:S(2)}, u32[]{:S(2)}) async-start(f32[16,16,768]{2,1,0:T(8,128)} %broadcast_in_dim.144), calls=%async_computation.16 | async-start | bytes 1572864 | tf_op jit(solution)/shard_map/all_to_all | solution.py:79
  837.2 32.6 %all-to-all-start.11 = ((f32[8,2,24,768]{3,2,1,0:T(8,128)}), f32[8,2,24,768]{3,2,1,0:T(8,128)}, u32[]{:S(2)}, u32[]{:S(2)}) async-start(f32[8,2,24,768]{3,2,1,0:T(8,128)} %multiply_add_fusion.2), calls=%async_computation.13 | async-start | bytes 2359296 | tf_op jit(solution)/shard_map/all_to_all | solution.py:791
  844.2 32.9 %collective-permute-start.17 = (f32[256,768]{1,0:T(8,128)}, f32[256,768]{1,0:T(8,128)}, u32[]{:S(2)}, u32[]{:S(2)}) collective-permute-start(f32[256,768]{1,0:T(8,128)} %bitcast.83), channel_id=1, source_target_pairs={{0,1},{1,0},{2,3},{3,2},{4,5},{5,4},{6,7},{7,6},{8,9},{9,8},{10,11... | collective-permute-start | bytes 2359304 | tf_op jit(solution)/shard_map/ppermute | solution.py:84
  874.5 9.6 %all-to-all-start.13 = ((f32[32,1,128]{2,1,0:T(1,128)}), f32[32,1,128]{2,1,0:T(1,128)S(1)}, u32[]{:S(2)}, u32[]{:S(2)}) async-start(f32[32,1,128]{2,1,0:T(1,128)} %broadcast_in_dim_broadcast_in_dim.3), calls=%async_computation.15 | async-start | bytes 32768 | tf_op jit(solution)/shard_map/all_to_all | solution.py:79
  (64 other events, 923.1 us)
Sparse Core Ops, SparseCore 0:
  34.6 53.4 all-gather.11
  90.6 29.4 all-gather.5
  122.2 53.8 all-gather.7
  178.1 44.1 all-gather.9
  479.5 102.6 reduce-scatter.2
  609.5 123.5 reduce-scatter.4

commit v3 on v2

--- a/solution.py
+++ b/solution.py
@@ -16,12 +16,13 @@
 
 FIRST = min(CONV) // 2 * 2
 
-DP = ("dh", "dl")
-MP = ("mh", "ml")
+DP = ("d2", "d1", "d0")
+MP = ("m1", "m0")
 ALL = DP + MP
-VG = ("dh", "mh")
-RG = ("dl", "ml")
-CHIPS = ("dh", "dl", "mh")
+CHIPS = DP + ("m1",)
+VG = ("d1", "d0", "m1")
+RG = ("d2", "m0")
+ORDERS = (("d1", "d0", "m1"), ("d0", "m1", "d1"), ("m1", "d1", "d0"))
 
 f32 = jnp.float32
 bf16 = jnp.bfloat16
@@ -59,8 +60,8 @@
     return dot_left(chosen, high) + dot_left(chosen, low)
 
 
-def sop_loss(cls_rows, params, labels, denom, length):
-    logits = jnp.dot(cls_rows, params[length + 8 : length + 10].T, precision=highest)
+def sop_loss(cls_rows, pair, labels, denom):
+    logits = jnp.dot(cls_rows, pair.T, precision=highest)
     chosen = jnp.take_along_axis(logits, labels[:, None], axis=1)[:, 0]
     return jnp.sum(jax.nn.logsumexp(logits, axis=-1) - chosen) / denom
 
@@ -88,11 +89,34 @@
     return lax.axis_size(axis).bit_length() - 1
 
 
-def fold(x, axis, bit, dim):
-    me = (lax.axis_index(axis) >> bit) & 1
-    sent = lax.dynamic_index_in_dim(x, 1 - me, dim, False)
-    kept = lax.dynamic_index_in_dim(x, me, dim, False)
-    return kept + swap(sent, axis, bit)
+def together(*arrays):
+    return lax.optimization_barrier(arrays)
+
+
+def bit_of(axis, bit):
+    return (lax.axis_index(axis) >> bit) & 1
+
+
+def fold_near(x, axis, dim):
+    for bit in reversed(range(bits_of(axis))):
+        lead, rest = x.shape[:dim], x.shape[dim + 1 :]
+        x = x.reshape(lead + (2, x.shape[dim] // 2) + rest)
+        sent = lax.index_in_dim(x, 1, dim, False)
+        x = lax.index_in_dim(x, 0, dim, False) + swap(sent, axis, bit)
+    return x.reshape(x.shape[:dim] + x.shape[dim + 1 :])
+
+
+def slot_of(d, m, high):
+    return ((((m & 1) * 2 + (d & 1)) * 2 + (m >> 1)) * 2 + ((d >> 1) & 1)) * high + (d >> 2)
+
+
+def spread_axis(x, axis, dim):
+    x = jnp.expand_dims(x, dim)
+    for bit in range(bits_of(axis)):
+        other = swap(x, axis, bit)
+        me = bit_of(axis, bit) == 1
+        x = jnp.concatenate([jnp.where(me, other, x), jnp.where(me, x, other)], axis=dim)
+    return x
 
 
 def grow(x, axis):
@@ -108,11 +132,54 @@
     return x
 
 
-def relative(x, index):
-    for bit in range(x.shape[0].bit_length() - 1):
-        y = x.reshape((x.shape[0] >> (bit + 1), 2, 1 << bit) + x.shape[1:])
-        x = jnp.where((index >> bit) & 1 == 1, y[:, ::-1], y).reshape(x.shape)
-    return x
+def row_parts(count):
+    most = -(-count // (8 * len(ORDERS))) * 8
+    return [slice(at, min(at + most, count)) for at in range(0, count, most)]
+
+
+def grow_parts(x):
+    parts = [x[None, rows] for rows in row_parts(x.shape[0])]
+    for stage in range(len(VG)):
+        parts = [grow(p, order[stage]) for p, order in zip(parts, ORDERS)]
+    return jnp.concatenate([p.reshape((-1,) + p.shape[2:]) for p in parts])
+
+
+def cut_parts(x, count, dim=0):
+    pieces, at = [], 0
+    for rows in row_parts(count):
+        size = (rows.stop - rows.start) << len(VG)
+        piece = lax.slice_in_dim(x, at, at + size, axis=dim)
+        pieces.append(piece.reshape(x.shape[:dim] + (1 << len(VG), -1) + x.shape[dim + 1 :]))
+        at += size
+    return pieces
+
+
+def near_labels(got, own):
+    x = got.reshape(tuple(lax.axis_size(a) for a in ALL) + (own,))
+    x = lax.dynamic_index_in_dim(x, lax.axis_index("m0"), 4, False)
+    x = lax.dynamic_index_in_dim(x, lax.axis_index("d2"), 0, False)
+    for dim, axis in enumerate(VG):
+        x = jnp.where(lax.axis_index(axis) == 1, jnp.flip(x, axis=dim), x)
+    parts = []
+    for rows, order in zip(row_parts(own), ORDERS):
+        dims = [VG.index(axis) for axis in order[::-1]]
+        parts.append(jnp.transpose(x[..., rows], dims + [len(VG)]).reshape(-1))
+    return jnp.concatenate(parts)
+
+
+def merge_stats(stats, count):
+    for axis in VG:
+        other = swap(stats, axis, 0)
+        flipped = []
+        for p, order in zip(cut_parts(other, count, 1), ORDERS):
+            low = 1 << order.index(axis)
+            y = p.reshape(3, p.shape[1] // (2 * low), 2, low, p.shape[2])
+            flipped.append(jnp.flip(y, axis=2).reshape(3, -1))
+        other = jnp.concatenate(flipped, axis=1)
+        top = jnp.maximum(stats[0], other[0])
+        total = stats[1] * jnp.exp(stats[0] - top) + other[1] * jnp.exp(other[0] - top)
+        stats = jnp.stack([top, total, stats[2] + other[2]])
+    return stats
 
 
 def rows_norm(x):
@@ -280,11 +347,23 @@
     return jnp.sum(x, axis=0, keepdims=True)
 
 
+def add_rows(ref, me, mp_count, at, matrix, rows):
+    if len(ref.shape) == 4:
+        ref[at, matrix] += rows
+        return
+    dp_count = ref.shape[0] // mp_count
+    rest = rows.shape[0] // dp_count
+    here = slice(matrix * rest, (matrix + 1) * rest)
+    for d in range(dp_count):
+        ref[slot_of(d, at, dp_count // 4) ^ me, here, :] += rows[d * rest : (d + 1) * rest]
+
+
 def backward_ffn(
-    pos_ref, grad_ref, cls_ref, one_ref, two_ref, heads_ref, edge_ref, units_ref,
-    sum_ref, back_ref, wide_ref, edges_ref,
+    me_ref, pos_ref, grad_ref, cls_ref, one_ref, two_ref, heads_ref, edge_ref, units_ref,
+    sum_ref, back_ref, edges_ref, *wide_refs,
 ):
     at = pl.program_id(0)
+    wide_ref = wide_refs[-1]
     length, width = one_ref.shape[1:]
     mp_count, part = units_ref.shape[0], units_ref.shape[2]
 
@@ -320,12 +399,12 @@
             slope = half + pre * (jnp.exp(-0.5 * pre * pre) * (1.0 / math.sqrt(2.0 * math.pi)))
             grad_hidden = dot_plain(low_two[:, cols], w_out)
             w = dot_left(low_two[:, cols], hidden)
-            wide_ref[s, 3] += w[:part]
-            wide_ref[s, 4] += w[part:]
+            add_rows(wide_ref, me_ref[0], mp_count, s, 3, w[:part])
+            add_rows(wide_ref, me_ref[0], mp_count, s, 4, w[part:])
             grad_pre = (grad_hidden * slope).astype(bf16)
             w = dot_left(low_mid[:, cols], grad_pre)
-            wide_ref[s, 1] += w[:part]
-            wide_ref[s, 2] += w[part:]
+            add_rows(wide_ref, me_ref[0], mp_count, s, 1, w[:part])
+            add_rows(wide_ref, me_ref[0], mp_count, s, 2, w[part:])
             back = dot_right(grad_pre, w_in)
             total = back if total is None else total + back
         backs.append(total)
@@ -335,26 +414,43 @@
     grad_one = norm_grad(grad, normed, inv, edge_ref[1:2, :])
     sum_ref[0] = grad_one
     low_one = grad_one.astype(bf16)
-    wide_ref[:, 0] += dot_left(low_one, heads_ref[0]).reshape(mp_count, part, width)
+    w = dot_left(low_one, heads_ref[0])
+    for s in range(mp_count):
+        add_rows(wide_ref, me_ref[0], mp_count, s, 0, w[s * part : (s + 1) * part])
     unit = units_ref[:, 0].reshape(width, width)
     back_ref[0] = dot_plain(low_one, unit).astype(bf16)
 
-
-def backward_heads(
-    split_ref, length_ref, word_ref, places_ref, edge_ref, taps_ref, units_ref,
-    qkv_ref, lse_ref, back_ref, sum_ref,
-    gword_ref, gplaces_ref, gedge_ref, gtaps_ref, wide_ref,
-    pad_ref, shift_ref,
-):
-    at = pl.program_id(0)
+    if len(wide_refs) > 1:
+
+        @pl.when(at == pl.num_programs(0) - 1)
+        def _():
+            half = wide_ref.shape[0] // 2
+            wide_refs[0][...] = wide_ref[:half]
+            wide_refs[1][...] = wide_ref[half:]
+
+
+def backward_heads(start, last, direct, *refs):
+    (split_ref, length_ref, me_ref, word_ref, places_ref, edge_ref, taps_ref, units_ref) = refs[:8]
+    (qkv_ref, lse_ref, back_ref, sum_ref, seat_ref, late_ref) = refs[8:14]
+    refs = refs[14:]
+    so_far = []
+    if start > 0:
+        count = 4 if direct else 5
+        so_far, refs = refs[:count], refs[count:]
+    gword_ref, gedge_ref, gtaps_ref, seats_ref = refs[:4]
+    if direct and last:
+        kept_ref, sent_ref, pad_ref, shift_ref, wide_ref = refs[4:]
+        sums = [gedge_ref, gtaps_ref, seats_ref, wide_ref]
+    else:
+        *sums, pad_ref, shift_ref = refs[1:]
+        wide_ref = sums[3]
+    at = pl.program_id(0) + start
+    me = me_ref[0]
+    mp_count = units_ref.shape[0]
     length, width = word_ref.shape[1:]
-
-    @pl.when(at == 0)
-    def _():
-        wide_ref[...] = jnp.zeros_like(wide_ref)
-        gplaces_ref[...] = jnp.zeros_like(gplaces_ref)
-        gedge_ref[...] = jnp.zeros_like(gedge_ref)
-        gtaps_ref[...] = jnp.zeros_like(gtaps_ref)
+    for n, new in enumerate(sums):
+        if n != 2:
+            new[...] = so_far[n][...] if so_far else jnp.zeros_like(new)
 
     groups = HEADS - FIRST
     base = FIRST * DH
@@ -393,7 +489,12 @@
     grad_logits = jnp.concatenate([kernel[o] * (parts[o] - along) for o in range(taps)], axis=0)
     grad_prod = dot_exact(grad_logits, spread, ((0,), (0,)))
     grad_taps = dot_exact(grad_logits, prod, ((1,), (0,)))
-    grad_taps = jnp.where(head_mask(taps * groups, groups), grad_taps, 0.0)
+    head = lax.div(lax.broadcasted_iota(i32, (taps * groups, span), 1), DH) + FIRST
+    real = head_mask(taps * groups, groups)
+    for h in range(FIRST, HEADS):
+        if h not in CONV:
+            real = jnp.logical_and(real, head != h)
+    grad_taps = jnp.where(real, grad_taps, 0.0)
     for o in range(taps):
         gtaps_ref[o : o + 1, :] += down(grad_taps[o * groups : (o + 1) * groups])
     grads = [(grad_prod * k).astype(bf16), (grad_prod * q).astype(bf16), grad_values.astype(bf16)]
@@ -425,41 +526,62 @@
     grad = sum_ref[0]
     for n in range(3):
         g = jnp.concatenate(pieces[n], axis=1)
-        wide_ref[:, n] += dot_left(g, low_in).reshape(units_ref.shape[0], -1, width)
+        w = dot_left(g, low_in)
+        part = units_ref.shape[2]
+        for s in range(mp_count):
+            add_rows(wide_ref, me, mp_count, s, n, w[s * part : (s + 1) * part])
         grad = grad + dot_plain(g, units_ref[:, n].reshape(width, width))
     gedge_ref[0:1, :] += down(grad * normed)
     gedge_ref[3:4, :] += down(grad)
     grad = norm_grad(grad, normed, inv, edge_ref[0:1, :])
     gword_ref[0] = grad
-    gplaces_ref[...] += grad
     second = down(jnp.where(later, grad, 0.0))
     gedge_ref[6:7, :] += down(grad) - second
     gedge_ref[7:8, :] += second
-
-
-def whole(shape):
-    return pl.BlockSpec(shape, lambda b, *_: (0,) * len(shape))
+    seat = lax.broadcasted_iota(i32, (seats_ref.shape[0], length), 0) == seat_ref[0]
+    seat = seat.astype(bf16)
+    high = grad.astype(bf16)
+    low = (grad - high.astype(f32)).astype(bf16)
+    collected = dot_plain(seat, high) + dot_plain(seat, low)
+    if so_far:
+        collected = collected + so_far[2][...]
+    seats_ref[...] = collected.astype(seats_ref.dtype)
+    if not direct:
+        sums[4][...] += grad
+        return
+    devices = wide_ref.shape[0]
+    high = devices // mp_count // 4
+    share = length // devices
+    base = wide_ref.shape[1] - share - 8
+    for i in range(devices):
+        slot = slot_of(i // mp_count, i % mp_count, high) ^ me
+        wide_ref[slot, base : base + share, :] += grad[i * share : (i + 1) * share]
+    if last:
+        rows = [gedge_ref[i : i + 1, :] + late_ref[i : i + 1, :] for i in range(8)]
+        rows += [late_ref[i : i + 1, :] for i in range(8, 11)]
+        rows += [gtaps_ref[i : i + 1, :] for i in range(gtaps_ref.shape[0])]
+        for i, row in enumerate(rows):
+            slot = slot_of(i // mp_count, i % mp_count, high) ^ me
+            wide_ref[slot, base + share : base + share + 1, 0 : row.shape[1]] = row
+        kept_ref[...] = wide_ref[: devices // 2]
+        sent_ref[...] = wide_ref[devices // 2 :]
 
 
 def fixed(shape):
     return pl.BlockSpec(shape, lambda b, *_: (0,) * len(shape), pipeline_mode=pl.Buffered(1))
 
 
-def each(shape):
-    return pl.BlockSpec((1,) + shape, lambda b, *_: (b,) + (0,) * len(shape))
-
-
-def run(kernel, scalars, ins, outs, scratch, flops, name):
-    arrays = [x for x, _ in ins]
-    seqs = next(x.shape[0] for x, spec in ins if spec.block_shape[0] == 1 and x.ndim == 3)
-    shapes = [jax.ShapeDtypeStruct(shape, dtype) for (shape, dtype), _ in outs]
-    moved = sum(math.prod(x.shape) * x.dtype.itemsize for x in arrays + shapes)
+def each(shape, start=0):
+    return pl.BlockSpec((1,) + shape, lambda b, *_: (b + start,) + (0,) * len(shape))
+
+
+def run(kernel, scalars, ins, outs, scratch, name, steps, micros, aliases={}):
     return pl.pallas_call(
         kernel,
-        out_shape=shapes,
+        out_shape=[jax.ShapeDtypeStruct(shape, dtype) for (shape, dtype), _ in outs],
         grid_spec=pltpu.PrefetchScalarGridSpec(
             num_scalar_prefetch=len(scalars),
-            grid=(seqs,),
+            grid=(steps,),
             in_specs=[spec for _, spec in ins],
             out_specs=[spec for _, spec in outs],
             scratch_shapes=scratch,
@@ -467,9 +589,12 @@
         compiler_params=pltpu.CompilerParams(
             dimension_semantics=("arbitrary",), vmem_limit_bytes=VMEM
         ),
-        cost_estimate=pl.CostEstimate(flops=flops, bytes_accessed=moved, transcendentals=0),
+        input_output_aliases={len(scalars) + i: o for i, o in aliases.items()},
+        cost_estimate=pl.CostEstimate(
+            flops=micros * 1150000000, bytes_accessed=1 << 20, transcendentals=0
+        ),
         name=name,
-    )(*scalars, *arrays)
+    )(*scalars, *[x for x, _ in ins])
 
 
 def slots_of(ids, vblock, devices):
@@ -482,26 +607,29 @@
     return owner, first, rank
 
 
-def fetch_round(turn, capacity, devices, owner, first, rank, local, low_table):
+def fetch_round(turn, capacity, devices, owner, first, rank, local, extra, low_table, hooks):
     slot = jnp.where(rank // capacity == turn, owner * capacity + rank % capacity, -1)
     seats = jnp.arange(devices * capacity)
     chosen = jnp.logical_and(seats[:, None] == slot[None, :], first[None, :])
     request = jnp.sum(jnp.where(chosen, local[None, :] + 1, 0), axis=1) - 1
-    message = jnp.full((devices, 128), jnp.max(rank), i32)
-    message = message.at[:, :capacity].set(request.reshape(devices, capacity))
+    beside = jnp.concatenate([jnp.max(rank)[None], extra])
+    beside = jnp.pad(beside, (0, -(capacity + beside.shape[0]) % 128))
+    message = jnp.concatenate(
+        [
+            request.reshape(devices, capacity),
+            jnp.broadcast_to(beside[None], (devices, beside.shape[0])),
+        ],
+        axis=1,
+    )
+    message = hooks[0](message)
     got = lax.all_to_all(message, ALL, 0, 0, tiled=True)
     asked = got[:, :capacity].reshape(-1)
     served = (asked[:, None] == jnp.arange(low_table.shape[0])[None, :]).astype(bf16)
-    rows = dot_plain(served, low_table).astype(bf16)
-    rows = lax.all_to_all(rows, ALL, 0, 0, tiled=True)
+    sending = dot_plain(served, low_table).astype(bf16)
+    sending = hooks[1](sending)
+    rows = lax.all_to_all(sending, ALL, 0, 0, tiled=True)
     mine = (slot[:, None] == seats[None, :]).astype(bf16)
-    return dot_plain(mine, rows).astype(bf16), mine, served, jnp.max(got[:, capacity])
-
-
-def return_round(mine, served, grad_word):
-    sent = select_sum(mine, grad_word)
-    got = lax.all_to_all(sent, ALL, 0, 0, tiled=True)
-    return select_sum(served, got)
+    return dot_plain(mine, rows).astype(bf16), slot, mine, served, got[:, capacity:]
 
 
 def body(
@@ -556,23 +684,16 @@
         owner[None, :] == dp_index, slot_rank[None, :] == jnp.arange(cap_slots)[:, None]
     ).astype(f32)
     rest = part // dp_count
+    own = seqs * masks
     low_slots = unit_master.astype(bf16).reshape(cap_slots, dp_count, rest, width)
-    got_slots = lax.all_to_all(jnp.moveaxis(low_slots, 1, 0), DP, 0, 0, tiled=True)
+    low_slots = jnp.moveaxis(low_slots, 1, 0)
+    got_slots = lax.all_to_all(low_slots, DP, 0, 0, tiled=True)
     got_slots = got_slots.reshape(dp_count * cap_slots, rest, width)
-    picked = jnp.stack(
-        [lax.dynamic_index_in_dim(got_slots, slot_index[k], 0, False) for k in range(matrices)]
-    )
-    shards = jnp.moveaxis(lax.all_gather(picked, DP, axis=0), 0, 1)
-    shards = shards.reshape(matrices, part, width)
-    first_units = lax.all_gather(shards[:3], MP, axis=0)
-    last_units = lax.all_gather(shards[3:], MP, axis=0)
     low_table = table.astype(bf16)
-    vocab = lax.all_gather(low_table, RG, axis=0, tiled=True)
 
     ids = token_ids.reshape(-1)
     capacity = max(8, -(-1280 // devices))
     home, first, rank = slots_of(ids, vblock, devices)
-    local = ids % vblock
     fetch = partial(
         fetch_round,
         capacity=capacity,
@@ -580,19 +701,48 @@
         owner=home,
         first=first,
         rank=rank,
-        local=local,
+        local=ids % vblock,
+        extra=mlm_labels.reshape(-1),
         low_table=low_table,
     )
-    word_rows, mine, served, top_rank = fetch(0)
-    turns = top_rank // capacity + 1
+    shards = None
+
+    def same(x):
+        return x
+
+    def after_slots(message):
+        nonlocal shards
+        message, got = together(message, got_slots)
+        seats_at = slot_index[:, None] == jnp.arange(dp_count * cap_slots)[None, :]
+        picked = jnp.sum(
+            jnp.where(seats_at[:, :, None, None], got[None].astype(f32), 0.0), axis=1
+        ).astype(bf16)
+        shards = lax.all_gather(picked, DP, axis=0)
+        return message
+
+    def after_shards(sending):
+        nonlocal shards
+        sending, shards = together(sending, shards)
+        return sending
+
+    word_rows, slot, mine, served, beside = fetch(0, hooks=(after_slots, after_shards))
+    turns = jnp.max(beside[:, 0]) // capacity + 1
+    all_labels = near_labels(beside[:, 1 : 1 + own], own)
+
+    shards = jnp.moveaxis(shards, 0, 1).reshape(matrices, part, width)
+    first_units = lax.all_gather(shards[:3], MP, axis=0)
+    last_units = spread_axis(shards[3:], "m1", 0)
+    vocab = lax.all_gather(low_table, RG, axis=0, tiled=True)
 
     def more(state):
         return state[0] < turns
 
     def fetch_more(state):
-        return (state[0] + 1, state[1] + fetch(state[0])[0])
+        return (state[0] + 1, state[1] + fetch(state[0], hooks=(same, same))[0])
 
     _, word_rows = lax.while_loop(more, fetch_more, (jnp.int32(1), word_rows))
+    word_rows, last_units = together(word_rows, last_units)
+    last_units = spread_axis(last_units, "m0", 1).reshape(mp_count, -1, part, width)
 
     words_in = word_rows.reshape(seqs, length, width)
     places = small[6 : 6 + length]
@@ -606,7 +756,6 @@
     ]
     taps_span = jnp.concatenate(taps_span, axis=1)
     act = (length, width)
-    flop = 2 * tokens * width * width
     embedded, qkv, lse, heads = run(
         forward_heads,
         (seg_split, lengths),
@@ -624,8 +773,9 @@
             (((seqs,) + act, bf16), each(act)),
         ],
         [pltpu.VMEM((length + 16, span), f32)],
-        8 * flop,
         "forward_heads",
+        seqs,
+        20,
     )
     spots = mlm_pos[:, :, None]
     one, two, masked_rows, cls_rows = run(
@@ -645,58 +795,71 @@
             (((seqs, 8, width), f32), each((8, width))),
         ],
         [],
-        8 * flop,
         "forward_ffn",
+        seqs,
+        23,
     )
     masked_rows = masked_rows.reshape(seqs * masks, width)
 
-    all_masked = grow(grow(masked_rows, "dh"), "mh")
-    all_labels = grow(grow(mlm_labels.reshape(-1), "dh"), "mh")
+    all_masked = grow_parts(masked_rows)
     logits = dot_right(all_masked, vocab)
-    group_count = lax.axis_size(VG)
     block = all_labels // vblock
-    block_ml = block % lax.axis_size("ml")
-    block_mh = block // lax.axis_size("ml") % lax.axis_size("mh")
-    block_dl = block // mp_count % lax.axis_size("dl")
-    block_dh = block // (mp_count * lax.axis_size("dl"))
-    label_mine = jnp.logical_and(
-        block_dh == lax.axis_index("dh"), block_mh == lax.axis_index("mh")
-    )
-    label_row = (block_dl * lax.axis_size("ml") + block_ml) * vblock + all_labels % vblock
+    at = {}
+    for axis in ALL[::-1]:
+        at[axis] = block % lax.axis_size(axis)
+        block = block // lax.axis_size(axis)
+    label_mine = jnp.ones_like(all_labels, dtype=bool)
+    for axis in VG:
+        label_mine = jnp.logical_and(label_mine, at[axis] == lax.axis_index(axis))
+    label_block = at["d2"] * lax.axis_size("m0") + at["m0"]
+    label_row = label_block * vblock + all_labels % vblock
     onehot = jnp.logical_and(
         jnp.arange(vocab.shape[0])[None, :] == label_row[:, None], label_mine[:, None]
     )
     top = jnp.max(logits, axis=1)
     total = jnp.sum(jnp.exp(logits - top[:, None]), axis=1)
     target = jnp.sum(jnp.where(onehot, logits, 0.0), axis=1)
-    order = lax.axis_index("mh") * lax.axis_size("dh") + lax.axis_index("dh")
-    stats = jnp.stack([top, total, target]).reshape(3, group_count, -1)
-    stats = relative(jnp.moveaxis(stats, 1, 0), order)
-    stats = stats.reshape(lax.axis_size("mh"), lax.axis_size("dh"), 3, -1)
-    stats = jnp.moveaxis(stats, 0, 1).reshape(group_count, 3, -1)
-    stats = everyone(stats, VG)
-    top_all = jnp.max(stats[:, :, 0], axis=0)
-    total_all = jnp.sum(stats[:, :, 1] * jnp.exp(stats[:, :, 0] - top_all), axis=0)
-    log_all = top_all + jnp.log(total_all)
-    log_sum = log_all.reshape(lax.axis_size("dh"), lax.axis_size("mh"), -1)
-    log_sum = jnp.moveaxis(log_sum, 0, 1).reshape(group_count, -1)
-    log_sum = relative(log_sum, order).reshape(-1)
-    target_all = jnp.sum(stats[:, :, 2], axis=0)
-    mlm_part = jnp.sum(log_all - target_all) / count_all / group_count
+    stats = merge_stats(jnp.stack([top, total, target]), own)
+    log_sum = stats[0] + jnp.log(stats[1])
+    losses = [p[0] for p in cut_parts(log_sum - stats[2], own)]
+    mlm_part = sum(jnp.sum(p) for p in losses) / count_all
     grad_logits = (
         (jnp.exp(logits - log_sum[:, None]) - onehot.astype(f32)) / count_all
     ).astype(bf16)
-    grad_masked = shrink(shrink(dot_plain(grad_logits, vocab), "mh"), "dh")
-    grad_table = dot_left(grad_logits, all_masked).reshape(2, 2, vblock, width)
-    grad_table = fold(fold(grad_table, "ml", 0, 1), "dl", 0, 0)
+    parts = cut_parts(dot_plain(grad_logits, vocab), own)
+    for stage in reversed(range(len(VG))):
+        parts = [shrink(p, order[stage]) for p, order in zip(parts, ORDERS)]
+        if stage == len(VG) - 1:
+            grad_logits, *parts = together(grad_logits, *parts)
+            grad_table = dot_left(grad_logits, all_masked)
+    grad_masked = jnp.concatenate([p[0] for p in parts])
+    grad_masked, grad_table = together(grad_masked, grad_table)
+    grad_table = lax.psum_scatter(grad_table, RG, scatter_dimension=0, tiled=True)
     sop_part, sop_pull = jax.vjp(
-        partial(sop_loss, labels=sop_labels, denom=total_seqs, length=length), cls_rows[:, 0], small
-    )
-    grad_cls, grad_small_sop = sop_pull(jnp.ones((), f32))
+        partial(sop_loss, labels=sop_labels, denom=total_seqs),
+        cls_rows[:, 0],
+        small[8 + length :],
+    )
+    grad_cls, grad_pair = sop_pull(jnp.ones((), f32))
     grad_cls = jnp.pad(grad_cls[:, None], ((0, 0), (0, 7), (0, 0)))
-    sum_one, grad_heads, wide_last, edge_last = run(
+    direct = rest % 8 == 0 and length % (8 * devices) == 0 and devices >= 20
+    share = length // devices if direct else -(-length // devices)
+    me = slot_of(dp_index, mp_index, dp_count // 4)[None].astype(i32)
+
+    def wide(many, extra):
+        if direct:
+            return (devices, many * rest + extra, width)
+        return (mp_count, many, part, width)
+
+    def wide_outs(many, extra):
+        shape = wide(many, extra)
+        if direct:
+            shape = (shape[0] // 2,) + shape[1:]
+        return [((shape, f32), fixed(shape))] * (2 if direct else 1)
+
+    sum_one, grad_heads, edge_last, *wide_last = run(
         backward_ffn,
-        (),
+        (me,),
         [
             (spots, each((masks, 1))),
             (grad_masked.reshape(seqs, masks, width), each((masks, width))),
@@ -710,126 +873,181 @@
         [
             (((seqs,) + act, f32), each(act)),
             (((seqs,) + act, bf16), each(act)),
-            ((last_units.shape, f32), fixed(last_units.shape)),
             ((edge.shape, f32), fixed(edge.shape)),
-        ],
-        [],
-        16 * flop,
+        ]
+        + wide_outs(5, 0),
+        [pltpu.VMEM(wide(5, 0), f32)] if direct else [],
         "backward_ffn",
-    )
-    grad_word, grad_places, edge_first, grad_taps, wide_first = run(
-        backward_heads,
-        (seg_split, lengths),
-        [
-            (words_in, each(act)),
+        seqs,
+        46,
+    )
+    names = ["m0", "d0", "m1", "d1", "d2"]
+    sizes = tuple(lax.axis_size(a) for a in names)
+
+    def near(x):
+        x = x.reshape(tuple(lax.axis_size(a) for a in ALL) + x.shape[1:])
+        x = jnp.transpose(x, [ALL.index(a) for a in names] + list(range(5, x.ndim)))
+        for dim, axis in enumerate(names):
+            for bit in range(bits_of(axis)):
+                lead, tail = x.shape[:dim], x.shape[dim + 1 :]
+                y = x.reshape(lead + (x.shape[dim] >> (bit + 1), 2, 1 << bit) + tail)
+                flipped = jnp.flip(y, axis=dim + 1)
+                x = jnp.where(bit_of(axis, bit) == 1, flipped, y).reshape(x.shape)
+        return x
+
+    def by_device(x):
+        x = x.reshape(mp_count, -1, dp_count, rest, width)
+        return jnp.transpose(x, (2, 0, 1, 3, 4)).reshape(devices, -1, width)
+
+    tracks = (["d0", "m1", "d1", "d2"], ["m1", "d0", "d1", "d2"])
+
+    def pair_of(kept, sent):
+        x = kept + swap(sent, "m0", 0)
+        x = x.reshape(sizes[1:] + x.shape[1:])
+        return [x[..., : width // 2], x[..., width // 2 :]]
+
+    def fold_stage(pair, stage):
+        done = []
+        for x, track in zip(pair, tracks):
+            left = [a for a in names[1:] if a not in track[:stage]]
+            done.append(fold_near(x, track[stage], left.index(track[stage])))
+        return done
+
+    loss_row = jnp.pad(jnp.reshape(mlm_part + sop_part, (1, 1)), ((0, 0), (0, width - 1)))
+    late = jnp.concatenate([edge_last, grad_pair, loss_row])
+    late = jnp.pad(late, ((0, 16 - late.shape[0]), (0, 0)))
+    seat_rows = slot.reshape(seqs, 1, length)
+    seat_count = (devices * capacity, width)
+    ways = wide(3, share + 8)
+
+    def heads_call(start, sums, back):
+        last = start == seqs - 1
+        some = [
+            (words_in, each(act, start)),
             (places, fixed(places.shape)),
             (edge, fixed(edge.shape)),
             (taps_span, fixed(taps_span.shape)),
             (first_units, fixed(first_units.shape)),
-            (qkv, each((length, 3 * width))),
-            (lse, each((length, 128))),
-            (grad_heads, each(act)),
-            (sum_one, each(act)),
-        ],
-        [
-            (((seqs,) + act, f32), each(act)),
-            ((act, f32), fixed(act)),
+            (qkv, each((length, 3 * width), start)),
+            (lse, each((length, 128), start)),
+            (back, each(act, start)),
+            (sum_one, each(act, start)),
+            (seat_rows, each((1, length), start)),
+            (late, fixed(late.shape)),
+        ]
+        count = len(some)
+        outs = [
+            (((1,) + act, f32), each(act)),
             ((edge.shape, f32), fixed(edge.shape)),
             ((taps_span.shape, f32), fixed(taps_span.shape)),
-            ((first_units.shape, f32), fixed(first_units.shape)),
-        ],
-        [pltpu.VMEM((length + 16, span), f32)] * 2,
-        20 * flop,
-        "backward_heads",
-    )
-    grad_taps = jnp.concatenate(
-        [grad_taps[:, (h - FIRST) * DH : (h - FIRST + 1) * DH] for h in CONV], axis=1
-    )
-    grad_word = grad_word.reshape(tokens, width)
-
-    words = return_round(mine, served, grad_word)
+            ((seat_count, bf16 if last else f32), fixed(seat_count)),
+        ]
+        scratch = [pltpu.VMEM((length + 16, span), f32)] * 2
+        kept_whole = [0, 1, 3, 4]
+        if direct and last:
+            outs += wide_outs(3, share + 8)
+            scratch.append(pltpu.VMEM(ways, f32))
+            kept_whole = [0, 1]
+        else:
+            outs.append(((ways, f32), fixed(ways)))
+        if not direct:
+            outs.append(((act, f32), fixed(act)))
+        return run(
+            partial(backward_heads, start, last, direct),
+            (seg_split, lengths, me),
+            some + [(x, fixed(x.shape)) for x in sums],
+            outs,
+            scratch,
+            "backward_heads",
+            1,
+            33,
+            {count + i: 1 + i for i in range(len(sums)) if i in kept_whole},
+        )
+
+    if not direct:
+        wide_last = near(by_device(wide_last[0])).reshape(2, devices // 2, -1, width)
+    pair_last = pair_of(*wide_last)
+    back = grad_heads
+    grad_words, sums = [], []
+    for start in range(seqs):
+        if start == 1:
+            back, *pair_last = together(back, *pair_last)
+            pair_last = fold_stage(pair_last, 0)
+        word, *sums = heads_call(start, sums, back)
+        grad_words.append(word.reshape(length, width))
+    if seqs == 1:
+        pair_last = fold_stage(pair_last, 0)
+    edge_first, grad_taps, sent, *wide_first = sums
+    if not direct:
+        rows = jnp.pad(wide_first[1], ((0, share * devices - length), (0, 0)))
+        tops = jnp.pad(grad_taps, ((0, 0), (0, width - span)))
+        small_rows = jnp.concatenate([edge_first + late[:8], late[8:11], tops])
+        small_rows = jnp.pad(small_rows, ((0, devices - small_rows.shape[0]), (0, 0)))
+        small_rows = jnp.pad(small_rows[:, None], ((0, 0), (0, 7), (0, 0)))
+        rows = rows.reshape(devices, share, width)
+        wide_first = near(
+            jnp.concatenate([by_device(wide_first[0]), rows, small_rows], axis=1)
+        ).reshape(2, devices // 2, -1, width)
+
+    sent, a, b, *pair_last = together(sent, *wide_first, *pair_last)
+    wide_first = [a, b]
+    words = dot_left(served, lax.all_to_all(sent, ALL, 0, 0, tiled=True))
 
     def return_more(state):
-        _, mine_r, served_r, _ = fetch(state[0])
-        return (state[0] + 1, state[1] + return_round(mine_r, served_r, grad_word))
-
+        _, _, mine_r, served_r, _ = fetch(state[0], hooks=(same, same))
+        live = (state[0] > 0).astype(f32)
+        sent_r = sum(
+            select_sum(mine_r[at * length : (at + 1) * length], g * live)
+            for at, g in enumerate(grad_words)
+        ).astype(bf16)
+        got = lax.all_to_all(sent_r, ALL, 0, 0, tiled=True)
+        return (state[0] + 1, state[1] + dot_left(served_r, got))
+
+    grad_table, *pair_first = together(grad_table, *pair_of(*wide_first))
+    pair_last = fold_stage(pair_last, 1)
+    pair_first = fold_stage(pair_first, 0)
+    pair_last = fold_stage(pair_last, 2)
+    pair_first = fold_stage(pair_first, 1)
     _, words = lax.while_loop(more, return_more, (jnp.int32(1), words))
     grad_table_own = grad_table + words
-
-    def reduce_units(x, axes):
-        many = x.shape[1]
-        x = x.reshape(2, 2, many, dp_count, rest, width)
-        dims = {"mh": 0, "ml": 1}
-        for axis in axes:
-            if axis in dims:
-                x = fold(x, axis, 0, dims.pop(axis))
-                dims = {name: 0 for name in dims}
-            else:
-                where = x.ndim - 3
-                lead = x.shape[:where]
-                if axis == "dl":
-                    x = x.reshape(lead + (x.shape[where] // 2, 2) + x.shape[-2:])
-                    x = fold(x, "dl", 0, where + 1)
-                else:
-                    for bit in reversed(range(bits_of("dh"))):
-                        x = x.reshape(lead + (2, x.shape[where] // 2) + x.shape[-2:])
-                        x = fold(x, "dh", bit, where)
-        return x.reshape(many, rest, width)
-
-    pieces_last = lax.psum_scatter(
-        wide_last.reshape(-1, width), MP, scatter_dimension=0, tiled=True
-    )
-    pieces_last = jnp.moveaxis(pieces_last.reshape(-1, dp_count, rest, width), 1, 0)
-    pieces_last = lax.psum_scatter(
-        pieces_last.reshape(-1, width), DP, scatter_dimension=0, tiled=True
-    ).reshape(-1, rest, width)
-    pieces_first = reduce_units(wide_first, ("ml", "dl", "mh", "dh"))
-    summed = jnp.concatenate([pieces_first, pieces_last])
+    square = jnp.sum(grad_table_own * grad_table_own)
+    square, *pair_first = together(square, *pair_first)
+    pair_last = fold_stage(pair_last, 3)
+    pair_first = fold_stage(pair_first, 2)
+    pair_first = fold_stage(pair_first, 3)
+    piece_first = jnp.concatenate(pair_first, axis=-1)
+    pieces_last = jnp.concatenate(pair_last, axis=-1)
+    summed = jnp.concatenate([piece_first[: 3 * rest], pieces_last]).reshape(-1, rest, width)
     seat = (slot_index[None, :] == jnp.arange(dp_count * cap_slots)[:, None]).astype(f32)
     slotted = sum(seat[:, k, None, None] * summed[k][None] for k in range(matrices))
     slotted = slotted.reshape(dp_count, cap_slots, rest, width)
     grad_slots = lax.all_to_all(slotted, DP, 0, 0, tiled=True)
     grad_slots = jnp.moveaxis(grad_slots, 0, 1).reshape(cap_slots, part, width)
 
-    edge_sum = edge_first + edge_last
-    same = devices // 2
-    half = fold(grad_places.reshape(2, length // 2, width), "ml", 0, 0)
-    piece = -(-(length // 2) // same)
-    half = jnp.pad(half, ((0, piece * same - length // 2), (0, 0)))
-    got = lax.all_to_all(half.reshape(same, piece, width), CHIPS, 0, 0, tiled=True)
-    places_own = jnp.sum(got, axis=0)
-    places_half = everyone(places_own, CHIPS).reshape(same * piece, width)[: length // 2]
-    other = swap(places_half, "ml", 0)
-    low_first = lax.axis_index("ml") == 0
-    places_sum = jnp.concatenate(
-        [jnp.where(low_first, places_half, other), jnp.where(low_first, other, places_half)]
-    )
-    misc = jnp.concatenate(
-        [
-            edge_sum.reshape(-1),
-            grad_small_sop[8 + length :].reshape(-1),
-            grad_taps.reshape(-1),
-            jnp.reshape(mlm_part + sop_part, (1,)),
-        ]
-    )
-    size = misc.shape[0]
-    lane = -(-size // (devices * 128)) * 128
-    misc = jnp.pad(misc, (0, devices * lane - size)).reshape(devices, lane)
-    misc_own = jnp.sum(lax.all_to_all(misc, ALL, 0, 0, tiled=True), axis=0)
-    misc = everyone(misc_own, ALL).reshape(-1)
-    ends = (small.shape[0] - length) * width
-    ends_sum = misc[:ends].reshape(-1, width)
-    small_sum = jnp.concatenate([ends_sum[:6], places_sum, ends_sum[6:]])
-    taps_sum = misc[ends : size - 1].reshape(taps.shape)
-    loss = misc[size - 1]
+    lone_row = piece_first[3 * rest + share]
+    loss_at = lax.axis_index(ALL) == 10
     square = (
-        jnp.sum(grad_table_own * grad_table_own)
-        + jnp.sum(grad_slots * grad_slots)
-        + jnp.sum(places_own * places_own)
-        + (jnp.sum(ends_sum * ends_sum) + jnp.sum(taps_sum * taps_sum)) / devices
-    )
-    squares = everyone(jnp.full((128,), square, f32), ALL)
-    grad_norm = jnp.sqrt(jnp.sum(squares[:, 0]))
+        square
+        + jnp.sum(summed * summed)
+        + jnp.sum(piece_first[3 * rest : 3 * rest + share] ** 2)
+        + jnp.where(loss_at, 0.0, jnp.sum(lone_row * lone_row))
+    )
+    row = jnp.arange(share + 8)[:, None] == share + 1
+    pieces = jnp.where(row, square, piece_first[3 * rest :])
+    for axis in ("d2", "d1", "d0"):
+        pieces = spread_axis(pieces, axis, {"d2": 0, "d1": 1, "d0": 2}[axis])
+    for axis in ("m1", "m0"):
+        pieces = spread_axis(pieces, axis, {"m1": 3, "m0": 4}[axis])
+    pieces = pieces.reshape(devices, share + 8, width)
+    place_sum = pieces[:, :share].reshape(-1, width)[:length]
+    lone = pieces[:, share]
+    small_sum = jnp.concatenate([lone[:6], place_sum, lone[6:10]])
+    taps_rows = lone[11 : 11 + taps.shape[0], :span]
+    taps_sum = jnp.concatenate(
+        [taps_rows[:, (h - FIRST) * DH : (h - FIRST + 1) * DH] for h in CONV], axis=1
+    )
+    loss = lone[10, 0]
+    grad_norm = jnp.sqrt(jnp.sum(pieces[:, share + 1, 0]))
     scale = clip_bound / jnp.maximum(grad_norm, clip_bound)
     count = step_count[0].astype(f32)
     table_new, table_m_new, table_v_new = adam(
@@ -864,7 +1082,7 @@
 
 def solution(mesh):
     dp, mp = mesh.devices.shape
-    fine = Mesh(mesh.devices.reshape(dp // 2, 2, mp // 2, 2), ALL)
+    fine = Mesh(mesh.devices.reshape(dp // 4, 2, 2, mp // 2, 2), ALL)
     rows = P(DP)
     vocab = P(ALL)
     slots = P(DP, MP)

time: 919 us -> 758 us (0.82)
  waiting for transfers between devices: 456 us -> 252 us
  starting transfers between devices: 54.2 us -> 77.4 us
  Pallas kernels: 136 us -> 158 us
  other arithmetic: 94.5 us -> 113 us
  between operations: 40.3 us -> 25.5 us
  local copies, waits for them, and re-layouts: 46.2 us -> 59.9 us
  blocking collectives: 12.5 us -> 0 us
  matrix products: 64.6 us -> 54.6 us
    all_to_all x8 -> x3, waiting for transfers between devices: 122 us -> 6.05 us  [the longest x1 6.05 us: body(): got_slots = lax.all_to_all(low_slots, DP, 0, 0, tiled=True)]
    ppermute x18 -> x46, waiting for transfers between devices: 256 us -> 200 us  [swap(): return lax.ppermute(x, axis, [(i, i ^ 1 << bit) for i in range(count)])]
    ppermute x18 -> x46, starting transfers between devices: 10.7 us -> 54 us  [swap(): return lax.ppermute(x, axis, [(i, i ^ 1 << bit) for i in range(count)])]
    pallas_call x4 -> x5, Pallas kernels: 136 us -> 158 us  [run(): pl.pallas_call(kernel, out_shape=[jax.ShapeDtypeStruct(shape, dtype) for...]
    all_to_all x8 -> x3, starting transfers between devices: 35.3 us -> 15.1 us  [the longest x1 7.25 us: body(): got_slots = lax.all_to_all(low_slots, DP, 0, 0, tiled=True)]
    all_gather x2 -> x1, waiting for transfers between devices: 53.6 us -> 33.7 us  [after_slots(): shards = lax.all_gather(picked, DP, axis=0)]
    slice x11 -> x26, local copies, waits for them, and re-layouts: 5.18 us -> 17.8 us  [the longest x2 6.17 us: body(): place_sum = pieces[:, :share].reshape(-1, width)[:length]]
    all_to_all x1 -> x0, blocking collectives: 12.5 us -> none  [everyone(): lax.all_to_all(jnp.broadcast_to(x, (count,) + x.shape), axes, 0, 0, tiled...]
  transfers between devices with their start and end apart: 34 -> 55, of which waited for: 20 -> 30; matrix products, arithmetic and copies ran while one was open for 14% -> 19% of each run, Pallas kernels for 10% -> 21%
where the time goes in v3:
time: 758 us; the launch traced here: 748 us
  waiting for transfers between devices  252 us (33%)
  Pallas kernels  158 us (21%)
  other arithmetic  113 us (15%)
  starting transfers between devices  77.4 us (10%)
  local copies, waits for them, and re-layouts  59.9 us (8%)
  matrix products  54.6 us (7%)
  between operations  25.5 us (3%)
    ppermute x46, waiting for transfers between devices, swap(): return lax.ppermute(x, axis, [(i, i ^ 1 << bit) for i in range(count)])  200 us
    pallas_call x5, Pallas kernels, run(): pl.pallas_call(kernel, out_shape=[jax.ShapeDtypeStruct(shape, dtype) for...  158 us
    ppermute x46, starting transfers between devices, swap(): return lax.ppermute(x, axis, [(i, i ^ 1 << bit) for i in range(count)])  54 us
    all_gather x1, waiting for transfers between devices, after_slots(): shards = lax.all_gather(picked, DP, axis=0)  33.7 us
    dot_general x3, matrix products, dot_plain(): lax.dot_general(left, right, (((1,), (0,)), ((), ())), preferred_element_...  21.2 us
    dot_general x2, matrix products, dot_left(): lax.dot_general(left, right, (((0,), (0,)), ((), ())), preferred_element_...  16.5 us
    dot_general x1, matrix products, dot_right(): lax.dot_general(left, right, (((1,), (1,)), ((), ())), preferred_element_...  16.3 us
  transfers between devices with their start and end apart: 55, of which 30 were waited for; matrix products, arithmetic and copies ran while one was open for 19% of the time, Pallas kernels for 21%

profile of v3, /device:TPU:0, one launch (start us, length us, event | category | flops | bytes accessed | tf_op | source)
XLA Modules:
  0.0 747.5 jit_solution(16923184586302227553)
XLA Ops:
  16.8 7.3 all-to-all-start.4
  33.9 6.0 all-to-all-done.4
  49.3 6.0 all-to-all-done.5
  60.5 33.7 %all-gather.9.cloned.1.call-done = bf16[64,24,768]{2,1,0:T(8,128)(2,1)} async-done(((bf16[8,24,768]{2,1,0:T(8,128)(2,1)}), bf16[64,24,768]{2,1,0:T(8,128)(2,1)}) %all-gather.9.cloned.1.call-update) | async-done | bytes 2359312 | tf_op jit(solution)/shard_map/all_gather | solution.py:720
  110.3 64.1 %collective-permute-done = bf16[1,5,192,768]{3,2,1,0:T(8,128)(2,1)} collective-permute-done((bf16[1,5,192,768]{3,2,1,0:T(8,128)(2,1)S(1)}, bf16[1,5,192,768]{3,2,1,0:T(8,128)(2,1)}, u32[]{:S(2)}, u32[]{:S(2)}) %collective-permute-start) | collective-permute-done | bytes 1474592 | tf_op jit(solution)/shard_map/ppermute | solution.py:85
  178.0 5.2 fusion.49
  183.2 7.2 while.27
  191.1 20.7 %forward_heads.1 = (f32[2,512,768]{2,1,0:T(8,128)}, bf16[2,512,2304]{2,1,0:T(8,128)(2,1)}, f32[2,512,128]{2,1,0:T(8,128)}, bf16[2,512,768]{2,1,0:T(8,128)(2,1)}) custom-call(s32[2]{0:T(128)} %dynamic_slice.25.split_ref.refs_0_, s32[2]{0:T(128)} %dynamic_slice.26.length_ref.refs_1_, bf16[2,512,768]{2,1,0:T(8,128)(2,1)} %bitcast.335, ...), custom_call_target="tpu_custom_call" | custom-call | flops 23000000512 | bytes 1048576 | tf_op jit(solution)/shard_map/forward_heads/pallas_call | solution.py:579
  217.6 22.8 %forward_ffn.1 = (f32[2,512,768]{2,1,0:T(8,128)}, f32[2,512,768]{2,1,0:T(8,128)}, bf16[2,80,768]{2,1,0:T(8,128)(2,1)}, f32[2,8,768]{2,1,0:T(8,128)}) custom-call(s32[2,80,1]{2,1,0:T(8,128)} %copy.149.pos_ref, bf16[2,512,768]{2,1,0:T(8,128)(2,1)} %get-tuple-element.454.heads_ref, f32[2,512,768]{2,1,0:T(8,128)} %get-tuple-element.455.emb_ref, ...), custom_call_target="tpu_custom_call" | custom-call | flops 26449999872 | bytes 1048576 | tf_op jit(solution)/shard_map/forward_ffn/pallas_call | solution.py:579
  263.4 16.3 %fusion.157 = (f32[1280]{0:T(1024)S(1)}, f32[1280,3840]{1,0:T(8,128)}) fusion(bf16[3840,768]{1,0:T(8,128)(2,1)} %all-gather.7.cloned.1.call-done, bf16[384,768]{1,0:T(8,128)(2,1)S(1)} %bitcast.320, bf16[448,768]{1,0:T(8,128)(2,1)S(1)} %bitcast.314, bf16[448,768]{1,0:T(8,128)(2,1)S(1)} %bitcast.316), kind=kOutput, calls=%fused_computation.429 | convolution fusion | flops 7560559616 | bytes 27530240 | tf_op jit(solution)/shard_map/dot_general | solution.py:42
  279.7 10.7 %exponential_reduce_fusion = (f32[1280]{0:T(1024)S(1)}, f32[1280]{0:T(1024)S(1)}) fusion(f32[1280,3840]{1,0:T(8,128)} %get-tuple-element.651, f32[1280]{0:T(1024)S(1)} %get-tuple-element.650, pred[1280]{0:T(1024)(128)(4,1)S(1)} %fusion.109, s32[1280]{0:T(1024)S(1)} %fusion.94), kind=kLoop, calls=%fused_computation.76 | loop fusion | flops 29488640 | bytes 19682560 | tf_op jit(solution)/shard_map/reduce_sum | solution.py:820
  304.8 12.2 %multiply_convert_fusion = bf16[1280,3840]{1,0:T(8,128)(2,1)S(1)} fusion(f32[1280,3840]{1,0:T(8,128)} %get-tuple-element.651, f32[1280]{0:T(1024)S(1)} %get-tuple-element.580, s32[1280]{0:T(1024)S(1)} %fusion.94, pred[1280]{0:T(1024)(128)(4,1)S(1)} %fusion.109), kind=kLoop, calls=%fused_computation.73 | loop fusion | flops 34406400 | bytes 29502720 | tf_op jit(solution)/shard_map/convert_element_type | solution.py:828
  317.0 10.9 %fusion.159 = f32[1280,768]{1,0:T(8,128)S(1)} fusion(bf16[1280,3840]{1,0:T(8,128)(2,1)S(1)} %multiply_convert_fusion, bf16[3840,768]{1,0:T(8,128)(2,1)} %all-gather.7.cloned.1.call-done), kind=kOutput, calls=%fused_computation.431 | convolution fusion | flops 7549747200 | bytes 19660800 | tf_op jit(solution)/shard_map/dot_general | solution.py:50
  332.2 12.1 %collective-permute-done.16 = f32[4,48,768]{2,1,0:T(8,128)S(1)} collective-permute-done((f32[4,48,768]{2,1,0:T(8,128)S(1)}, f32[4,48,768]{2,1,0:T(8,128)S(1)}, u32[]{:S(2)}, u32[]{:S(2)}) %collective-permute-start.16) | collective-permute-done | bytes 589856 | tf_op jit(solution)/shard_map/ppermute | solution.py:85
  349.7 10.8 %fusion.56 = f32[3840,768]{1,0:T(8,128)} fusion(bf16[1280,3840]{1,0:T(8,128)(2,1)S(1)} %multiply_convert_fusion, bf16[384,768]{1,0:T(8,128)(2,1)S(1)} %bitcast.321, bf16[448,768]{1,0:T(8,128)(2,1)S(1)} %bitcast.315, bf16[448,768]{1,0:T(8,128)(2,1)S(1)} %bitcast.317), kind=kOutput, calls=%fused_computation.131 | convolution fusion | flops 7555645440 | bytes 23592960 | tf_op jit(solution)/shard_map/dot_general | solution.py:46
  377.3 47.9 %backward_ffn.1 = (f32[2,512,768]{2,1,0:T(8,128)}, bf16[2,512,768]{2,1,0:T(8,128)(2,1)}, f32[8,768]{1,0:T(8,128)}, f32[16,120,768]{2,1,0:T(8,128)}, f32[16,120,768]{2,1,0:T(8,128)}) custom-call(s32[1]{0:T(128)} %bitcast.39.me_ref.refs_2_, s32[2,80,1]{2,1,0:T(8,128)} %copy.149.pos_ref, f32[2,80,768]{2,1,0:T(8,128)} %bitcast.323, f32[2,8,768]{2,1,0:T(8,128)} %pad.33.cls_ref, ...), custom_call_target="tpu_custom_call" | custom-call | flops 52899999744 | bytes 1048576 | tf_op jit(solution)/shard_map/backward_ffn/pallas_call | solution.py:579
  432.2 30.5 %backward_heads.2 = (f32[1,512,768]{2,1,0:T(8,128)S(1)}, f32[8,768]{1,0:T(8,128)}, f32[9,512]{1,0:T(8,128)}, f32[1280,768]{1,0:T(8,128)}, f32[32,96,768]{2,1,0:T(8,128)}) custom-call(s32[2]{0:T(128)} %dynamic_slice.25.split_ref.refs_0_, s32[2]{0:T(128)} %dynamic_slice.26.length_ref.refs_1_, s32[1]{0:T(128)} %bitcast.39.me_ref.refs_2_, ...), custom_call_target="tpu_custom_call" | custom-call | flops 37950001152 | bytes 1048576 | tf_op jit(solution)/shard_map/backward_heads/pallas_call | solution.py:579
  462.7 5.1 add.751
  472.0 36.3 %backward_heads.3 = (f32[1,512,768]{2,1,0:T(8,128)}, f32[8,768]{1,0:T(8,128)}, f32[9,512]{1,0:T(8,128)}, bf16[1280,768]{1,0:T(8,128)(2,1)}, f32[16,96,768]{2,1,0:T(8,128)}, /*index=5*/f32[16,96,768]{2,1,0:T(8,128)}) custom-call(s32[2]{0:T(128)} %dynamic_slice.25.split_ref.refs_0_, ...), custom_call_target="tpu_custom_call", output_to_operand_aliasing={{1}: (14, {}), {2}: (15, {})} | custom-call | flops 37950001152 | bytes 1048576 | tf_op jit(solution)/shard_map/backward_heads/pallas_call | solution.py:579
  525.0 29.5 %collective-permute-done.38 = f32[1,2,2,120,384]{4,3,2,1,0:T(8,128)} collective-permute-done((f32[1,2,2,120,384]{4,3,2,1,0:T(8,128)}, f32[1,2,2,120,384]{4,3,2,1,0:T(8,128)}, u32[]{:S(2)}, u32[]{:S(2)}) %collective-permute-start.38) | collective-permute-done | bytes 737312 | tf_op jit(solution)/shard_map/ppermute | solution.py:85
  560.2 13.9 %collective-permute-done.39 = f32[1,2,120,384]{3,2,1,0:T(8,128)S(1)} collective-permute-done((f32[1,2,120,384]{3,2,1,0:T(8,128)S(1)}, f32[1,2,120,384]{3,2,1,0:T(8,128)S(1)}, u32[]{:S(2)}, u32[]{:S(2)}) %collective-permute-start.39) | collective-permute-done | bytes 368672 | tf_op jit(solution)/shard_map/ppermute | solution.py:85
  591.4 5.7 fusion.39
  597.1 14.1 %collective-permute-done.27 = f32[1,2,2,2,96,384]{5,4,3,2,1,0:T(8,128)S(1)} collective-permute-done((f32[1,2,2,2,96,384]{5,4,3,2,1,0:T(8,128)}, f32[1,2,2,2,96,384]{5,4,3,2,1,0:T(8,128)S(1)}, u32[]{:S(2)}, u32[]{:S(2)}) %collective-permute-start.27) | collective-permute-done | bytes 1179680 | tf_op jit(solution)/shard_map/ppermute | solution.py:85
  619.5 5.7 multiply_reduce_fusion
  636.9 7.1 collective-permute-done.31
  650.0 6.2 collective-permute-done.32
  662.5 5.6 collective-permute-done.41
  668.2 5.1 collective-permute-done.42
  673.5 6.7 collective-permute-done.43
  681.6 9.2 %collective-permute-done.44 = f32[2,2,2,1,24,768]{5,4,0,1,2,3:T(8,128)S(1)} collective-permute-done((f32[2,2,2,1,24,768]{5,4,0,1,2,3:T(8,128)S(1)}, f32[2,2,2,1,24,768]{5,4,0,1,2,3:T(8,128)S(1)}, u32[]{:S(2)}, u32[]{:S(2)}) %collective-permute-start.44) | collective-permute-done | bytes 589856 | tf_op jit(solution)/shard_map/ppermute | solution.py:85
  716.4 6.9 fusion.148
  723.3 6.3 all-to-all-done.8
  (473 shorter events, 234.3 us)
Async XLA Ops:
  16.8 23.1 %all-to-all-start.4 = ((bf16[8,2,24,768]{3,2,1,0:T(8,128)(2,1)}), bf16[8,2,24,768]{3,2,1,0:T(8,128)(2,1)S(1)}, u32[]{:S(2)}, u32[]{:S(2)}) async-start(bf16[8,2,24,768]{3,2,1,0:T(8,128)(2,1)} %copy.145), calls=%async_computation.4 | async-start | bytes 1179648 | tf_op jit(solution)/shard_map/all_to_all | solution.py:690
  24.1 70.1 %all-gather.9.cloned.1.call-start = ((), (), s32[]{:S(2)}) async-start(), calls=%async_computation.13 | async-start | bytes 2654208 | tf_op jit(solution)/shard_map/all_gather | solution.py:720
  47.9 143.2 %all-gather.5.cloned.1.call-start = ((), (), s32[]{:S(2)}) async-start(), calls=%async_computation.10 | async-start | bytes 4423680 | tf_op jit(solution)/shard_map/all_gather | solution.py:733
  96.4 81.5 %all-to-all-start.6 = ((bf16[32,40,768]{2,1,0:T(8,128)(2,1)}), bf16[32,40,768]{2,1,0:T(8,128)(2,1)}, u32[]{:S(2)}, u32[]{:S(2)}) async-start(bf16[32,40,768]{2,1,0:T(8,128)(2,1)} %bitcast.303), calls=%async_computation.6 | async-start | bytes 3932160 | tf_op jit(solution)/shard_map/all_to_all | solution.py:630
  100.0 163.4 %all-gather.7.cloned.1.call-start = ((), (), s32[]{:S(2)}) async-start(), calls=%async_computation.11 | async-start | bytes 7372800 | tf_op jit(solution)/shard_map/all_gather | solution.py:735
  100.3 74.1 %collective-permute-start = (bf16[1,5,192,768]{3,2,1,0:T(8,128)(2,1)S(1)}, bf16[1,5,192,768]{3,2,1,0:T(8,128)(2,1)}, u32[]{:S(2)}, u32[]{:S(2)}) collective-permute-start(bf16[1,5,192,768]{3,2,1,0:T(8,128)(2,1)S(1)} %bitcast.292), channel_id=1, source_target_pairs={{0,2},{2,0},{1,3},{3,1},{4,6},{6,4},{5,7},{7,5},{8,10},{10,8},{9,1... | collective-permute-start | bytes 4423688 | tf_op jit(solution)/shard_map/ppermute | solution.py:85
  102.0 480.0 %reduce-scatter.2.cloned.1.call-start = ((), (), s32[]{:S(2)}) async-start(), calls=%async_computation.12 | async-start | bytes 14745600 | tf_op jit(solution)/shard_map/reduce_scatter | solution.py:837
  190.4 21.4 %collective-permute-start.1 = (bf16[2,1,5,192,768]{4,3,2,0,1:T(8,128)(2,1)}, bf16[2,1,5,192,768]{4,3,2,0,1:T(8,128)(2,1)}, u32[]{:S(2)}, u32[]{:S(2)}) collective-permute-start(bf16[2,1,5,192,768]{4,3,2,0,1:T(8,128)(2,1)} %bitcast.284), channel_id=1, source_target_pairs={{0,1},{1,0},{2,3},{3,2},{4,5},{5,4},{6,7},{7,6},{8,9},{9,8},{10,11... | collective-permute-start | bytes 8847368 | tf_op jit(solution)/shard_map/ppermute | solution.py:85
  328.2 16.2 %collective-permute-start.14 = (f32[4,56,768]{2,1,0:T(8,128)S(1)}, f32[4,56,768]{2,1,0:T(8,128)S(1)}, u32[]{:S(2)}, u32[]{:S(2)}) collective-permute-start(f32[4,56,768]{2,1,0:T(8,128)S(1)} %bitcast.319), channel_id=1, source_target_pairs={{0,2},{2,0},{1,3},{3,1},{4,6},{6,4},{5,7},{7,5},{8,10},{10,8},{9,1... | collective-permute-start | bytes 2064392 | tf_op jit(solution)/shard_map/ppermute | solution.py:85
  330.0 14.5 %collective-permute-start.15 = (f32[4,56,768]{2,1,0:T(8,128)S(1)}, f32[4,56,768]{2,1,0:T(8,128)S(1)}, u32[]{:S(2)}, u32[]{:S(2)}) collective-permute-start(f32[4,56,768]{2,1,0:T(8,128)S(1)} %bitcast.318), channel_id=1, source_target_pairs={{0,8},{8,0},{1,9},{9,1},{2,10},{10,2},{3,11},{11,3},{4,12},{12,4},... | collective-permute-start | bytes 2064392 | tf_op jit(solution)/shard_map/ppermute | solution.py:85
  332.1 12.2 %collective-permute-start.16 = (f32[4,48,768]{2,1,0:T(8,128)S(1)}, f32[4,48,768]{2,1,0:T(8,128)S(1)}, u32[]{:S(2)}, u32[]{:S(2)}) collective-permute-start(f32[4,48,768]{2,1,0:T(8,128)S(1)} %bitcast.322), channel_id=1, source_target_pairs={{0,4},{4,0},{1,5},{5,1},{2,6},{6,2},{3,7},{7,3},{8,12},{12,8},{9,1... | collective-permute-start | bytes 1769480 | tf_op jit(solution)/shard_map/ppermute | solution.py:85
  345.4 15.1 %collective-permute-start.21 = (f32[2,48,768]{2,1,0:T(8,128)}, f32[2,48,768]{2,1,0:T(8,128)}, u32[]{:S(2)}, u32[]{:S(2)}) collective-permute-start(f32[2,48,768]{2,1,0:T(8,128)} %slice.554), channel_id=1, source_target_pairs={{0,8},{8,0},{1,9},{9,1},{2,10},{10,2},{3,11},{11,3},{4,12},{12,4},... | collective-permute-start | bytes 884744 | tf_op jit(solution)/shard_map/ppermute | solution.py:85
  347.7 14.7 %collective-permute-start.19 = (f32[2,56,768]{2,1,0:T(8,128)}, f32[2,56,768]{2,1,0:T(8,128)}, u32[]{:S(2)}, u32[]{:S(2)}) collective-permute-start(f32[2,56,768]{2,1,0:T(8,128)} %slice.550), channel_id=1, source_target_pairs={{0,2},{2,0},{1,3},{3,1},{4,6},{6,4},{5,7},{7,5},{8,10},{10,8},{9,1... | collective-permute-start | bytes 1032200 | tf_op jit(solution)/shard_map/ppermute | solution.py:85
  348.7 16.8 %collective-permute-start.17 = (f32[2,56,768]{2,1,0:T(8,128)}, f32[2,56,768]{2,1,0:T(8,128)}, u32[]{:S(2)}, u32[]{:S(2)}) collective-permute-start(f32[2,56,768]{2,1,0:T(8,128)} %slice.546), channel_id=1, source_target_pairs={{0,4},{4,0},{1,5},{5,1},{2,6},{6,2},{3,7},{7,3},{8,12},{12,8},{9,1... | collective-permute-start | bytes 1032200 | tf_op jit(solution)/shard_map/ppermute | solution.py:85
  425.2 37.5 %collective-permute-start.23 = (f32[16,120,768]{2,1,0:T(8,128)}, f32[16,120,768]{2,1,0:T(8,128)}, u32[]{:S(2)}, u32[]{:S(2)}) collective-permute-start(f32[16,120,768]{2,1,0:T(8,128)} %get-tuple-element.471), channel_id=1, source_target_pairs={{0,1},{1,0},{2,3},{3,2},{4,5},{5,4},{6,7},{7,6},{8,9},{9,8},{10,11... | collective-permute-start | bytes 17694728 | tf_op jit(solution)/shard_map/ppermute | solution.py:85
  468.5 39.8 %collective-permute-start.24 = (f32[1,2,2,2,120,384]{5,4,3,2,1,0:T(8,128)S(1)}, f32[1,2,2,2,120,384]{5,4,3,2,1,0:T(8,128)}, u32[]{:S(2)}, u32[]{:S(2)}) collective-permute-start(f32[1,2,2,2,120,384]{5,4,3,2,1,0:T(8,128)S(1)} %slice.566), channel_id=1, source_target_pairs={{0,4},{4,0},{1,5},{5,1},{2,6},{6,2},{3,7},{7,3},{8,12},{12,8},{9,1... | collective-permute-start | bytes 4423688 | tf_op jit(solution)/shard_map/ppermute | solution.py:85
  471.4 39.0 %collective-permute-start.25 = (f32[2,1,2,2,120,384]{5,4,3,2,0,1:T(8,128)}, f32[2,1,2,2,120,384]{5,4,3,2,0,1:T(8,128)}, u32[]{:S(2)}, u32[]{:S(2)}) collective-permute-start(f32[2,1,2,2,120,384]{5,4,3,2,0,1:T(8,128)} %slice_bitcast_fusion), channel_id=1, source_target_pairs={{0,2},{2,0},{1,3},{3,1},{4,6},{6,4},{5,7},{7,5},{8,10},{10,8},{9,1... | collective-permute-start | bytes 4423688 | tf_op jit(solution)/shard_map/ppermute | solution.py:85
  513.6 61.2 %collective-permute-start.26 = (f32[16,96,768]{2,1,0:T(8,128)}, f32[16,96,768]{2,1,0:T(8,128)}, u32[]{:S(2)}, u32[]{:S(2)}) collective-permute-start(f32[16,96,768]{2,1,0:T(8,128)} %get-tuple-element.485), channel_id=1, source_target_pairs={{0,1},{1,0},{2,3},{3,2},{4,5},{5,4},{6,7},{7,6},{8,9},{9,8},{10,11... | collective-permute-start | bytes 14155784 | tf_op jit(solution)/shard_map/ppermute | solution.py:85
  513.8 77.5 %all-to-all-start.7 = ((bf16[32,40,768]{2,1,0:T(8,128)(2,1)}), bf16[32,40,768]{2,1,0:T(8,128)(2,1)}, u32[]{:S(2)}, u32[]{:S(2)}) async-start(bf16[32,40,768]{2,1,0:T(8,128)(2,1)} %bitcast.304), calls=%async_computation.8 | async-start | bytes 3932160 | tf_op jit(solution)/shard_map/all_to_all | solution.py:994
  520.1 34.4 %collective-permute-start.38 = (f32[1,2,2,120,384]{4,3,2,1,0:T(8,128)}, f32[1,2,2,120,384]{4,3,2,1,0:T(8,128)}, u32[]{:S(2)}, u32[]{:S(2)}) collective-permute-start(f32[1,2,2,120,384]{4,3,2,1,0:T(8,128)} %slice.595), channel_id=1, source_target_pairs={{0,4},{4,0},{1,5},{5,1},{2,6},{6,2},{3,7},{7,3},{8,12},{12,8},{9,1... | collective-permute-start | bytes 2211848 | tf_op jit(solution)/shard_map/ppermute | solution.py:85
  522.9 33.8 %collective-permute-start.35 = (f32[1,2,2,120,384]{4,3,2,1,0:T(8,128)}, f32[1,2,2,120,384]{4,3,2,1,0:T(8,128)}, u32[]{:S(2)}, u32[]{:S(2)}) collective-permute-start(f32[1,2,2,120,384]{4,3,2,1,0:T(8,128)} %slice.589), channel_id=1, source_target_pairs={{0,2},{2,0},{1,3},{3,1},{4,6},{6,4},{5,7},{7,5},{8,10},{10,8},{9,1... | collective-permute-start | bytes 2211848 | tf_op jit(solution)/shard_map/ppermute | solution.py:85
  556.0 18.0 %collective-permute-start.39 = (f32[1,2,120,384]{3,2,1,0:T(8,128)S(1)}, f32[1,2,120,384]{3,2,1,0:T(8,128)S(1)}, u32[]{:S(2)}, u32[]{:S(2)}) collective-permute-start(f32[1,2,120,384]{3,2,1,0:T(8,128)S(1)} %slice_bitcast_fusion.8), channel_id=1, source_target_pairs={{0,8},{8,0},{1,9},{9,1},{2,10},{10,2},{3,11},{11,3},{4,12},{12,4},... | collective-permute-start | bytes 1105928 | tf_op jit(solution)/shard_map/ppermute | solution.py:85
  558.8 25.9 %collective-permute-start.36 = (f32[1,2,120,384]{3,2,1,0:T(8,128)}, f32[1,2,120,384]{3,2,1,0:T(8,128)}, u32[]{:S(2)}, u32[]{:S(2)}) collective-permute-start(f32[1,2,120,384]{3,2,1,0:T(8,128)} %slice_bitcast_fusion.10), channel_id=1, source_target_pairs={{0,8},{8,0},{1,9},{9,1},{2,10},{10,2},{3,11},{11,3},{4,12},{12,4},... | collective-permute-start | bytes 1105928 | tf_op jit(solution)/shard_map/ppermute | solution.py:85
  574.8 60.1 %collective-permute-start.40 = (f32[1,120,384]{2,1,0:T(8,128)}, f32[1,120,384]{2,1,0:T(8,128)}, u32[]{:S(2)}, u32[]{:S(2)}) collective-permute-start(f32[1,120,384]{2,1,0:T(8,128)} %slice_bitcast_fusion.12), channel_id=1, source_target_pairs={{0,16},{16,0},{1,17},{17,1},{2,18},{18,2},{3,19},{19,3},{4,20},{20... | collective-permute-start | bytes 552968 | tf_op jit(solution)/shard_map/ppermute | solution.py:85
  584.6 26.6 %collective-permute-start.27 = (f32[1,2,2,2,96,384]{5,4,3,2,1,0:T(8,128)}, f32[1,2,2,2,96,384]{5,4,3,2,1,0:T(8,128)S(1)}, u32[]{:S(2)}, u32[]{:S(2)}) collective-permute-start(f32[1,2,2,2,96,384]{5,4,3,2,1,0:T(8,128)} %slice.572), channel_id=1, source_target_pairs={{0,4},{4,0},{1,5},{5,1},{2,6},{6,2},{3,7},{7,3},{8,12},{12,8},{9,1... | collective-permute-start | bytes 3538952 | tf_op jit(solution)/shard_map/ppermute | solution.py:85
  586.9 27.5 %collective-permute-start.29 = (f32[2,1,2,2,96,384]{5,4,3,2,0,1:T(8,128)}, f32[2,1,2,2,96,384]{5,4,3,2,0,1:T(8,128)}, u32[]{:S(2)}, u32[]{:S(2)}) collective-permute-start(f32[2,1,2,2,96,384]{5,4,3,2,0,1:T(8,128)} %slice_bitcast_fusion.2), channel_id=1, source_target_pairs={{0,2},{2,0},{1,3},{3,1},{4,6},{6,4},{5,7},{7,5},{8,10},{10,8},{9,1... | collective-permute-start | bytes 3538952 | tf_op jit(solution)/shard_map/ppermute | solution.py:85
  588.9 46.9 %collective-permute-start.37 = (f32[1,120,384]{2,1,0:T(8,128)}, f32[1,120,384]{2,1,0:T(8,128)}, u32[]{:S(2)}, u32[]{:S(2)}) collective-permute-start(f32[1,120,384]{2,1,0:T(8,128)} %slice_bitcast_fusion.14), channel_id=1, source_target_pairs={{0,16},{16,0},{1,17},{17,1},{2,18},{18,2},{3,19},{19,3},{4,20},{20... | collective-permute-start | bytes 552968 | tf_op jit(solution)/shard_map/ppermute | solution.py:85
  612.3 14.8 %collective-permute-start.28 = (f32[1,2,2,96,384]{4,3,2,1,0:T(8,128)}, f32[1,2,2,96,384]{4,3,2,1,0:T(8,128)}, u32[]{:S(2)}, u32[]{:S(2)}) collective-permute-start(f32[1,2,2,96,384]{4,3,2,1,0:T(8,128)} %slice_bitcast_fusion.6), channel_id=1, source_target_pairs={{0,2},{2,0},{1,3},{3,1},{4,6},{6,4},{5,7},{7,5},{8,10},{10,8},{9,1... | collective-permute-start | bytes 1769480 | tf_op jit(solution)/shard_map/ppermute | solution.py:85
  617.0 14.1 %collective-permute-start.30 = (f32[1,2,2,96,384]{4,3,2,1,0:T(8,128)}, f32[1,2,2,96,384]{4,3,2,1,0:T(8,128)}, u32[]{:S(2)}, u32[]{:S(2)}) collective-permute-start(f32[1,2,2,96,384]{4,3,2,1,0:T(8,128)} %slice_bitcast_fusion.4), channel_id=1, source_target_pairs={{0,4},{4,0},{1,5},{5,1},{2,6},{6,2},{3,7},{7,3},{8,12},{12,8},{9,1... | collective-permute-start | bytes 1769480 | tf_op jit(solution)/shard_map/ppermute | solution.py:85
  632.3 11.7 %collective-permute-start.31 = (f32[1,2,96,384]{3,2,1,0:T(8,128)S(1)}, f32[1,2,96,384]{3,2,1,0:T(8,128)S(1)}, u32[]{:S(2)}, u32[]{:S(2)}) collective-permute-start(f32[1,2,96,384]{3,2,1,0:T(8,128)S(1)} %slice.580), channel_id=1, source_target_pairs={{0,8},{8,0},{1,9},{9,1},{2,10},{10,2},{3,11},{11,3},{4,12},{12,4},... | collective-permute-start | bytes 884744 | tf_op jit(solution)/shard_map/ppermute | solution.py:85
  644.2 12.0 %collective-permute-start.32 = (f32[1,96,384]{2,1,0:T(8,128)S(1)}, f32[1,96,384]{2,1,0:T(8,128)S(1)}, u32[]{:S(2)}, u32[]{:S(2)}) collective-permute-start(f32[1,96,384]{2,1,0:T(8,128)S(1)} %slice_bitcast_fusion.18), channel_id=1, source_target_pairs={{0,16},{16,0},{1,17},{17,1},{2,18},{18,2},{3,19},{19,3},{4,20},{20... | collective-permute-start | bytes 442376 | tf_op jit(solution)/shard_map/ppermute | solution.py:85
  695.5 34.0 %all-to-all-start.8 = ((f32[8,2,24,768]{3,2,1,0:T(8,128)}), f32[8,2,24,768]{3,2,1,0:T(8,128)}, u32[]{:S(2)}, u32[]{:S(2)}) async-start(f32[8,2,24,768]{3,2,1,0:T(8,128)} %multiply_add_fusion.2), calls=%async_computation.9 | async-start | bytes 2359296 | tf_op jit(solution)/shard_map/all_to_all | solution.py:1024
  (86 other events, 810.3 us)
Sparse Core Ops, SparseCore 0:
  43.0 51.1 all-gather.8
  96.5 66.3 all-gather.4
  165.1 75.7 all-gather.6
  373.1 183.7 reduce-scatter.1

commit v4 on v3

--- a/solution.py
+++ b/solution.py
@@ -97,13 +97,16 @@
     return (lax.axis_index(axis) >> bit) & 1
 
 
-def fold_near(x, axis, dim):
+def fold_near(x, axis, dim, beside=()):
     for bit in reversed(range(bits_of(axis))):
         lead, rest = x.shape[:dim], x.shape[dim + 1 :]
         x = x.reshape(lead + (2, x.shape[dim] // 2) + rest)
         sent = lax.index_in_dim(x, 1, dim, False)
-        x = lax.index_in_dim(x, 0, dim, False) + swap(sent, axis, bit)
-    return x.reshape(x.shape[:dim] + x.shape[dim + 1 :])
+        kept = lax.index_in_dim(x, 0, dim, False)
+        if beside:
+            kept, *beside = together(kept, *beside)
+        x = kept + swap(sent, axis, bit)
+    return (x.reshape(x.shape[:dim] + x.shape[dim + 1 :]), *beside)
 
 
 def slot_of(d, m, high):
@@ -264,9 +267,8 @@
     embedded = normed * edge_ref[0:1, :] + edge_ref[3:4, :]
     emb_ref[0] = embedded
     low_in = embedded.astype(bf16)
-    part = units_ref.shape[2]
     for k in range(3):
-        unit = units_ref[:, k].reshape(width, width)
+        unit = whole_unit(units_ref, k)
         qkv_ref[0, :, k * width : (k + 1) * width] = dot_right(low_in, unit).astype(bf16)
     allowed = lax.broadcasted_iota(i32, (length, length), 1) < length_ref[at]
     lanes = lax.broadcasted_iota(i32, (length, 128), 1)
@@ -304,15 +306,21 @@
 
 
 def ffn_weights(units_ref, s, first):
-    return jnp.concatenate([units_ref[s, first], units_ref[s, first + 1]], axis=0)
+    at = units_ref.at[s % 2, s // 2]
+    return jnp.concatenate([at[first], at[first + 1]], axis=0)
+
+
+def whole_unit(units_ref, k):
+    count = units_ref.shape[0] * units_ref.shape[1]
+    return jnp.concatenate([units_ref[s % 2, s // 2, k] for s in range(count)], axis=0)
 
 
 def forward_ffn(
     pos_ref, heads_ref, emb_ref, edge_ref, units_ref, one_ref, two_ref, mask_ref, cls_ref
 ):
     length, width = emb_ref.shape[1:]
-    mp_count, part = units_ref.shape[0], units_ref.shape[2]
-    unit = units_ref[:, 0].reshape(width, width)
+    part = units_ref.shape[3]
+    unit = whole_unit(units_ref, 0)
     projected = dot_right(heads_ref[0], unit).astype(bf16).astype(f32)
     one = emb_ref[0] + projected
     one_ref[0] = one
@@ -365,7 +373,7 @@
     at = pl.program_id(0)
     wide_ref = wide_refs[-1]
     length, width = one_ref.shape[1:]
-    mp_count, part = units_ref.shape[0], units_ref.shape[2]
+    mp_count, part = units_ref.shape[0] * units_ref.shape[1], units_ref.shape[3]
 
     @pl.when(at == 0)
     def _():
@@ -417,7 +425,7 @@
     w = dot_left(low_one, heads_ref[0])
     for s in range(mp_count):
         add_rows(wide_ref, me_ref[0], mp_count, s, 0, w[s * part : (s + 1) * part])
-    unit = units_ref[:, 0].reshape(width, width)
+    unit = whole_unit(units_ref, 0)
     back_ref[0] = dot_plain(low_one, unit).astype(bf16)
 
     if len(wide_refs) > 1:
@@ -446,7 +454,7 @@
         wide_ref = sums[3]
     at = pl.program_id(0) + start
     me = me_ref[0]
-    mp_count = units_ref.shape[0]
+    mp_count = units_ref.shape[0] * units_ref.shape[1]
     length, width = word_ref.shape[1:]
     for n, new in enumerate(sums):
         if n != 2:
@@ -527,10 +535,10 @@
     for n in range(3):
         g = jnp.concatenate(pieces[n], axis=1)
         w = dot_left(g, low_in)
-        part = units_ref.shape[2]
+        part = units_ref.shape[3]
         for s in range(mp_count):
             add_rows(wide_ref, me, mp_count, s, n, w[s * part : (s + 1) * part])
-        grad = grad + dot_plain(g, units_ref[:, n].reshape(width, width))
+        grad = grad + dot_plain(g, whole_unit(units_ref, n))
     gedge_ref[0:1, :] += down(grad * normed)
     gedge_ref[3:4, :] += down(grad)
     grad = norm_grad(grad, normed, inv, edge_ref[0:1, :])
@@ -565,6 +573,50 @@
             wide_ref[slot, base + share : base + share + 1, 0 : row.shape[1]] = row
         kept_ref[...] = wide_ref[: devices // 2]
         sent_ref[...] = wide_ref[devices // 2 :]
+
+
+def near_logits(words_ref, masked_ref, label_ref):
+    logits = dot_right(words_ref[...], masked_ref[...])
+    row = lax.broadcasted_iota(i32, logits.shape, 0) + pl.program_id(0) * logits.shape[0]
+    return logits, row == label_ref[...]
+
+
+def head_stats(masked_ref, label_ref, words_ref, stats_ref):
+    logits, target = near_logits(words_ref, masked_ref, label_ref)
+    top = jnp.max(logits, axis=0, keepdims=True)
+    here = jnp.sum(jnp.where(target, logits, 0.0), axis=0, keepdims=True)
+
+    @pl.when(pl.program_id(0) == 0)
+    def _():
+        stats_ref[...] = jnp.zeros_like(stats_ref)
+        stats_ref[0:1, :] = top
+        stats_ref[1:2, :] = jnp.sum(jnp.exp(logits - top), axis=0, keepdims=True)
+        stats_ref[2:3, :] = here
+
+    @pl.when(pl.program_id(0) > 0)
+    def _():
+        old = stats_ref[0:1, :]
+        new = jnp.maximum(old, top)
+        total = jnp.sum(jnp.exp(logits - new), axis=0, keepdims=True)
+        stats_ref[1:2, :] = stats_ref[1:2, :] * jnp.exp(old - new) + total
+        stats_ref[0:1, :] = new
+        stats_ref[2:3, :] += here
+
+
+def head_grads(share, masked_ref, label_ref, log_ref, words_ref, back_ref, table_ref):
+    logits, target = near_logits(words_ref, masked_ref, label_ref)
+    probs = jnp.exp(logits - log_ref[...])
+    grad = ((probs - jnp.where(target, 1.0, 0.0)) * share).astype(bf16)
+    table_ref[...] = dot_plain(grad, masked_ref[...])
+    back = dot_left(grad, words_ref[...])
+
+    @pl.when(pl.program_id(0) == 0)
+    def _():
+        back_ref[...] = back
+
+    @pl.when(pl.program_id(0) > 0)
+    def _():
+        back_ref[...] += back
 
 
 def fixed(shape):
@@ -730,9 +782,12 @@
     all_labels = near_labels(beside[:, 1 : 1 + own], own)
 
     shards = jnp.moveaxis(shards, 0, 1).reshape(matrices, part, width)
-    first_units = lax.all_gather(shards[:3], MP, axis=0)
-    last_units = spread_axis(shards[3:], "m1", 0)
-    vocab = lax.all_gather(low_table, RG, axis=0, tiled=True)
+    first_units, last_units, late_table = together(
+        spread_axis(shards[:3], "m1", 0), shards[3:], low_table
+    )
+    first_units = spread_axis(first_units, "m0", 0)
+    last_units = spread_axis(last_units, "m1", 0)
+    vocab = lax.all_gather(late_table, RG, axis=0, tiled=True)
 
     def more(state):
         return state[0] < turns
@@ -741,8 +796,7 @@
         return (state[0] + 1, state[1] + fetch(state[0], hooks=(same, same))[0])
 
     _, word_rows = lax.while_loop(more, fetch_more, (jnp.int32(1), word_rows))
-    word_rows, last_units = together(word_rows, last_units)
-    last_units = spread_axis(last_units, "m0", 1).reshape(mp_count, -1, part, width)
+    last_units = spread_axis(last_units, "m0", 0)
 
     words_in = word_rows.reshape(seqs, length, width)
     places = small[6 : 6 + length]
@@ -801,8 +855,15 @@
     )
     masked_rows = masked_rows.reshape(seqs * masks, width)
 
-    all_masked = grow_parts(masked_rows)
-    logits = dot_right(all_masked, vocab)
+    sop_part, sop_pull = jax.vjp(
+        partial(sop_loss, labels=sop_labels, denom=total_seqs),
+        cls_rows[:, 0],
+        small[8 + length :],
+    )
+    grad_cls, grad_pair = sop_pull(jnp.ones((), f32))
+    all_masked, sop_part, grad_cls, grad_pair = together(
+        grow_parts(masked_rows), sop_part, grad_cls, grad_pair
+    )
     block = all_labels // vblock
     at = {}
     for axis in ALL[::-1]:
@@ -813,34 +874,47 @@
         label_mine = jnp.logical_and(label_mine, at[axis] == lax.axis_index(axis))
     label_block = at["d2"] * lax.axis_size("m0") + at["m0"]
     label_row = label_block * vblock + all_labels % vblock
-    onehot = jnp.logical_and(
-        jnp.arange(vocab.shape[0])[None, :] == label_row[:, None], label_mine[:, None]
-    )
-    top = jnp.max(logits, axis=1)
-    total = jnp.sum(jnp.exp(logits - top[:, None]), axis=1)
-    target = jnp.sum(jnp.where(onehot, logits, 0.0), axis=1)
-    stats = merge_stats(jnp.stack([top, total, target]), own)
+    label_row = jnp.where(label_mine, label_row, -1)[None]
+    tall = vocab.shape[0]
+    tile = next(t for t in (768, 640, 512, 384, 256, 128, 64, 32, 16, 8) if tall % t == 0)
+    tiles = pl.BlockSpec((tile, width), lambda b, *_: (b, 0))
+    rows_shape = (1 << 3, all_masked.shape[0])
+    head_ins = [
+        (all_masked, fixed(all_masked.shape)),
+        (label_row, fixed(label_row.shape)),
+    ]
+    (stats,) = run(
+        head_stats,
+        (),
+        head_ins + [(vocab, tiles)],
+        [((rows_shape, f32), fixed(rows_shape))],
+        [],
+        "head_stats",
+        tall // tile,
+        13,
+    )
+    stats = merge_stats(stats[:3], own)
     log_sum = stats[0] + jnp.log(stats[1])
     losses = [p[0] for p in cut_parts(log_sum - stats[2], own)]
     mlm_part = sum(jnp.sum(p) for p in losses) / count_all
-    grad_logits = (
-        (jnp.exp(logits - log_sum[:, None]) - onehot.astype(f32)) / count_all
-    ).astype(bf16)
-    parts = cut_parts(dot_plain(grad_logits, vocab), own)
+    grad_rows, grad_table = run(
+        partial(head_grads, 1.0 / count_all),
+        (),
+        head_ins + [(log_sum[None], fixed(label_row.shape)), (vocab, tiles)],
+        [
+            ((all_masked.shape, f32), fixed(all_masked.shape)),
+            ((vocab.shape, f32), tiles),
+        ],
+        [],
+        "head_grads",
+        tall // tile,
+        26,
+    )
+    parts = cut_parts(grad_rows, own)
     for stage in reversed(range(len(VG))):
         parts = [shrink(p, order[stage]) for p, order in zip(parts, ORDERS)]
-        if stage == len(VG) - 1:
-            grad_logits, *parts = together(grad_logits, *parts)
-            grad_table = dot_left(grad_logits, all_masked)
-    grad_masked = jnp.concatenate([p[0] for p in parts])
-    grad_masked, grad_table = together(grad_masked, grad_table)
+    grad_masked, mlm_part = together(jnp.concatenate([p[0] for p in parts]), mlm_part)
     grad_table = lax.psum_scatter(grad_table, RG, scatter_dimension=0, tiled=True)
-    sop_part, sop_pull = jax.vjp(
-        partial(sop_loss, labels=sop_labels, denom=total_seqs),
-        cls_rows[:, 0],
-        small[8 + length :],
-    )
-    grad_cls, grad_pair = sop_pull(jnp.ones((), f32))
     grad_cls = jnp.pad(grad_cls[:, None], ((0, 0), (0, 7), (0, 0)))
     direct = rest % 8 == 0 and length % (8 * devices) == 0 and devices >= 20
     share = length // devices if direct else -(-length // devices)
@@ -906,12 +980,13 @@
         x = x.reshape(sizes[1:] + x.shape[1:])
         return [x[..., : width // 2], x[..., width // 2 :]]
 
-    def fold_stage(pair, stage):
+    def fold_stage(pair, stage, beside=()):
         done = []
         for x, track in zip(pair, tracks):
             left = [a for a in names[1:] if a not in track[:stage]]
-            done.append(fold_near(x, track[stage], left.index(track[stage])))
-        return done
+            x, *beside = fold_near(x, track[stage], left.index(track[stage]), beside)
+            done.append(x)
+        return [*done, *beside]
 
     loss_row = jnp.pad(jnp.reshape(mlm_part + sop_part, (1, 1)), ((0, 0), (0, width - 1)))
     late = jnp.concatenate([edge_last, grad_pair, loss_row])
@@ -933,7 +1008,7 @@
             (back, each(act, start)),
             (sum_one, each(act, start)),
             (seat_rows, each((1, length), start)),
-            (late, fixed(late.shape)),
+            (late if last else jnp.zeros_like(late), fixed(late.shape)),
         ]
         count = len(some)
         outs = [
@@ -991,7 +1066,7 @@
 
     sent, a, b, *pair_last = together(sent, *wide_first, *pair_last)
     wide_first = [a, b]
-    words = dot_left(served, lax.all_to_all(sent, ALL, 0, 0, tiled=True))
+    got_words = lax.all_to_all(sent, ALL, 0, 0, tiled=True)
 
     def return_more(state):
         _, _, mine_r, served_r, _ = fetch(state[0], hooks=(same, same))
@@ -1003,9 +1078,9 @@
         got = lax.all_to_all(sent_r, ALL, 0, 0, tiled=True)
         return (state[0] + 1, state[1] + dot_left(served_r, got))
 
-    grad_table, *pair_first = together(grad_table, *pair_of(*wide_first))
-    pair_last = fold_stage(pair_last, 1)
-    pair_first = fold_stage(pair_first, 0)
+    *pair_last, a, b = fold_stage(pair_last, 1, pair_of(*wide_first))
+    grad_table, seen, *pair_first = together(grad_table, served, *fold_stage([a, b], 0))
+    words = dot_left(seen, got_words)
     pair_last = fold_stage(pair_last, 2)
     pair_first = fold_stage(pair_first, 1)
     _, words = lax.while_loop(more, return_more, (jnp.int32(1), words))
@@ -1036,6 +1111,7 @@
     pieces = jnp.where(row, square, piece_first[3 * rest :])
     for axis in ("d2", "d1", "d0"):
         pieces = spread_axis(pieces, axis, {"d2": 0, "d1": 1, "d0": 2}[axis])
+    pieces, grad_slots = together(pieces, grad_slots)
     for axis in ("m1", "m0"):
         pieces = spread_axis(pieces, axis, {"m1": 3, "m0": 4}[axis])
     pieces = pieces.reshape(devices, share + 8, width)

time: 758 us -> 734 us (0.968)
  Pallas kernels: 158 us -> 201 us
  matrix products: 54.6 us -> 16.8 us
  other arithmetic: 113 us -> 91.8 us
    pallas_call x5 -> x7, Pallas kernels: 158 us -> 201 us  [run(): pl.pallas_call(kernel, out_shape=[jax.ShapeDtypeStruct(shape, dtype) for...]
    dot_general x1 -> x0, matrix products: 16.3 us -> none  [dot_right(): lax.dot_general(left, right, (((1,), (1,)), ((), ())), preferred_element_...]
    dot_general x3 -> x2, matrix products: 21.2 us -> 10.2 us  [dot_plain(): lax.dot_general(left, right, (((1,), (0,)), ((), ())), preferred_element_...]
    reduce_sum x1 -> x0, other arithmetic: 10.7 us -> none  [body(): total = jnp.sum(jnp.exp(logits - top[:, None]), axis=1)]
    dot_general x2 -> x1, matrix products: 16.5 us -> 6.07 us  [dot_left(): lax.dot_general(left, right, (((0,), (0,)), ((), ())), preferred_element_...]
    convert_element_type x1, other arithmetic: 12.2 us -> 1.98 us  [fetch_round(): (asked[:, None] == jnp.arange(low_table.shape[0])[None, :]).astype(bf16)]
    ppermute x46 -> x48, waiting for transfers between devices: 200 us -> 201 us  [swap(): return lax.ppermute(x, axis, [(i, i ^ 1 << bit) for i in range(count)])]
    ppermute x46 -> x48, starting transfers between devices: 54 us -> 53.7 us  [swap(): return lax.ppermute(x, axis, [(i, i ^ 1 << bit) for i in range(count)])]
  transfers between devices with their start and end apart: 55 -> 56, of which waited for: 30 -> 35; matrix products, arithmetic and copies ran while one was open for 19% -> 15% of each run, Pallas kernels for 21% -> 21%
where the time goes in v4:
time: 734 us; the launch traced here: 725 us
  waiting for transfers between devices  253 us (34%)
  Pallas kernels  201 us (27%)
  other arithmetic  91.8 us (13%)
  starting transfers between devices  77.9 us (11%)
  local copies, waits for them, and re-layouts  57.7 us (8%)
  between operations  25.8 us (4%)
  matrix products  16.8 us (2%)
    pallas_call x7, Pallas kernels, run(): pl.pallas_call(kernel, out_shape=[jax.ShapeDtypeStruct(shape, dtype) for...  201 us
    ppermute x48, waiting for transfers between devices, swap(): return lax.ppermute(x, axis, [(i, i ^ 1 << bit) for i in range(count)])  201 us
    ppermute x48, starting transfers between devices, swap(): return lax.ppermute(x, axis, [(i, i ^ 1 << bit) for i in range(count)])  53.7 us
    all_gather x1, waiting for transfers between devices, after_slots(): shards = lax.all_gather(picked, DP, axis=0)  34.5 us
  transfers between devices with their start and end apart: 56, of which 35 were waited for; matrix products, arithmetic and copies ran while one was open for 15% of the time, Pallas kernels for 21%

profile of v4, /device:TPU:0, one launch (start us, length us, event | category | flops | bytes accessed | tf_op | source)
XLA Modules:
  0.0 724.6 jit_solution(1191723058227538060)
XLA Ops:
  16.3 7.3 %all-to-all-start.4 = ((bf16[8,2,24,768]{3,2,1,0:T(8,128)(2,1)}), bf16[8,2,24,768]{3,2,1,0:T(8,128)(2,1)S(1)}, u32[]{:S(2)}, u32[]{:S(2)}) async-start(bf16[8,2,24,768]{3,2,1,0:T(8,128)(2,1)} %copy.119), calls=%async_computation.4 | async-start | bytes 1179648 | tf_op jit(solution)/shard_map/all_to_all | solution.py:742
  27.2 12.2 %all-to-all-done.4 = bf16[8,2,24,768]{3,2,1,0:T(8,128)(2,1)S(1)} async-done(((bf16[8,2,24,768]{3,2,1,0:T(8,128)(2,1)}), bf16[8,2,24,768]{3,2,1,0:T(8,128)(2,1)S(1)}, u32[]{:S(2)}, u32[]{:S(2)}) %all-to-all-start.4) | async-done | bytes 589856 | tf_op jit(solution)/shard_map/all_to_all | solution.py:742
  47.8 6.0 all-to-all-done.5
  53.9 5.1 fusion.43
  59.0 34.5 %all-gather.6.cloned.1.call-done = bf16[64,24,768]{2,1,0:T(8,128)(2,1)} async-done(((bf16[8,24,768]{2,1,0:T(8,128)(2,1)}), bf16[64,24,768]{2,1,0:T(8,128)(2,1)}) %all-gather.6.cloned.1.call-update) | async-done | bytes 2359312 | tf_op jit(solution)/shard_map/all_gather | solution.py:772
  107.5 24.1 %collective-permute-done = bf16[1,3,192,768]{3,2,1,0:T(8,128)(2,1)S(1)} collective-permute-done((bf16[1,3,192,768]{3,2,1,0:T(8,128)(2,1)S(1)}, bf16[1,3,192,768]{3,2,1,0:T(8,128)(2,1)S(1)}, u32[]{:S(2)}, u32[]{:S(2)}) %collective-permute-start) | collective-permute-done | bytes 884768 | tf_op jit(solution)/shard_map/ppermute | solution.py:85
  139.0 28.8 %collective-permute-done.2 = bf16[1,5,192,768]{3,2,1,0:T(8,128)(2,1)} collective-permute-done((bf16[1,5,192,768]{3,2,1,0:T(8,128)(2,1)S(1)}, bf16[1,5,192,768]{3,2,1,0:T(8,128)(2,1)}, u32[]{:S(2)}, u32[]{:S(2)}) %collective-permute-start.2) | collective-permute-done | bytes 1474592 | tf_op jit(solution)/shard_map/ppermute | solution.py:85
  175.8 5.1 fusion.47
  181.3 20.7 %forward_heads.1 = (f32[2,512,768]{2,1,0:T(8,128)}, bf16[2,512,2304]{2,1,0:T(8,128)(2,1)}, f32[2,512,128]{2,1,0:T(8,128)}, bf16[2,512,768]{2,1,0:T(8,128)(2,1)}) custom-call(s32[2]{0:T(128)} %dynamic_slice.25.split_ref.refs_0_, s32[2]{0:T(128)} %dynamic_slice.26.length_ref.refs_1_, bf16[2,512,768]{2,1,0:T(8,128)(2,1)} %bitcast.306, ...), custom_call_target="tpu_custom_call" | custom-call | flops 23000000512 | bytes 1048576 | tf_op jit(solution)/shard_map/forward_heads/pallas_call | solution.py:631
  207.2 22.9 %forward_ffn.1 = (f32[2,512,768]{2,1,0:T(8,128)}, f32[2,512,768]{2,1,0:T(8,128)}, bf16[2,80,768]{2,1,0:T(8,128)(2,1)}, f32[2,8,768]{2,1,0:T(8,128)}) custom-call(s32[2,80,1]{2,1,0:T(8,128)} %copy.122.pos_ref, bf16[2,512,768]{2,1,0:T(8,128)(2,1)} %get-tuple-element.466.heads_ref, f32[2,512,768]{2,1,0:T(8,128)} %get-tuple-element.467.emb_ref, ...), custom_call_target="tpu_custom_call" | custom-call | flops 26449999872 | bytes 1048576 | tf_op jit(solution)/shard_map/forward_ffn/pallas_call | solution.py:631
  255.8 14.9 %head_stats.1 = f32[8,1280]{1,0:T(8,128)} custom-call(bf16[1280,768]{1,0:T(8,128)(2,1)} %pad_maximum_fusion.3.masked_ref, s32[1,1280]{1,0:T(1,128)} %and_select_fusion.4.label_ref, bf16[3840,768]{1,0:T(8,128)(2,1)} %all-gather.4.cloned.1.call-done.words_ref), custom_call_target="tpu_custom_call" | custom-call | flops 14949999616 | bytes 1048576 | tf_op jit(solution)/shard_map/head_stats/pallas_call | solution.py:631
  287.1 30.4 %head_grads.1 = (f32[1280,768]{1,0:T(8,128)}, f32[3840,768]{1,0:T(8,128)}) custom-call(bf16[1280,768]{1,0:T(8,128)(2,1)} %pad_maximum_fusion.3.masked_ref, s32[1,1280]{1,0:T(1,128)} %and_select_fusion.4.label_ref, f32[1,1280]{1,0:T(1,128)} %get-tuple-element.662.log_ref, bf16[3840,768]{1,0:T(8,128)(2,1)} %all-gather.4.cloned.1.call-done.words_ref), custom_call_target="tpu_custom_call" | custom-call | flops 29899999232 | bytes 1048576 | tf_op jit(solution)/shard_map/head_grads/pallas_call | solution.py:631
  352.0 4.3 collective-permute-done.18
  357.2 45.4 %backward_ffn.1 = (f32[2,512,768]{2,1,0:T(8,128)}, bf16[2,512,768]{2,1,0:T(8,128)(2,1)}, f32[8,768]{1,0:T(8,128)}, f32[16,120,768]{2,1,0:T(8,128)}, f32[16,120,768]{2,1,0:T(8,128)}) custom-call(s32[1]{0:T(128)} %bitcast.33.me_ref.refs_2_, s32[2,80,1]{2,1,0:T(8,128)} %copy.122.pos_ref, f32[2,80,768]{2,1,0:T(8,128)} %bitcast.294, f32[2,8,768]{2,1,0:T(8,128)} %pad.33.cls_ref, ...), custom_call_target="tpu_custom_call" | custom-call | flops 52899999744 | bytes 1048576 | tf_op jit(solution)/shard_map/backward_ffn/pallas_call | solution.py:631
  406.2 30.6 %backward_heads.2 = (f32[1,512,768]{2,1,0:T(8,128)S(1)}, f32[8,768]{1,0:T(8,128)}, f32[9,512]{1,0:T(8,128)}, f32[1280,768]{1,0:T(8,128)}, f32[32,96,768]{2,1,0:T(8,128)}) custom-call(s32[2]{0:T(128)} %dynamic_slice.25.split_ref.refs_0_, s32[2]{0:T(128)} %dynamic_slice.26.length_ref.refs_1_, s32[1]{0:T(128)} %bitcast.33.me_ref.refs_2_, ...), custom_call_target="tpu_custom_call" | custom-call | flops 37950001152 | bytes 1048576 | tf_op jit(solution)/shard_map/backward_heads/pallas_call | solution.py:631
  436.8 5.1 add.778
  445.5 35.9 %backward_heads.3 = (f32[1,512,768]{2,1,0:T(8,128)}, f32[8,768]{1,0:T(8,128)}, f32[9,512]{1,0:T(8,128)}, bf16[1280,768]{1,0:T(8,128)(2,1)}, f32[16,96,768]{2,1,0:T(8,128)}, /*index=5*/f32[16,96,768]{2,1,0:T(8,128)}) custom-call(s32[2]{0:T(128)} %dynamic_slice.25.split_ref.refs_0_, ...), custom_call_target="tpu_custom_call", output_to_operand_aliasing={{1}: (14, {}), {2}: (15, {})} | custom-call | flops 37950001152 | bytes 1048576 | tf_op jit(solution)/shard_map/backward_heads/pallas_call | solution.py:631
  496.1 5.6 all-to-all-start.7
  505.8 4.4 add.784
  510.8 27.4 %collective-permute-done.37 = f32[1,2,2,120,384]{4,3,2,1,0:T(8,128)S(1)} collective-permute-done((f32[1,2,2,120,384]{4,3,2,1,0:T(8,128)S(1)}, f32[1,2,2,120,384]{4,3,2,1,0:T(8,128)S(1)}, u32[]{:S(2)}, u32[]{:S(2)}) %collective-permute-start.37) | collective-permute-done | bytes 737312 | tf_op jit(solution)/shard_map/ppermute | solution.py:85
  544.7 8.9 %collective-permute-done.38 = f32[1,2,120,384]{3,2,1,0:T(8,128)S(1)} collective-permute-done((f32[1,2,120,384]{3,2,1,0:T(8,128)S(1)}, f32[1,2,120,384]{3,2,1,0:T(8,128)S(1)}, u32[]{:S(2)}, u32[]{:S(2)}) %collective-permute-start.38) | collective-permute-done | bytes 368672 | tf_op jit(solution)/shard_map/ppermute | solution.py:85
  555.3 9.6 %collective-permute-done.41 = f32[1,2,120,384]{3,2,1,0:T(8,128)S(1)} collective-permute-done((f32[1,2,120,384]{3,2,1,0:T(8,128)S(1)}, f32[1,2,120,384]{3,2,1,0:T(8,128)S(1)}, u32[]{:S(2)}, u32[]{:S(2)}) %collective-permute-start.41) | collective-permute-done | bytes 368672 | tf_op jit(solution)/shard_map/ppermute | solution.py:85
  577.0 6.1 fusion.138
  583.1 5.7 multiply_reduce_fusion
  594.8 8.4 %collective-permute-done.35 = f32[1,2,96,384]{3,2,1,0:T(8,128)S(1)} collective-permute-done((f32[1,2,96,384]{3,2,1,0:T(8,128)S(1)}, f32[1,2,96,384]{3,2,1,0:T(8,128)S(1)}, u32[]{:S(2)}, u32[]{:S(2)}) %collective-permute-start.35) | collective-permute-done | bytes 294944 | tf_op jit(solution)/shard_map/ppermute | solution.py:85
  610.2 5.3 collective-permute-done.36
  623.9 3.8 all-to-all-start.8
  630.7 28.0 %collective-permute-done.43 = f32[1,24,768]{2,1,0:T(8,128)S(1)} collective-permute-done((f32[1,24,768]{2,1,0:T(8,128)S(1)}, f32[1,24,768]{2,1,0:T(8,128)S(1)}, u32[]{:S(2)}, u32[]{:S(2)}) %collective-permute-start.43) | collective-permute-done | bytes 73760 | tf_op jit(solution)/shard_map/ppermute | solution.py:85
  658.8 5.1 collective-permute-done.44
  665.3 5.5 collective-permute-done.45
  672.8 10.7 %collective-permute-done.46 = f32[2,2,2,1,24,768]{5,4,0,1,2,3:T(8,128)S(1)} collective-permute-done((f32[2,2,2,1,24,768]{5,4,0,1,2,3:T(8,128)S(1)}, f32[2,2,2,1,24,768]{5,4,0,1,2,3:T(8,128)S(1)}, u32[]{:S(2)}, u32[]{:S(2)}) %collective-permute-start.46) | collective-permute-done | bytes 589856 | tf_op jit(solution)/shard_map/ppermute | solution.py:85
  702.0 7.5 %fusion.126 = (bf16[960,768]{1,0:T(8,128)(2,1)}, f32[960,768]{1,0:T(8,128)}, f32[960,768]{1,0:T(8,128)}, f32[960,768]{1,0:T(8,128)}) fusion(f32[960,768]{1,0:T(8,128)S(1)} %copy-done.5, f32[]{:T(128)} %bitcast.89, f32[]{:T(128)} %bitcast.88, f32[960,768]{1,0:T(8,128)} %get-tuple-element.600, f32[]{:T(128)S(6)} %div.216, f32[960,768]{1,0:T(8,128)} %param.34, ...), kind=kLoop, calls=%fused_computation.391 | loop fusion | flops 12533760 | bytes 22118412 | tf_op jit(solution)/shard_map/convert_element_type | solution.py:1145
  (483 shorter events, 223.5 us)
Async XLA Ops:
  16.3 23.2 %all-to-all-start.4 = ((bf16[8,2,24,768]{3,2,1,0:T(8,128)(2,1)}), bf16[8,2,24,768]{3,2,1,0:T(8,128)(2,1)S(1)}, u32[]{:S(2)}, u32[]{:S(2)}) async-start(bf16[8,2,24,768]{3,2,1,0:T(8,128)(2,1)} %copy.119), calls=%async_computation.4 | async-start | bytes 1179648 | tf_op jit(solution)/shard_map/all_to_all | solution.py:742
  23.6 69.9 %all-gather.6.cloned.1.call-start = ((), (), s32[]{:S(2)}) async-start(), calls=%async_computation.12 | async-start | bytes 2654208 | tf_op jit(solution)/shard_map/all_gather | solution.py:772
  94.8 36.8 %collective-permute-start = (bf16[1,3,192,768]{3,2,1,0:T(8,128)(2,1)S(1)}, bf16[1,3,192,768]{3,2,1,0:T(8,128)(2,1)S(1)}, u32[]{:S(2)}, u32[]{:S(2)}) collective-permute-start(bf16[1,3,192,768]{3,2,1,0:T(8,128)(2,1)S(1)} %bitcast.270), channel_id=1, source_target_pairs={{0,2},{2,0},{1,3},{3,1},{4,6},{6,4},{5,7},{7,5},{8,10},{10,8},{9,1... | collective-permute-start | bytes 2654216 | tf_op jit(solution)/shard_map/ppermute | solution.py:85
  97.1 78.6 %all-to-all-start.6 = ((bf16[32,40,768]{2,1,0:T(8,128)(2,1)}), bf16[32,40,768]{2,1,0:T(8,128)(2,1)}, u32[]{:S(2)}, u32[]{:S(2)}) async-start(bf16[32,40,768]{2,1,0:T(8,128)(2,1)} %bitcast.283), calls=%async_computation.6 | async-start | bytes 3932160 | tf_op jit(solution)/shard_map/all_to_all | solution.py:682
  100.7 155.1 %all-gather.4.cloned.1.call-start = ((), (), s32[]{:S(2)}) async-start(), calls=%async_computation.10 | async-start | bytes 7372800 | tf_op jit(solution)/shard_map/all_gather | solution.py:790
  131.9 35.9 %collective-permute-start.2 = (bf16[1,5,192,768]{3,2,1,0:T(8,128)(2,1)S(1)}, bf16[1,5,192,768]{3,2,1,0:T(8,128)(2,1)}, u32[]{:S(2)}, u32[]{:S(2)}) collective-permute-start(bf16[1,5,192,768]{3,2,1,0:T(8,128)(2,1)S(1)} %bitcast.267), channel_id=1, source_target_pairs={{0,2},{2,0},{1,3},{3,1},{4,6},{6,4},{5,7},{7,5},{8,10},{10,8},{9,1... | collective-permute-start | bytes 4423688 | tf_op jit(solution)/shard_map/ppermute | solution.py:85
  134.5 37.5 %collective-permute-start.1 = (bf16[1,2,3,192,768]{4,3,2,1,0:T(8,128)(2,1)S(1)}, bf16[1,2,3,192,768]{4,3,2,1,0:T(8,128)(2,1)}, u32[]{:S(2)}, u32[]{:S(2)}) collective-permute-start(bf16[1,2,3,192,768]{4,3,2,1,0:T(8,128)(2,1)S(1)} %bitcast.265), channel_id=1, source_target_pairs={{0,1},{1,0},{2,3},{3,2},{4,5},{5,4},{6,7},{7,6},{8,9},{9,8},{10,11... | collective-permute-start | bytes 5308424 | tf_op jit(solution)/shard_map/ppermute | solution.py:85
  138.7 433.1 %reduce-scatter.2.cloned.1.call-start = ((), (), s32[]{:S(2)}) async-start(), calls=%async_computation.11 | async-start | bytes 14745600 | tf_op jit(solution)/shard_map/reduce_scatter | solution.py:917
  172.0 30.0 %collective-permute-start.3 = (bf16[1,2,5,192,768]{4,3,2,1,0:T(8,128)(2,1)}, bf16[1,2,5,192,768]{4,3,2,1,0:T(8,128)(2,1)}, u32[]{:S(2)}, u32[]{:S(2)}) collective-permute-start(bf16[1,2,5,192,768]{4,3,2,1,0:T(8,128)(2,1)} %maximum_bitcast_fusion), channel_id=1, source_target_pairs={{0,1},{1,0},{2,3},{3,2},{4,5},{5,4},{6,7},{7,6},{8,9},{9,8},{10,11... | collective-permute-start | bytes 8847368 | tf_op jit(solution)/shard_map/ppermute | solution.py:85
  323.4 14.4 %collective-permute-start.19 = (f32[4,56,768]{2,1,0:T(8,128)}, f32[4,56,768]{2,1,0:T(8,128)}, u32[]{:S(2)}, u32[]{:S(2)}) collective-permute-start(f32[4,56,768]{2,1,0:T(8,128)} %bitcast.38), channel_id=1, source_target_pairs={{0,8},{8,0},{1,9},{9,1},{2,10},{10,2},{3,11},{11,3},{4,12},{12,4},... | collective-permute-start | bytes 2064392 | tf_op jit(solution)/shard_map/ppermute | solution.py:85
  325.0 17.0 %collective-permute-start.16 = (f32[4,56,768]{2,1,0:T(8,128)}, f32[4,56,768]{2,1,0:T(8,128)S(1)}, u32[]{:S(2)}, u32[]{:S(2)}) collective-permute-start(f32[4,56,768]{2,1,0:T(8,128)} %bitcast.35), channel_id=1, source_target_pairs={{0,2},{2,0},{1,3},{3,1},{4,6},{6,4},{5,7},{7,5},{8,10},{10,8},{9,1... | collective-permute-start | bytes 2064392 | tf_op jit(solution)/shard_map/ppermute | solution.py:85
  402.7 34.1 %collective-permute-start.25 = (f32[16,120,768]{2,1,0:T(8,128)}, f32[16,120,768]{2,1,0:T(8,128)}, u32[]{:S(2)}, u32[]{:S(2)}) collective-permute-start(f32[16,120,768]{2,1,0:T(8,128)} %get-tuple-element.483), channel_id=1, source_target_pairs={{0,1},{1,0},{2,3},{3,2},{4,5},{5,4},{6,7},{7,6},{8,9},{9,8},{10,11... | collective-permute-start | bytes 17694728 | tf_op jit(solution)/shard_map/ppermute | solution.py:85
  442.6 38.8 %collective-permute-start.26 = (f32[1,2,2,2,120,384]{5,4,3,2,1,0:T(8,128)S(1)}, f32[1,2,2,2,120,384]{5,4,3,2,1,0:T(8,128)}, u32[]{:S(2)}, u32[]{:S(2)}) collective-permute-start(f32[1,2,2,2,120,384]{5,4,3,2,1,0:T(8,128)S(1)} %slice.591), channel_id=1, source_target_pairs={{0,4},{4,0},{1,5},{5,1},{2,6},{6,2},{3,7},{7,3},{8,12},{12,8},{9,1... | collective-permute-start | bytes 4423688 | tf_op jit(solution)/shard_map/ppermute | solution.py:85
  445.5 38.0 %collective-permute-start.27 = (f32[2,1,2,2,120,384]{5,4,3,2,0,1:T(8,128)}, f32[2,1,2,2,120,384]{5,4,3,2,0,1:T(8,128)}, u32[]{:S(2)}, u32[]{:S(2)}) collective-permute-start(f32[2,1,2,2,120,384]{5,4,3,2,0,1:T(8,128)} %slice_bitcast_fusion), channel_id=1, source_target_pairs={{0,2},{2,0},{1,3},{3,1},{4,6},{6,4},{5,7},{7,5},{8,10},{10,8},{9,1... | collective-permute-start | bytes 4423688 | tf_op jit(solution)/shard_map/ppermute | solution.py:85
  486.8 19.0 %collective-permute-start.28 = (f32[16,96,768]{2,1,0:T(8,128)}, f32[16,96,768]{2,1,0:T(8,128)}, u32[]{:S(2)}, u32[]{:S(2)}) collective-permute-start(f32[16,96,768]{2,1,0:T(8,128)} %get-tuple-element.502), channel_id=1, source_target_pairs={{0,1},{1,0},{2,3},{3,2},{4,5},{5,4},{6,7},{7,6},{8,9},{9,8},{10,11... | collective-permute-start | bytes 14155784 | tf_op jit(solution)/shard_map/ppermute | solution.py:85
  495.9 44.4 %collective-permute-start.40 = (f32[1,2,2,120,384]{4,3,2,1,0:T(8,128)}, f32[1,2,2,120,384]{4,3,2,1,0:T(8,128)}, u32[]{:S(2)}, u32[]{:S(2)}) collective-permute-start(f32[1,2,2,120,384]{4,3,2,1,0:T(8,128)} %get-tuple-element.634), channel_id=1, source_target_pairs={{0,4},{4,0},{1,5},{5,1},{2,6},{6,2},{3,7},{7,3},{8,12},{12,8},{9,1... | collective-permute-start | bytes 2211848 | tf_op jit(solution)/shard_map/ppermute | solution.py:85
  496.1 80.9 %all-to-all-start.7 = ((bf16[32,40,768]{2,1,0:T(8,128)(2,1)}), bf16[32,40,768]{2,1,0:T(8,128)(2,1)}, u32[]{:S(2)}, u32[]{:S(2)}) async-start(bf16[32,40,768]{2,1,0:T(8,128)(2,1)} %bitcast.284), calls=%async_computation.8 | async-start | bytes 3932160 | tf_op jit(solution)/shard_map/all_to_all | solution.py:1069
  501.8 36.3 %collective-permute-start.37 = (f32[1,2,2,120,384]{4,3,2,1,0:T(8,128)S(1)}, f32[1,2,2,120,384]{4,3,2,1,0:T(8,128)S(1)}, u32[]{:S(2)}, u32[]{:S(2)}) collective-permute-start(f32[1,2,2,120,384]{4,3,2,1,0:T(8,128)S(1)} %get-tuple-element.632), channel_id=1, source_target_pairs={{0,2},{2,0},{1,3},{3,1},{4,6},{6,4},{5,7},{7,5},{8,10},{10,8},{9,1... | collective-permute-start | bytes 2211848 | tf_op jit(solution)/shard_map/ppermute | solution.py:85
  538.3 15.4 %collective-permute-start.38 = (f32[1,2,120,384]{3,2,1,0:T(8,128)S(1)}, f32[1,2,120,384]{3,2,1,0:T(8,128)S(1)}, u32[]{:S(2)}, u32[]{:S(2)}) collective-permute-start(f32[1,2,120,384]{3,2,1,0:T(8,128)S(1)} %slice_bitcast_fusion.6), channel_id=1, source_target_pairs={{0,8},{8,0},{1,9},{9,1},{2,10},{10,2},{3,11},{11,3},{4,12},{12,4},... | collective-permute-start | bytes 1105928 | tf_op jit(solution)/shard_map/ppermute | solution.py:85
  541.6 23.3 %collective-permute-start.41 = (f32[1,2,120,384]{3,2,1,0:T(8,128)S(1)}, f32[1,2,120,384]{3,2,1,0:T(8,128)S(1)}, u32[]{:S(2)}, u32[]{:S(2)}) collective-permute-start(f32[1,2,120,384]{3,2,1,0:T(8,128)S(1)} %slice_bitcast_fusion.4), channel_id=1, source_target_pairs={{0,8},{8,0},{1,9},{9,1},{2,10},{10,2},{3,11},{11,3},{4,12},{12,4},... | collective-permute-start | bytes 1105928 | tf_op jit(solution)/shard_map/ppermute | solution.py:85
  541.8 28.0 %collective-permute-start.29 = (f32[1,2,2,2,96,384]{5,4,3,2,1,0:T(8,128)S(1)}, f32[1,2,2,2,96,384]{5,4,3,2,1,0:T(8,128)S(1)}, u32[]{:S(2)}, u32[]{:S(2)}) collective-permute-start(f32[1,2,2,2,96,384]{5,4,3,2,1,0:T(8,128)S(1)} %slice.599), channel_id=1, source_target_pairs={{0,4},{4,0},{1,5},{5,1},{2,6},{6,2},{3,7},{7,3},{8,12},{12,8},{9,1... | collective-permute-start | bytes 3538952 | tf_op jit(solution)/shard_map/ppermute | solution.py:85
  543.9 26.7 %collective-permute-start.30 = (f32[2,1,2,2,96,384]{5,4,3,2,0,1:T(8,128)S(1)}, f32[2,1,2,2,96,384]{5,4,3,2,0,1:T(8,128)S(1)}, u32[]{:S(2)}, u32[]{:S(2)}) collective-permute-start(f32[2,1,2,2,96,384]{5,4,3,2,0,1:T(8,128)S(1)} %slice_bitcast_fusion.2), channel_id=1, source_target_pairs={{0,2},{2,0},{1,3},{3,1},{4,6},{6,4},{5,7},{7,5},{8,10},{10,8},{9,1... | collective-permute-start | bytes 3538952 | tf_op jit(solution)/shard_map/ppermute | solution.py:85
  553.7 12.1 %collective-permute-start.39 = (f32[1,120,384]{2,1,0:T(8,128)S(1)}, f32[1,120,384]{2,1,0:T(8,128)S(1)}, u32[]{:S(2)}, u32[]{:S(2)}) collective-permute-start(f32[1,120,384]{2,1,0:T(8,128)S(1)} %slice_bitcast_fusion.10), channel_id=1, source_target_pairs={{0,16},{16,0},{1,17},{17,1},{2,18},{18,2},{3,19},{19,3},{4,20},{20... | collective-permute-start | bytes 552968 | tf_op jit(solution)/shard_map/ppermute | solution.py:85
  565.7 27.9 %collective-permute-start.42 = (f32[1,120,384]{2,1,0:T(8,128)}, f32[1,120,384]{2,1,0:T(8,128)}, u32[]{:S(2)}, u32[]{:S(2)}) collective-permute-start(f32[1,120,384]{2,1,0:T(8,128)} %slice_bitcast_fusion.8), channel_id=1, source_target_pairs={{0,16},{16,0},{1,17},{17,1},{2,18},{18,2},{3,19},{19,3},{4,20},{20... | collective-permute-start | bytes 552968 | tf_op jit(solution)/shard_map/ppermute | solution.py:85
  574.6 14.4 %collective-permute-start.32 = (f32[1,2,2,96,384]{4,3,2,1,0:T(8,128)}, f32[1,2,2,96,384]{4,3,2,1,0:T(8,128)}, u32[]{:S(2)}, u32[]{:S(2)}) collective-permute-start(f32[1,2,2,96,384]{4,3,2,1,0:T(8,128)} %slice.605), channel_id=1, source_target_pairs={{0,4},{4,0},{1,5},{5,1},{2,6},{6,2},{3,7},{7,3},{8,12},{12,8},{9,1... | collective-permute-start | bytes 1769480 | tf_op jit(solution)/shard_map/ppermute | solution.py:85
  576.4 14.0 %collective-permute-start.31 = (f32[1,2,2,96,384]{4,3,2,1,0:T(8,128)}, f32[1,2,2,96,384]{4,3,2,1,0:T(8,128)}, u32[]{:S(2)}, u32[]{:S(2)}) collective-permute-start(f32[1,2,2,96,384]{4,3,2,1,0:T(8,128)} %slice.603), channel_id=1, source_target_pairs={{0,2},{2,0},{1,3},{3,1},{4,6},{6,4},{5,7},{7,5},{8,10},{10,8},{9,1... | collective-permute-start | bytes 1769480 | tf_op jit(solution)/shard_map/ppermute | solution.py:85
  591.7 11.6 %collective-permute-start.35 = (f32[1,2,96,384]{3,2,1,0:T(8,128)S(1)}, f32[1,2,96,384]{3,2,1,0:T(8,128)S(1)}, u32[]{:S(2)}, u32[]{:S(2)}) collective-permute-start(f32[1,2,96,384]{3,2,1,0:T(8,128)S(1)} %slice.611), channel_id=1, source_target_pairs={{0,8},{8,0},{1,9},{9,1},{2,10},{10,2},{3,11},{11,3},{4,12},{12,4},... | collective-permute-start | bytes 884744 | tf_op jit(solution)/shard_map/ppermute | solution.py:85
  594.7 12.4 %collective-permute-start.33 = (f32[1,2,96,384]{3,2,1,0:T(8,128)S(1)}, f32[1,2,96,384]{3,2,1,0:T(8,128)S(1)}, u32[]{:S(2)}, u32[]{:S(2)}) collective-permute-start(f32[1,2,96,384]{3,2,1,0:T(8,128)S(1)} %slice.607), channel_id=1, source_target_pairs={{0,8},{8,0},{1,9},{9,1},{2,10},{10,2},{3,11},{11,3},{4,12},{12,4},... | collective-permute-start | bytes 884744 | tf_op jit(solution)/shard_map/ppermute | solution.py:85
  603.3 12.2 %collective-permute-start.36 = (f32[1,96,384]{2,1,0:T(8,128)S(1)}, f32[1,96,384]{2,1,0:T(8,128)S(1)}, u32[]{:S(2)}, u32[]{:S(2)}) collective-permute-start(f32[1,96,384]{2,1,0:T(8,128)S(1)} %slice_bitcast_fusion.12), channel_id=1, source_target_pairs={{0,16},{16,0},{1,17},{17,1},{2,18},{18,2},{3,19},{19,3},{4,20},{20... | collective-permute-start | bytes 442376 | tf_op jit(solution)/shard_map/ppermute | solution.py:85
  623.9 47.0 %all-to-all-start.8 = ((f32[8,2,24,768]{3,2,1,0:T(8,128)}), f32[8,2,24,768]{3,2,1,0:T(8,128)S(1)}, u32[]{:S(2)}, u32[]{:S(2)}) async-start(f32[8,2,24,768]{3,2,1,0:T(8,128)} %multiply_add_fusion.3), calls=%async_computation.9 | async-start | bytes 2359296 | tf_op jit(solution)/shard_map/all_to_all | solution.py:1099
  627.7 31.0 %collective-permute-start.43 = (f32[1,24,768]{2,1,0:T(8,128)S(1)}, f32[1,24,768]{2,1,0:T(8,128)S(1)}, u32[]{:S(2)}, u32[]{:S(2)}) collective-permute-start(f32[1,24,768]{2,1,0:T(8,128)S(1)} %get-tuple-element.646), channel_id=1, source_target_pairs={{0,16},{16,0},{1,17},{17,1},{2,18},{18,2},{3,19},{19,3},{4,20},{20... | collective-permute-start | bytes 221192 | tf_op jit(solution)/shard_map/ppermute | solution.py:85
  672.0 11.5 %collective-permute-start.46 = (f32[2,2,2,1,24,768]{5,4,0,1,2,3:T(8,128)S(1)}, f32[2,2,2,1,24,768]{5,4,0,1,2,3:T(8,128)S(1)}, u32[]{:S(2)}, u32[]{:S(2)}) collective-permute-start(f32[2,2,2,1,24,768]{5,4,0,1,2,3:T(8,128)S(1)} %bitcast.277), channel_id=1, source_target_pairs={{0,2},{2,0},{1,3},{3,1},{4,6},{6,4},{5,7},{7,5},{8,10},{10,8},{9,1... | collective-permute-start | bytes 1769480 | tf_op jit(solution)/shard_map/ppermute | solution.py:85
  (92 other events, 875.2 us)
Sparse Core Ops, SparseCore 0:
  42.3 51.1 all-gather.5
  138.9 75.0 all-gather.3
  327.3 156.5 reduce-scatter.1

commit v5 on v4

--- a/solution.py
+++ b/solution.py
@@ -1096,8 +1096,6 @@
     seat = (slot_index[None, :] == jnp.arange(dp_count * cap_slots)[:, None]).astype(f32)
     slotted = sum(seat[:, k, None, None] * summed[k][None] for k in range(matrices))
     slotted = slotted.reshape(dp_count, cap_slots, rest, width)
-    grad_slots = lax.all_to_all(slotted, DP, 0, 0, tiled=True)
-    grad_slots = jnp.moveaxis(grad_slots, 0, 1).reshape(cap_slots, part, width)
 
     lone_row = piece_first[3 * rest + share]
     loss_at = lax.axis_index(ALL) == 10
@@ -1109,11 +1107,13 @@
     )
     row = jnp.arange(share + 8)[:, None] == share + 1
     pieces = jnp.where(row, square, piece_first[3 * rest :])
-    for axis in ("d2", "d1", "d0"):
-        pieces = spread_axis(pieces, axis, {"d2": 0, "d1": 1, "d0": 2}[axis])
+    pieces = spread_axis(spread_axis(pieces, "d2", 0), "d1", 1)
+    pieces, slotted = together(pieces, slotted)
+    grad_slots = lax.all_to_all(slotted, DP, 0, 0, tiled=True)
+    grad_slots = jnp.moveaxis(grad_slots, 0, 1).reshape(cap_slots, part, width)
+    pieces = spread_axis(spread_axis(pieces, "d0", 2), "m1", 3)
     pieces, grad_slots = together(pieces, grad_slots)
-    for axis in ("m1", "m0"):
-        pieces = spread_axis(pieces, axis, {"m1": 3, "m0": 4}[axis])
+    pieces = spread_axis(pieces, "m0", 4)
     pieces = pieces.reshape(devices, share + 8, width)
     place_sum = pieces[:, :share].reshape(-1, width)[:length]
     lone = pieces[:, share]

time: 734 us -> 716 us (0.975)
  waiting for transfers between devices: 253 us -> 237 us
    ppermute x48, waiting for transfers between devices: 201 us -> 184 us  [swap(): return lax.ppermute(x, axis, [(i, i ^ 1 << bit) for i in range(count)])]
  transfers between devices with their start and end apart: 56 -> 56, of which waited for: 35 -> 35; matrix products, arithmetic and copies ran while one was open for 15% -> 15% of each run, Pallas kernels for 21% -> 22%
where the time goes in v5:
time: 716 us; the launch traced here: 706 us
  waiting for transfers between devices  237 us (33%)
  Pallas kernels  201 us (28%)
  other arithmetic  90.8 us (13%)
  starting transfers between devices  77.1 us (11%)
  local copies, waits for them, and re-layouts  57.3 us (8%)
  between operations  25.8 us (4%)
  matrix products  16.8 us (2%)
    pallas_call x7, Pallas kernels, run(): pl.pallas_call(kernel, out_shape=[jax.ShapeDtypeStruct(shape, dtype) for...  201 us
    ppermute x48, waiting for transfers between devices, swap(): return lax.ppermute(x, axis, [(i, i ^ 1 << bit) for i in range(count)])  184 us
    ppermute x48, starting transfers between devices, swap(): return lax.ppermute(x, axis, [(i, i ^ 1 << bit) for i in range(count)])  53.3 us
    all_gather x1, waiting for transfers between devices, after_slots(): shards = lax.all_gather(picked, DP, axis=0)  34.5 us
  transfers between devices with their start and end apart: 56, of which 35 were waited for; matrix products, arithmetic and copies ran while one was open for 15% of the time, Pallas kernels for 22%

profile of v5, /device:TPU:0, one launch (start us, length us, event | category | flops | bytes accessed | tf_op | source)
XLA Modules:
  0.0 706.1 jit_solution(14557929547930502625)
XLA Ops:
  16.3 7.3 %all-to-all-start.4 = ((bf16[8,2,24,768]{3,2,1,0:T(8,128)(2,1)}), bf16[8,2,24,768]{3,2,1,0:T(8,128)(2,1)S(1)}, u32[]{:S(2)}, u32[]{:S(2)}) async-start(bf16[8,2,24,768]{3,2,1,0:T(8,128)(2,1)} %copy.119), calls=%async_computation.4 | async-start | bytes 1179648 | tf_op jit(solution)/shard_map/all_to_all | solution.py:742
  27.2 12.2 %all-to-all-done.4 = bf16[8,2,24,768]{3,2,1,0:T(8,128)(2,1)S(1)} async-done(((bf16[8,2,24,768]{3,2,1,0:T(8,128)(2,1)}), bf16[8,2,24,768]{3,2,1,0:T(8,128)(2,1)S(1)}, u32[]{:S(2)}, u32[]{:S(2)}) %all-to-all-start.4) | async-done | bytes 589856 | tf_op jit(solution)/shard_map/all_to_all | solution.py:742
  42.8 3.7 all-to-all-start.5
  47.8 6.0 all-to-all-done.5
  53.9 5.1 fusion.43
  59.0 34.5 %all-gather.6.cloned.1.call-done = bf16[64,24,768]{2,1,0:T(8,128)(2,1)} async-done(((bf16[8,24,768]{2,1,0:T(8,128)(2,1)}), bf16[64,24,768]{2,1,0:T(8,128)(2,1)}) %all-gather.6.cloned.1.call-update) | async-done | bytes 2359312 | tf_op jit(solution)/shard_map/all_gather | solution.py:772
  107.5 24.1 %collective-permute-done = bf16[1,3,192,768]{3,2,1,0:T(8,128)(2,1)S(1)} collective-permute-done((bf16[1,3,192,768]{3,2,1,0:T(8,128)(2,1)S(1)}, bf16[1,3,192,768]{3,2,1,0:T(8,128)(2,1)S(1)}, u32[]{:S(2)}, u32[]{:S(2)}) %collective-permute-start) | collective-permute-done | bytes 884768 | tf_op jit(solution)/shard_map/ppermute | solution.py:85
  139.0 28.8 %collective-permute-done.2 = bf16[1,5,192,768]{3,2,1,0:T(8,128)(2,1)} collective-permute-done((bf16[1,5,192,768]{3,2,1,0:T(8,128)(2,1)S(1)}, bf16[1,5,192,768]{3,2,1,0:T(8,128)(2,1)}, u32[]{:S(2)}, u32[]{:S(2)}) %collective-permute-start.2) | collective-permute-done | bytes 1474592 | tf_op jit(solution)/shard_map/ppermute | solution.py:85
  175.8 5.1 fusion.47
  181.3 20.7 %forward_heads.1 = (f32[2,512,768]{2,1,0:T(8,128)}, bf16[2,512,2304]{2,1,0:T(8,128)(2,1)}, f32[2,512,128]{2,1,0:T(8,128)}, bf16[2,512,768]{2,1,0:T(8,128)(2,1)}) custom-call(s32[2]{0:T(128)} %dynamic_slice.25.split_ref.refs_0_, s32[2]{0:T(128)} %dynamic_slice.26.length_ref.refs_1_, bf16[2,512,768]{2,1,0:T(8,128)(2,1)} %bitcast.304, ...), custom_call_target="tpu_custom_call" | custom-call | flops 23000000512 | bytes 1048576 | tf_op jit(solution)/shard_map/forward_heads/pallas_call | solution.py:631
  207.2 22.9 %forward_ffn.1 = (f32[2,512,768]{2,1,0:T(8,128)}, f32[2,512,768]{2,1,0:T(8,128)}, bf16[2,80,768]{2,1,0:T(8,128)(2,1)}, f32[2,8,768]{2,1,0:T(8,128)}) custom-call(s32[2,80,1]{2,1,0:T(8,128)} %copy.122.pos_ref, bf16[2,512,768]{2,1,0:T(8,128)(2,1)} %get-tuple-element.468.heads_ref, f32[2,512,768]{2,1,0:T(8,128)} %get-tuple-element.469.emb_ref, ...), custom_call_target="tpu_custom_call" | custom-call | flops 26449999872 | bytes 1048576 | tf_op jit(solution)/shard_map/forward_ffn/pallas_call | solution.py:631
  255.8 14.9 %head_stats.1 = f32[8,1280]{1,0:T(8,128)} custom-call(bf16[1280,768]{1,0:T(8,128)(2,1)} %pad_maximum_fusion.3.masked_ref, s32[1,1280]{1,0:T(1,128)} %and_select_fusion.4.label_ref, bf16[3840,768]{1,0:T(8,128)(2,1)} %all-gather.4.cloned.1.call-done.words_ref), custom_call_target="tpu_custom_call" | custom-call | flops 14949999616 | bytes 1048576 | tf_op jit(solution)/shard_map/head_stats/pallas_call | solution.py:631
  287.1 30.4 %head_grads.1 = (f32[1280,768]{1,0:T(8,128)}, f32[3840,768]{1,0:T(8,128)}) custom-call(bf16[1280,768]{1,0:T(8,128)(2,1)} %pad_maximum_fusion.3.masked_ref, s32[1,1280]{1,0:T(1,128)} %and_select_fusion.4.label_ref, f32[1,1280]{1,0:T(1,128)} %get-tuple-element.666.log_ref, bf16[3840,768]{1,0:T(8,128)(2,1)} %all-gather.4.cloned.1.call-done.words_ref), custom_call_target="tpu_custom_call" | custom-call | flops 29899999232 | bytes 1048576 | tf_op jit(solution)/shard_map/head_grads/pallas_call | solution.py:631
  352.0 4.3 collective-permute-done.18
  357.2 45.4 %backward_ffn.1 = (f32[2,512,768]{2,1,0:T(8,128)}, bf16[2,512,768]{2,1,0:T(8,128)(2,1)}, f32[8,768]{1,0:T(8,128)}, f32[16,120,768]{2,1,0:T(8,128)}, f32[16,120,768]{2,1,0:T(8,128)}) custom-call(s32[1]{0:T(128)} %bitcast.33.me_ref.refs_2_, s32[2,80,1]{2,1,0:T(8,128)} %copy.122.pos_ref, f32[2,80,768]{2,1,0:T(8,128)} %bitcast.292, f32[2,8,768]{2,1,0:T(8,128)} %pad.33.cls_ref, ...), custom_call_target="tpu_custom_call" | custom-call | flops 52899999744 | bytes 1048576 | tf_op jit(solution)/shard_map/backward_ffn/pallas_call | solution.py:631
  406.2 30.6 %backward_heads.2 = (f32[1,512,768]{2,1,0:T(8,128)S(1)}, f32[8,768]{1,0:T(8,128)}, f32[9,512]{1,0:T(8,128)}, f32[1280,768]{1,0:T(8,128)}, f32[32,96,768]{2,1,0:T(8,128)}) custom-call(s32[2]{0:T(128)} %dynamic_slice.25.split_ref.refs_0_, s32[2]{0:T(128)} %dynamic_slice.26.length_ref.refs_1_, s32[1]{0:T(128)} %bitcast.33.me_ref.refs_2_, ...), custom_call_target="tpu_custom_call" | custom-call | flops 37950001152 | bytes 1048576 | tf_op jit(solution)/shard_map/backward_heads/pallas_call | solution.py:631
  436.8 5.1 add.778
  445.5 35.9 %backward_heads.3 = (f32[1,512,768]{2,1,0:T(8,128)}, f32[8,768]{1,0:T(8,128)}, f32[9,512]{1,0:T(8,128)}, bf16[1280,768]{1,0:T(8,128)(2,1)}, f32[16,96,768]{2,1,0:T(8,128)}, /*index=5*/f32[16,96,768]{2,1,0:T(8,128)}) custom-call(s32[2]{0:T(128)} %dynamic_slice.25.split_ref.refs_0_, ...), custom_call_target="tpu_custom_call", output_to_operand_aliasing={{1}: (14, {}), {2}: (15, {})} | custom-call | flops 37950001152 | bytes 1048576 | tf_op jit(solution)/shard_map/backward_heads/pallas_call | solution.py:631
  493.4 4.3 all-to-all-start.7
  504.7 4.4 add.784
  509.7 24.6 %collective-permute-done.37 = f32[1,2,2,120,384]{4,3,2,1,0:T(8,128)S(1)} collective-permute-done((f32[1,2,2,120,384]{4,3,2,1,0:T(8,128)S(1)}, f32[1,2,2,120,384]{4,3,2,1,0:T(8,128)S(1)}, u32[]{:S(2)}, u32[]{:S(2)}) %collective-permute-start.37) | collective-permute-done | bytes 737312 | tf_op jit(solution)/shard_map/ppermute | solution.py:85
  539.5 10.0 %collective-permute-done.38 = f32[1,2,120,384]{3,2,1,0:T(8,128)S(1)} collective-permute-done((f32[1,2,120,384]{3,2,1,0:T(8,128)S(1)}, f32[1,2,120,384]{3,2,1,0:T(8,128)S(1)}, u32[]{:S(2)}, u32[]{:S(2)}) %collective-permute-start.38) | collective-permute-done | bytes 368672 | tf_op jit(solution)/shard_map/ppermute | solution.py:85
  551.8 8.1 %collective-permute-done.41 = f32[1,2,120,384]{3,2,1,0:T(8,128)S(1)} collective-permute-done((f32[1,2,120,384]{3,2,1,0:T(8,128)S(1)}, f32[1,2,120,384]{3,2,1,0:T(8,128)S(1)}, u32[]{:S(2)}, u32[]{:S(2)}) %collective-permute-start.41) | collective-permute-done | bytes 368672 | tf_op jit(solution)/shard_map/ppermute | solution.py:85
  572.7 6.1 fusion.138
  578.8 5.7 multiply_reduce_fusion
  591.8 7.5 %collective-permute-done.35 = f32[1,2,96,384]{3,2,1,0:T(8,128)S(1)} collective-permute-done((f32[1,2,96,384]{3,2,1,0:T(8,128)S(1)}, f32[1,2,96,384]{3,2,1,0:T(8,128)S(1)}, u32[]{:S(2)}, u32[]{:S(2)}) %collective-permute-start.35) | collective-permute-done | bytes 294944 | tf_op jit(solution)/shard_map/ppermute | solution.py:85
  606.7 5.1 collective-permute-done.36
  618.7 5.4 collective-permute-done.43
  629.3 4.6 all-to-all-start.8
  636.0 15.5 %collective-permute-done.45 = f32[2,2,1,24,768]{4,3,0,1,2:T(8,128)S(1)} collective-permute-done((f32[2,2,1,24,768]{4,3,0,1,2:T(8,128)S(1)}, f32[2,2,1,24,768]{4,3,0,1,2:T(8,128)S(1)}, u32[]{:S(2)}, u32[]{:S(2)}) %collective-permute-start.45) | collective-permute-done | bytes 294944 | tf_op jit(solution)/shard_map/ppermute | solution.py:85
  651.7 12.3 %collective-permute-done.46 = f32[2,2,2,1,24,768]{5,4,0,1,2,3:T(8,128)S(1)} collective-permute-done((f32[2,2,2,1,24,768]{5,4,0,1,2,3:T(8,128)S(1)}, f32[2,2,2,1,24,768]{5,4,0,1,2,3:T(8,128)S(1)}, u32[]{:S(2)}, u32[]{:S(2)}) %collective-permute-start.46) | collective-permute-done | bytes 589856 | tf_op jit(solution)/shard_map/ppermute | solution.py:85
  683.6 7.5 %fusion.126 = (bf16[960,768]{1,0:T(8,128)(2,1)}, f32[960,768]{1,0:T(8,128)}, f32[960,768]{1,0:T(8,128)}, f32[960,768]{1,0:T(8,128)}) fusion(f32[960,768]{1,0:T(8,128)S(1)} %copy-done.5, f32[]{:T(128)} %bitcast.89, f32[]{:T(128)} %bitcast.88, f32[960,768]{1,0:T(8,128)} %get-tuple-element.604, f32[]{:T(128)S(6)} %div.216, f32[960,768]{1,0:T(8,128)} %param.34, ...), kind=kLoop, calls=%fused_computation.391 | loop fusion | flops 12533760 | bytes 22118412 | tf_op jit(solution)/shard_map/convert_element_type | solution.py:1145
  (483 shorter events, 222.3 us)
Async XLA Ops:
  16.3 23.2 %all-to-all-start.4 = ((bf16[8,2,24,768]{3,2,1,0:T(8,128)(2,1)}), bf16[8,2,24,768]{3,2,1,0:T(8,128)(2,1)S(1)}, u32[]{:S(2)}, u32[]{:S(2)}) async-start(bf16[8,2,24,768]{3,2,1,0:T(8,128)(2,1)} %copy.119), calls=%async_computation.4 | async-start | bytes 1179648 | tf_op jit(solution)/shard_map/all_to_all | solution.py:742
  23.6 69.9 %all-gather.6.cloned.1.call-start = ((), (), s32[]{:S(2)}) async-start(), calls=%async_computation.12 | async-start | bytes 2654208 | tf_op jit(solution)/shard_map/all_gather | solution.py:772
  94.8 36.8 %collective-permute-start = (bf16[1,3,192,768]{3,2,1,0:T(8,128)(2,1)S(1)}, bf16[1,3,192,768]{3,2,1,0:T(8,128)(2,1)S(1)}, u32[]{:S(2)}, u32[]{:S(2)}) collective-permute-start(bf16[1,3,192,768]{3,2,1,0:T(8,128)(2,1)S(1)} %bitcast.268), channel_id=1, source_target_pairs={{0,2},{2,0},{1,3},{3,1},{4,6},{6,4},{5,7},{7,5},{8,10},{10,8},{9,1... | collective-permute-start | bytes 2654216 | tf_op jit(solution)/shard_map/ppermute | solution.py:85
  97.1 78.6 %all-to-all-start.6 = ((bf16[32,40,768]{2,1,0:T(8,128)(2,1)}), bf16[32,40,768]{2,1,0:T(8,128)(2,1)}, u32[]{:S(2)}, u32[]{:S(2)}) async-start(bf16[32,40,768]{2,1,0:T(8,128)(2,1)} %bitcast.281), calls=%async_computation.6 | async-start | bytes 3932160 | tf_op jit(solution)/shard_map/all_to_all | solution.py:682
  100.7 155.1 %all-gather.4.cloned.1.call-start = ((), (), s32[]{:S(2)}) async-start(), calls=%async_computation.10 | async-start | bytes 7372800 | tf_op jit(solution)/shard_map/all_gather | solution.py:790
  131.9 35.9 %collective-permute-start.2 = (bf16[1,5,192,768]{3,2,1,0:T(8,128)(2,1)S(1)}, bf16[1,5,192,768]{3,2,1,0:T(8,128)(2,1)}, u32[]{:S(2)}, u32[]{:S(2)}) collective-permute-start(bf16[1,5,192,768]{3,2,1,0:T(8,128)(2,1)S(1)} %bitcast.264), channel_id=1, source_target_pairs={{0,2},{2,0},{1,3},{3,1},{4,6},{6,4},{5,7},{7,5},{8,10},{10,8},{9,1... | collective-permute-start | bytes 4423688 | tf_op jit(solution)/shard_map/ppermute | solution.py:85
  134.5 37.5 %collective-permute-start.1 = (bf16[1,2,3,192,768]{4,3,2,1,0:T(8,128)(2,1)S(1)}, bf16[1,2,3,192,768]{4,3,2,1,0:T(8,128)(2,1)}, u32[]{:S(2)}, u32[]{:S(2)}) collective-permute-start(bf16[1,2,3,192,768]{4,3,2,1,0:T(8,128)(2,1)S(1)} %bitcast.262), channel_id=1, source_target_pairs={{0,1},{1,0},{2,3},{3,2},{4,5},{5,4},{6,7},{7,6},{8,9},{9,8},{10,11... | collective-permute-start | bytes 5308424 | tf_op jit(solution)/shard_map/ppermute | solution.py:85
  138.7 428.4 %reduce-scatter.2.cloned.1.call-start = ((), (), s32[]{:S(2)}) async-start(), calls=%async_computation.11 | async-start | bytes 14745600 | tf_op jit(solution)/shard_map/reduce_scatter | solution.py:917
  172.0 30.0 %collective-permute-start.3 = (bf16[1,2,5,192,768]{4,3,2,1,0:T(8,128)(2,1)}, bf16[1,2,5,192,768]{4,3,2,1,0:T(8,128)(2,1)}, u32[]{:S(2)}, u32[]{:S(2)}) collective-permute-start(bf16[1,2,5,192,768]{4,3,2,1,0:T(8,128)(2,1)} %maximum_bitcast_fusion), channel_id=1, source_target_pairs={{0,1},{1,0},{2,3},{3,2},{4,5},{5,4},{6,7},{7,6},{8,9},{9,8},{10,11... | collective-permute-start | bytes 8847368 | tf_op jit(solution)/shard_map/ppermute | solution.py:85
  323.4 14.4 %collective-permute-start.19 = (f32[4,56,768]{2,1,0:T(8,128)}, f32[4,56,768]{2,1,0:T(8,128)}, u32[]{:S(2)}, u32[]{:S(2)}) collective-permute-start(f32[4,56,768]{2,1,0:T(8,128)} %bitcast.38), channel_id=1, source_target_pairs={{0,8},{8,0},{1,9},{9,1},{2,10},{10,2},{3,11},{11,3},{4,12},{12,4},... | collective-permute-start | bytes 2064392 | tf_op jit(solution)/shard_map/ppermute | solution.py:85
  325.0 17.0 %collective-permute-start.16 = (f32[4,56,768]{2,1,0:T(8,128)}, f32[4,56,768]{2,1,0:T(8,128)S(1)}, u32[]{:S(2)}, u32[]{:S(2)}) collective-permute-start(f32[4,56,768]{2,1,0:T(8,128)} %bitcast.35), channel_id=1, source_target_pairs={{0,2},{2,0},{1,3},{3,1},{4,6},{6,4},{5,7},{7,5},{8,10},{10,8},{9,1... | collective-permute-start | bytes 2064392 | tf_op jit(solution)/shard_map/ppermute | solution.py:85
  402.7 34.1 %collective-permute-start.25 = (f32[16,120,768]{2,1,0:T(8,128)}, f32[16,120,768]{2,1,0:T(8,128)}, u32[]{:S(2)}, u32[]{:S(2)}) collective-permute-start(f32[16,120,768]{2,1,0:T(8,128)} %get-tuple-element.485), channel_id=1, source_target_pairs={{0,1},{1,0},{2,3},{3,2},{4,5},{5,4},{6,7},{7,6},{8,9},{9,8},{10,11... | collective-permute-start | bytes 17694728 | tf_op jit(solution)/shard_map/ppermute | solution.py:85
  442.6 38.8 %collective-permute-start.26 = (f32[1,2,2,2,120,384]{5,4,3,2,1,0:T(8,128)S(1)}, f32[1,2,2,2,120,384]{5,4,3,2,1,0:T(8,128)}, u32[]{:S(2)}, u32[]{:S(2)}) collective-permute-start(f32[1,2,2,2,120,384]{5,4,3,2,1,0:T(8,128)S(1)} %slice.591), channel_id=1, source_target_pairs={{0,4},{4,0},{1,5},{5,1},{2,6},{6,2},{3,7},{7,3},{8,12},{12,8},{9,1... | collective-permute-start | bytes 4423688 | tf_op jit(solution)/shard_map/ppermute | solution.py:85
  445.5 38.0 %collective-permute-start.27 = (f32[2,1,2,2,120,384]{5,4,3,2,0,1:T(8,128)}, f32[2,1,2,2,120,384]{5,4,3,2,0,1:T(8,128)}, u32[]{:S(2)}, u32[]{:S(2)}) collective-permute-start(f32[2,1,2,2,120,384]{5,4,3,2,0,1:T(8,128)} %slice_bitcast_fusion), channel_id=1, source_target_pairs={{0,2},{2,0},{1,3},{3,1},{4,6},{6,4},{5,7},{7,5},{8,10},{10,8},{9,1... | collective-permute-start | bytes 4423688 | tf_op jit(solution)/shard_map/ppermute | solution.py:85
  486.8 17.9 %collective-permute-start.28 = (f32[16,96,768]{2,1,0:T(8,128)}, f32[16,96,768]{2,1,0:T(8,128)}, u32[]{:S(2)}, u32[]{:S(2)}) collective-permute-start(f32[16,96,768]{2,1,0:T(8,128)} %get-tuple-element.504), channel_id=1, source_target_pairs={{0,1},{1,0},{2,3},{3,2},{4,5},{5,4},{6,7},{7,6},{8,9},{9,8},{10,11... | collective-permute-start | bytes 14155784 | tf_op jit(solution)/shard_map/ppermute | solution.py:85
  493.4 79.3 %all-to-all-start.7 = ((bf16[32,40,768]{2,1,0:T(8,128)(2,1)}), bf16[32,40,768]{2,1,0:T(8,128)(2,1)}, u32[]{:S(2)}, u32[]{:S(2)}) async-start(bf16[32,40,768]{2,1,0:T(8,128)(2,1)} %bitcast.280), calls=%async_computation.8 | async-start | bytes 3932160 | tf_op jit(solution)/shard_map/all_to_all | solution.py:1069
  499.2 37.3 %collective-permute-start.40 = (f32[1,2,2,120,384]{4,3,2,1,0:T(8,128)S(1)}, f32[1,2,2,120,384]{4,3,2,1,0:T(8,128)S(1)}, u32[]{:S(2)}, u32[]{:S(2)}) collective-permute-start(f32[1,2,2,120,384]{4,3,2,1,0:T(8,128)S(1)} %get-tuple-element.638), channel_id=1, source_target_pairs={{0,4},{4,0},{1,5},{5,1},{2,6},{6,2},{3,7},{7,3},{8,12},{12,8},{9,1... | collective-permute-start | bytes 2211848 | tf_op jit(solution)/shard_map/ppermute | solution.py:85
  501.2 33.1 %collective-permute-start.37 = (f32[1,2,2,120,384]{4,3,2,1,0:T(8,128)S(1)}, f32[1,2,2,120,384]{4,3,2,1,0:T(8,128)S(1)}, u32[]{:S(2)}, u32[]{:S(2)}) collective-permute-start(f32[1,2,2,120,384]{4,3,2,1,0:T(8,128)S(1)} %get-tuple-element.636), channel_id=1, source_target_pairs={{0,2},{2,0},{1,3},{3,1},{4,6},{6,4},{5,7},{7,5},{8,10},{10,8},{9,1... | collective-permute-start | bytes 2211848 | tf_op jit(solution)/shard_map/ppermute | solution.py:85
  534.5 15.1 %collective-permute-start.38 = (f32[1,2,120,384]{3,2,1,0:T(8,128)S(1)}, f32[1,2,120,384]{3,2,1,0:T(8,128)S(1)}, u32[]{:S(2)}, u32[]{:S(2)}) collective-permute-start(f32[1,2,120,384]{3,2,1,0:T(8,128)S(1)} %slice_bitcast_fusion.6), channel_id=1, source_target_pairs={{0,8},{8,0},{1,9},{9,1},{2,10},{10,2},{3,11},{11,3},{4,12},{12,4},... | collective-permute-start | bytes 1105928 | tf_op jit(solution)/shard_map/ppermute | solution.py:85
  536.6 23.3 %collective-permute-start.41 = (f32[1,2,120,384]{3,2,1,0:T(8,128)S(1)}, f32[1,2,120,384]{3,2,1,0:T(8,128)S(1)}, u32[]{:S(2)}, u32[]{:S(2)}) collective-permute-start(f32[1,2,120,384]{3,2,1,0:T(8,128)S(1)} %slice_bitcast_fusion.4), channel_id=1, source_target_pairs={{0,8},{8,0},{1,9},{9,1},{2,10},{10,2},{3,11},{11,3},{4,12},{12,4},... | collective-permute-start | bytes 1105928 | tf_op jit(solution)/shard_map/ppermute | solution.py:85
  537.0 28.4 %collective-permute-start.29 = (f32[1,2,2,2,96,384]{5,4,3,2,1,0:T(8,128)S(1)}, f32[1,2,2,2,96,384]{5,4,3,2,1,0:T(8,128)S(1)}, u32[]{:S(2)}, u32[]{:S(2)}) collective-permute-start(f32[1,2,2,2,96,384]{5,4,3,2,1,0:T(8,128)S(1)} %slice.599), channel_id=1, source_target_pairs={{0,4},{4,0},{1,5},{5,1},{2,6},{6,2},{3,7},{7,3},{8,12},{12,8},{9,1... | collective-permute-start | bytes 3538952 | tf_op jit(solution)/shard_map/ppermute | solution.py:85
  539.1 26.8 %collective-permute-start.30 = (f32[2,1,2,2,96,384]{5,4,3,2,0,1:T(8,128)S(1)}, f32[2,1,2,2,96,384]{5,4,3,2,0,1:T(8,128)S(1)}, u32[]{:S(2)}, u32[]{:S(2)}) collective-permute-start(f32[2,1,2,2,96,384]{5,4,3,2,0,1:T(8,128)S(1)} %slice_bitcast_fusion.2), channel_id=1, source_target_pairs={{0,2},{2,0},{1,3},{3,1},{4,6},{6,4},{5,7},{7,5},{8,10},{10,8},{9,1... | collective-permute-start | bytes 3538952 | tf_op jit(solution)/shard_map/ppermute | solution.py:85
  550.4 39.3 %collective-permute-start.39 = (f32[1,120,384]{2,1,0:T(8,128)}, f32[1,120,384]{2,1,0:T(8,128)}, u32[]{:S(2)}, u32[]{:S(2)}) collective-permute-start(f32[1,120,384]{2,1,0:T(8,128)} %slice_bitcast_fusion.10), channel_id=1, source_target_pairs={{0,16},{16,0},{1,17},{17,1},{2,18},{18,2},{3,19},{19,3},{4,20},{20... | collective-permute-start | bytes 552968 | tf_op jit(solution)/shard_map/ppermute | solution.py:85
  560.7 30.0 %collective-permute-start.42 = (f32[1,120,384]{2,1,0:T(8,128)}, f32[1,120,384]{2,1,0:T(8,128)}, u32[]{:S(2)}, u32[]{:S(2)}) collective-permute-start(f32[1,120,384]{2,1,0:T(8,128)} %slice_bitcast_fusion.8), channel_id=1, source_target_pairs={{0,16},{16,0},{1,17},{17,1},{2,18},{18,2},{3,19},{19,3},{4,20},{20... | collective-permute-start | bytes 552968 | tf_op jit(solution)/shard_map/ppermute | solution.py:85
  569.9 15.0 %collective-permute-start.32 = (f32[1,2,2,96,384]{4,3,2,1,0:T(8,128)}, f32[1,2,2,96,384]{4,3,2,1,0:T(8,128)}, u32[]{:S(2)}, u32[]{:S(2)}) collective-permute-start(f32[1,2,2,96,384]{4,3,2,1,0:T(8,128)} %slice.605), channel_id=1, source_target_pairs={{0,4},{4,0},{1,5},{5,1},{2,6},{6,2},{3,7},{7,3},{8,12},{12,8},{9,1... | collective-permute-start | bytes 1769480 | tf_op jit(solution)/shard_map/ppermute | solution.py:85
  571.7 14.6 %collective-permute-start.31 = (f32[1,2,2,96,384]{4,3,2,1,0:T(8,128)}, f32[1,2,2,96,384]{4,3,2,1,0:T(8,128)}, u32[]{:S(2)}, u32[]{:S(2)}) collective-permute-start(f32[1,2,2,96,384]{4,3,2,1,0:T(8,128)} %slice.603), channel_id=1, source_target_pairs={{0,2},{2,0},{1,3},{3,1},{4,6},{6,4},{5,7},{7,5},{8,10},{10,8},{9,1... | collective-permute-start | bytes 1769480 | tf_op jit(solution)/shard_map/ppermute | solution.py:85
  587.5 11.7 %collective-permute-start.35 = (f32[1,2,96,384]{3,2,1,0:T(8,128)S(1)}, f32[1,2,96,384]{3,2,1,0:T(8,128)S(1)}, u32[]{:S(2)}, u32[]{:S(2)}) collective-permute-start(f32[1,2,96,384]{3,2,1,0:T(8,128)S(1)} %slice.611), channel_id=1, source_target_pairs={{0,8},{8,0},{1,9},{9,1},{2,10},{10,2},{3,11},{11,3},{4,12},{12,4},... | collective-permute-start | bytes 884744 | tf_op jit(solution)/shard_map/ppermute | solution.py:85
  591.7 11.6 %collective-permute-start.33 = (f32[1,2,96,384]{3,2,1,0:T(8,128)S(1)}, f32[1,2,96,384]{3,2,1,0:T(8,128)S(1)}, u32[]{:S(2)}, u32[]{:S(2)}) collective-permute-start(f32[1,2,96,384]{3,2,1,0:T(8,128)S(1)} %slice.607), channel_id=1, source_target_pairs={{0,8},{8,0},{1,9},{9,1},{2,10},{10,2},{3,11},{11,3},{4,12},{12,4},... | collective-permute-start | bytes 884744 | tf_op jit(solution)/shard_map/ppermute | solution.py:85
  599.3 12.5 %collective-permute-start.36 = (f32[1,96,384]{2,1,0:T(8,128)S(1)}, f32[1,96,384]{2,1,0:T(8,128)S(1)}, u32[]{:S(2)}, u32[]{:S(2)}) collective-permute-start(f32[1,96,384]{2,1,0:T(8,128)S(1)} %slice_bitcast_fusion.12), channel_id=1, source_target_pairs={{0,16},{16,0},{1,17},{17,1},{2,18},{18,2},{3,19},{19,3},{4,20},{20... | collective-permute-start | bytes 442376 | tf_op jit(solution)/shard_map/ppermute | solution.py:85
  629.3 34.9 %all-to-all-start.8 = ((f32[8,2,24,768]{3,2,1,0:T(8,128)}), f32[8,2,24,768]{3,2,1,0:T(8,128)S(1)}, u32[]{:S(2)}, u32[]{:S(2)}) async-start(f32[8,2,24,768]{3,2,1,0:T(8,128)} %multiply_add_fusion.3), calls=%async_computation.9 | async-start | bytes 2359296 | tf_op jit(solution)/shard_map/all_to_all | solution.py:1112
  633.9 17.5 %collective-permute-start.45 = (f32[2,2,1,24,768]{4,3,0,1,2:T(8,128)S(1)}, f32[2,2,1,24,768]{4,3,0,1,2:T(8,128)S(1)}, u32[]{:S(2)}, u32[]{:S(2)}) collective-permute-start(f32[2,2,1,24,768]{4,3,0,1,2:T(8,128)S(1)} %bitcast.291), channel_id=1, source_target_pairs={{0,4},{4,0},{1,5},{5,1},{2,6},{6,2},{3,7},{7,3},{8,12},{12,8},{9,1... | collective-permute-start | bytes 884744 | tf_op jit(solution)/shard_map/ppermute | solution.py:85
  651.6 12.5 %collective-permute-start.46 = (f32[2,2,2,1,24,768]{5,4,0,1,2,3:T(8,128)S(1)}, f32[2,2,2,1,24,768]{5,4,0,1,2,3:T(8,128)S(1)}, u32[]{:S(2)}, u32[]{:S(2)}) collective-permute-start(f32[2,2,2,1,24,768]{5,4,0,1,2,3:T(8,128)S(1)} %maximum_bitcast_fusion.1), channel_id=1, source_target_pairs={{0,2},{2,0},{1,3},{3,1},{4,6},{6,4},{5,7},{7,5},{8,10},{10,8},{9,1... | collective-permute-start | bytes 1769480 | tf_op jit(solution)/shard_map/ppermute | solution.py:85
  (92 other events, 824.4 us)
Sparse Core Ops, SparseCore 0:
  42.3 51.1 all-gather.5
  138.9 75.0 all-gather.3
  327.3 156.5 reduce-scatter.1
